TPU v7x, 256 devices: a whole 4x4x8 slice. The times are simulated.
256 devices in a mesh: layer: 16 (over y, z_hi, core), feat: 16 (over x, z_lo).
Axes of the slice: x: 4, y: 4, z: 8 (z_hi: 2, z_lo: 4; z = z_hi * 4 + z_lo), core: 2. Of those that a mesh axis runs over, the one named last changes fastest.
Arguments:
- acts: bfloat16 [16, 768, 1024], P('layer'), may hold values from -6 to 6
- targets: bfloat16 [16, 768, 1024], P('layer', 'feat'), may hold values from -6 to 6
- enc_weight: bfloat16 [16, 1024, 20480], P('layer', None, 'feat'), may hold values from -0.1875 to 0.1875
- enc_bias: float32 [16, 20480], P('layer', 'feat'), may hold values from -3 to 3
- dec_weight: bfloat16 [16, 20480, 2, 1024], P('layer', 'feat'), may hold values from -0.0390625 to 0.0390625
- dec_bias: float32 [16, 1024], P('layer'), may hold values from -3 to 3
Outputs:
- errors: float32 [16, 768, 1024], P('layer', 'feat')
- enc_grad: bfloat16 [16, 1024, 20480], P('layer', None, 'feat')
All inputs are finite; a program needn't handle non-finite values.
Results may differ from a plain program's by a relative error of at most 0.006.
Values may be sent and summed in bfloat16 or wider, within the bound.
No kernel may reach another device: no remote copies, remote signals or barrier semaphores. Data moves between devices by JAX's collectives and lax.ppermute only.
A program may use at most 128 MiB of HBM per device.

v0:
```python
import jax
import jax.numpy as jnp
from jax import lax
from jax.sharding import Mesh
from jax.sharding import PartitionSpec as P

FEAT = ("feat_0", "feat_1")


def summed_rows(total, axes):
    for axis in axes:
        total = lax.psum_scatter(total, axis, scatter_dimension=0, tiled=True)
    return total


def passed_along(block, axis, distance):
    devices = range(lax.axis_size(axis))
    route = [(i - distance, i) for i in devices if i - distance in devices]
    return lax.ppermute(block, axis, route)


def copy_for_each(value, axis):
    peers = lax.axis_size(axis)
    return lax.all_to_all(
        jnp.broadcast_to(value[None], (peers, *value.shape)), axis, 0, 0, tiled=True
    )


def joined_along(tiles, dim):
    tiles = jnp.moveaxis(tiles, 0, dim)
    lengths = tiles.shape
    return tiles.reshape(*lengths[:dim], lengths[dim] * lengths[dim + 1], *lengths[dim + 2 :])


def gathered_copies(value, axis, dim):
    tiles = copy_for_each(value, axis)
    return joined_along(tiles, dim)


def contract_width(errs, decoder):
    return lax.dot_general(
        errs, decoder, (((1,), (1,)), ((), ())), preferred_element_type=jnp.float32
    )


def local(acts, targets, enc_weight, enc_bias, dec_weight, dec_bias):
    inputs = acts[0]
    wanted = targets[0]
    weight = enc_weight[0]
    bias = enc_bias[0]
    decoder = dec_weight[0]
    out_bias = dec_bias[0]
    tokens = inputs.shape[0]
    width = inputs.shape[1]
    shard = weight.shape[1]
    pre = jnp.dot(inputs, weight, preferred_element_type=jnp.float32) + bias
    latent = (jax.nn.softplus(4.0 * pre) * 0.25).astype(jnp.bfloat16)
    first_dec = decoder[:, 0, :]
    second_dec = decoder[:, 1, :]
    joined = decoder.reshape(shard, 2 * width)
    summed = summed_rows(jnp.dot(latent, joined, preferred_element_type=jnp.float32), FEAT)
    carried = passed_along(summed[:, width:], "layer", 1)
    recon = summed[:, :width] + carried
    errors = recon + out_bias - wanted.astype(jnp.float32)
    err_half = errors.astype(jnp.bfloat16)
    deriv = jax.nn.sigmoid(4.0 * pre)
    scale = tokens ** (-0.5)
    gathered = gathered_copies(err_half, FEAT, 0)
    following = passed_along(gathered, "layer", -1)
    grad_latent = contract_width(gathered, first_dec) + contract_width(following, second_dec)
    grad_pre = (grad_latent * deriv).astype(jnp.bfloat16)
    total = lax.dot_general(
        inputs, grad_pre, (((0,), (0,)), ((), ())), preferred_element_type=jnp.float32
    )
    enc_grad = (total * scale).astype(jnp.bfloat16)
    return (errors[None], enc_grad[None])


def solution(mesh):
    finer = Mesh(mesh.devices.reshape(mesh.shape["layer"], 4, 4), ("layer", "feat_0", "feat_1"))
    in_specs = (
        P("layer", None, None),
        P("layer", FEAT, None),
        P("layer", None, FEAT),
        P("layer", FEAT),
        P("layer", FEAT, None, None),
        P("layer", None),
    )
    out_specs = (P("layer", FEAT, None), P("layer", None, FEAT))
    return jax.shard_map(local, mesh=finer, in_specs=in_specs, out_specs=out_specs, check_vma=False)
```

profile of v0, /device:TPU:8, one launch (start us, length us, event | category | flops | bytes accessed | tf_op | source)
XLA Modules:
  0.0 257.5 jit_solution(3784378127968718519)
XLA Ops:
  7.2 0.0 copy-start
  7.2 0.0 reduce-scatter.3.cloned.1.call-start
  7.2 7.1 %copy.11 = bf16[160,8,2,1024]{3,1,2,0:T(8,128)(2,1)} copy(bf16[160,8,2,1024]{3,2,1,0:T(2,128)(2,1)} %bitcast.40) | data formatting | bytes 10485760
  14.4 3.8 %add_multiply_fusion = f32[768,1280]{1,0:T(8,128)S(1)} fusion(bf16[1,1024,1280]{2,1,0:T(8,128)(2,1)S(1)} %copy-done, f32[1280]{0:T(1024)S(1)} %reduce, bf16[1,768,1024]{2,1,0:T(8,128)(2,1)} %param.6), kind=kOutput, calls=%fused_computation.6 | convolution fusion | flops 2015232000 | bytes 8131584 | tf_op jit(solution)/shard_map/dot_general | solution.py:56
  18.2 0.0 copy-start.6
  18.2 1.9 copy-done.6
  20.0 7.5 %fusion.5 = f32[768,2048]{1,0:T(8,128)} fusion(bf16[1280,2048]{1,0:T(8,128)(2,1)S(1)} %bitcast.43, f32[768,1280]{1,0:T(8,128)S(1)} %add_multiply_fusion), kind=kOutput, calls=%fused_computation.12 | convolution fusion | flops 4034396160 | bytes 15466496 | tf_op jit(solution)/shard_map/dot_general | solution.py:61
  27.5 0.0 reduce-scatter.3.cloned.1.call-update
  27.5 0.0 reduce-scatter.5.cloned.1.call-start
  27.6 69.4 %reduce-scatter.3.cloned.1.call-done = f32[192,2048]{1,0:T(8,128)} async-done(((f32[768,2048]{1,0:T(8,128)}), f32[192,2048]{1,0:T(8,128)}) %reduce-scatter.3.cloned.1.call-update) | async-done | bytes 1572880 | tf_op jit(solution)/shard_map/reduce_scatter | solution.py:12
  97.0 0.0 reduce-scatter.5.cloned.1.call-update
  97.1 42.9 %reduce-scatter.5.cloned.1.call-done = f32[48,2048]{1,0:T(8,128)} async-done(((f32[192,2048]{1,0:T(8,128)}), f32[48,2048]{1,0:T(8,128)}) %reduce-scatter.5.cloned.1.call-update) | async-done | bytes 393232 | tf_op jit(solution)/shard_map/reduce_scatter | solution.py:12
  140.0 0.9 slice.17
  140.9 1.9 collective-permute-start
  142.9 11.6 %collective-permute-done = f32[48,1024]{1,0:T(8,128)S(1)} collective-permute-done((f32[48,1024]{1,0:T(8,128)S(1)}, f32[48,1024]{1,0:T(8,128)S(1)}, u32[]{:S(2)}, u32[]{:S(2)}) %collective-permute-start) | collective-permute-done | bytes 196640 | tf_op jit(solution)/shard_map/ppermute | solution.py:19
  154.4 1.6 fusion.13
  156.1 0.2 broadcast_in_dim.13
  156.3 41.8 %all_to_all.5 = bf16[16,48,1024]{2,1,0:T(8,128)(2,1)S(1)} all-to-all(bf16[16,48,1024]{2,1,0:T(8,128)(2,1)S(1)} %broadcast_in_dim.13), channel_id=1, replica_groups=mesh['layer'=16,'feat_0'=4,'feat_1'=4] {'feat_0','feat_1'}, dimensions={0} | all-to-all | bytes 3145728 | tf_op jit(solution)/shard_map/all_to_all | solution.py:24
  198.1 2.1 collective-permute-start.1
  200.2 4.2 %copy.13 = bf16[1,1280,2,1024]{3,1,2,0:T(8,128)(2,1)S(1)} copy(bf16[1,1280,2,1024]{3,2,1,0:T(2,128)(2,1)} %param.10) | data formatting | bytes 10485760 | tf_op args[4]
  204.4 4.2 %fusion.3 = f32[768,1280]{1,0:T(8,128)} fusion(bf16[768,1024]{1,0:T(8,128)(2,1)S(1)} %bitcast.45, bf16[1280,2,1024]{2,0,1:T(8,128)(2,1)S(1)} %bitcast.41), kind=kOutput, calls=%fused_computation.10 | convolution fusion | flops 2013265920 | bytes 8126464 | tf_op jit(solution)/shard_map/dot_general | solution.py:41
  208.5 26.2 %collective-permute-done.1 = bf16[768,1024]{1,0:T(8,128)(2,1)} collective-permute-done((bf16[768,1024]{1,0:T(8,128)(2,1)S(1)}, bf16[768,1024]{1,0:T(8,128)(2,1)}, u32[]{:S(2)}, u32[]{:S(2)}) %collective-permute-start.1) | collective-permute-done | bytes 1572896 | tf_op jit(solution)/shard_map/ppermute | solution.py:19
  234.8 11.5 %fusion.2 = bf16[1,1024,1280]{1,2,0:T(8,128)(2,1)} fusion(bf16[1,768,1024]{2,1,0:T(8,128)(2,1)} %param.6, f32[768,1280]{1,0:T(8,128)} %copy-done.6, f32[768,1280]{1,0:T(8,128)} %fusion.3, bf16[768,1024]{1,0:T(8,128)(2,1)} %collective-permute-done.1, bf16[1280,2,1024]{2,0,1:T(8,128)(2,1)} %bitcast.42), kind=kOutput, calls=%fused_computation.7 | convolution fusion | flops 4035051520 | bytes 16252928 | tf_op jit(solution)/shard_map/dot_general | solution.py:72
  246.3 4.4 %copy.10 = bf16[1,1024,1280]{2,1,0:T(8,128)(2,1)} copy(bf16[1,1024,1280]{1,2,0:T(8,128)(2,1)} %fusion.2) | data formatting | bytes 5242880
  (12 shorter events, 0.0 us)
Async XLA Ops:
  7.2 7.2 %copy-start = (bf16[1,1024,1280]{2,1,0:T(8,128)(2,1)S(1)}, bf16[1,1024,1280]{2,1,0:T(8,128)(2,1)}, u32[]{:S(2)}) copy-start(bf16[1,1024,1280]{2,1,0:T(8,128)(2,1)} %param.8) | copy-start | bytes 7864324
  7.2 89.9 %reduce-scatter.3.cloned.1.call-start = ((), (), s32[]{:S(2)}) async-start(), calls=%async_computation.3 | async-start | bytes 7864320 | tf_op jit(solution)/shard_map/reduce_scatter | solution.py:12
  7.2 7.1 %copy-start.4 = (f32[1,1280]{1,0:T(1,128)S(1)}, f32[1,1280]{1,0:T(1,128)}, u32[]{:S(2)}) copy-start(f32[1,1280]{1,0:T(1,128)} %param.9) | copy-start | bytes 15364
  14.4 5.6 %copy-start.2 = (bf16[160,8,2,1024]{3,1,2,0:T(8,128)(2,1)S(1)}, bf16[160,8,2,1024]{3,1,2,0:T(8,128)(2,1)}, u32[]{:S(2)}) copy-start(bf16[160,8,2,1024]{3,1,2,0:T(8,128)(2,1)} %copy.11) | copy-start | bytes 15728644
  18.2 1.9 copy-start.6
  27.5 126.9 %copy-start.3 = (bf16[1,48,1024]{2,1,0:T(8,128)(2,1)S(1)}, bf16[1,48,1024]{2,1,0:T(8,128)(2,1)}, u32[]{:S(2)}) copy-start(bf16[1,48,1024]{2,1,0:T(8,128)(2,1)} %param.7) | copy-start | bytes 294916
  27.5 126.9 %copy-start.5 = (f32[1,1024]{1,0:T(1,128)S(1)}, f32[1,1024]{1,0:T(1,128)}, u32[]{:S(2)}) copy-start(f32[1,1024]{1,0:T(1,128)} %param.11) | copy-start | bytes 12292
  27.5 112.4 %reduce-scatter.5.cloned.1.call-start = ((), (), s32[]{:S(2)}) async-start(), calls=%async_computation.4 | async-start | bytes 1966080 | tf_op jit(solution)/shard_map/reduce_scatter | solution.py:12
  140.9 13.5 %collective-permute-start = (f32[48,1024]{1,0:T(8,128)S(1)}, f32[48,1024]{1,0:T(8,128)S(1)}, u32[]{:S(2)}, u32[]{:S(2)}) collective-permute-start(f32[48,1024]{1,0:T(8,128)S(1)} %slice.17), channel_id=1, source_target_pairs={{0,16},{16,32},{32,48},{48,64},{64,80},{80,96},{96,112},{112,128},... | collective-permute-start | bytes 589832 | tf_op jit(solution)/shard_map/ppermute | solution.py:19
  198.1 36.7 %collective-permute-start.1 = (bf16[768,1024]{1,0:T(8,128)(2,1)S(1)}, bf16[768,1024]{1,0:T(8,128)(2,1)}, u32[]{:S(2)}, u32[]{:S(2)}) collective-permute-start(bf16[768,1024]{1,0:T(8,128)(2,1)S(1)} %bitcast.44), channel_id=1, source_target_pairs={{16,0},{32,16},{48,32},{64,48},{80,64},{96,80},{112,96},{128,112},... | collective-permute-start | bytes 4718600 | tf_op jit(solution)/shard_map/ppermute | solution.py:19
  204.4 4.2 %copy-start.1 = (bf16[1,1280,2,1024]{3,1,2,0:T(8,128)(2,1)}, bf16[1,1280,2,1024]{3,1,2,0:T(8,128)(2,1)S(1)}, u32[]{:S(2)}) copy-start(bf16[1,1280,2,1024]{3,1,2,0:T(8,128)(2,1)S(1)} %copy.13) | copy-start | bytes 15728644
Sparse Core Ops, SparseCore 0:
  27.7 69.3 reduce-scatter.2
  99.6 40.3 reduce-scatter.4
where the time goes:
time: 262 us; the launch traced here: 257 us
  waiting for transfers between devices  150 us (57%)
  blocking collectives  41.8 us (16%)
  matrix products  26.9 us (10%)
  local copies, waits for them, and re-layouts  18.7 us (7%)
  between operations  14.1 us (5%)
  starting transfers between devices  4.09 us (2%)
    reduce_scatter x2, waiting for transfers between devices, summed_rows(): total = lax.psum_scatter(total, axis, scatter_dimension=0, tiled=True)  112 us
    all_to_all x1, blocking collectives, copy_for_each(): lax.all_to_all(jnp.broadcast_to(value[None], (peers, *value.shape)), axis...  41.8 us
    ppermute x2, waiting for transfers between devices, passed_along(): return lax.ppermute(block, axis, route)  37.8 us
    unnamed x17, local copies, waits for them, and re-layouts  17.5 us
    dot_general x1, matrix products, local(): lax.dot_general(inputs, grad_pre, (((0,), (0,)), ((), ())), preferred_ele...  11.5 us
    dot_general x1, matrix products, local(): jnp.dot(latent, joined, preferred_element_type=jnp.float32)  7.49 us
  transfers between devices with their start and end apart: 4, of which 4 were waited for; matrix products, arithmetic and copies ran while one was open for 3% of the time, Pallas kernels for 0%

commit v1 on v0

v1 whole, which is shorter than its diff:
```python
import jax
import jax.numpy as jnp
from jax import lax
from jax.sharding import Mesh
from jax.sharding import PartitionSpec as P

FEAT = ("feat_0", "feat_1")
MAIN_CUTS = 2


def summed_pieces(total, axis):
    peers = lax.axis_size(axis)
    rows = total.shape[0] // peers
    pieces = total.reshape(peers, rows, total.shape[1])
    pieces = lax.all_to_all(pieces, axis, 0, 0, tiled=True)
    return jnp.sum(pieces.astype(jnp.float32), axis=0)


def reduced(total):
    part = summed_pieces(total, FEAT[0]).astype(jnp.bfloat16)
    return summed_pieces(part, FEAT[1])


def gathered_over(value, axis):
    peers = lax.axis_size(axis)
    copies = jnp.broadcast_to(value[None], (peers, *value.shape))
    tiles = lax.all_to_all(copies, axis, 0, 0, tiled=True)
    return tiles.reshape(peers * value.shape[0], value.shape[1])


def gathered(value):
    return gathered_over(gathered_over(value, FEAT[1]), FEAT[0])


def on_chip(value):
    layers = lax.axis_size("layer")
    return lax.ppermute(value, "layer", [(i, i ^ 1) for i in range(layers)])


def across_chips(value):
    layers = lax.axis_size("layer")
    pairs = [(i, i + 1) for i in range(1, layers - 1, 2)]
    return lax.ppermute(value, "layer", pairs + [(j, i) for i, j in pairs])


def dot(a, b):
    return jnp.dot(a, b, preferred_element_type=jnp.float32)


def contract_width(errs, decoder):
    return lax.dot_general(
        errs, decoder, (((1,), (1,)), ((), ())), preferred_element_type=jnp.float32
    )


def local(acts, targets, enc_weight, enc_bias, dec_weight, dec_bias):
    inputs = acts[0]
    weight = enc_weight[0]
    bias = enc_bias[0]
    decoder = dec_weight[0]
    tokens, width = inputs.shape
    half = width // 2
    layer = lax.axis_index("layer")
    first = layer % 2 == 0
    ends = layer == lax.axis_size("layer") - 1

    offset = dec_bias[0] - targets[0].astype(jnp.float32)
    peer_offset = on_chip(offset[:, :half])

    pre = dot(inputs, weight) + bias
    latent = (jax.nn.softplus(4.0 * pre) * 0.25).astype(jnp.bfloat16)
    deriv = jax.nn.sigmoid(4.0 * pre)

    main = jnp.where(first, decoder[:, 0, :], decoder[:, 1, :])
    keep = jnp.where(first, decoder[:, 1, :half], decoder[:, 0, half:])
    give = jnp.where(first, decoder[:, 1, half:], decoder[:, 0, :half])
    main, keep, give = lax.optimization_barrier((main, keep, give))

    cut = width // MAIN_CUTS
    cuts = [slice(i * cut, (i + 1) * cut) for i in range(MAIN_CUTS)]
    sums = [reduced(dot(latent, main[:, c]).astype(jnp.bfloat16)) for c in cuts]
    given = on_chip(dot(latent, give).astype(jnp.bfloat16))
    shared = dot(latent, keep) + given.astype(jnp.float32)
    shared = reduced(shared.astype(jnp.bfloat16))

    shared = shared + jnp.where(first, peer_offset, offset[:, half:])
    shared_rows = gathered(shared.astype(jnp.bfloat16))
    other_rows = on_chip(shared_rows)
    other = on_chip(shared)

    mains = []
    rows = []
    for c, part in zip(cuts, sums):
        part = part + jnp.where(first, offset[:, c], 0.0)
        part = part + across_chips(part.astype(jnp.bfloat16)).astype(jnp.float32)
        mains.append(part)
        rows.append(gathered(jnp.where(ends, 0.0, part).astype(jnp.bfloat16)))

    errors = jnp.where(
        first, jnp.concatenate(mains, 1), jnp.concatenate([other, shared], 1)
    )

    grad_latent = contract_width(shared_rows, keep) + contract_width(other_rows, give)
    for c, block in zip(cuts, rows):
        grad_latent = grad_latent + contract_width(block, main[:, c])
    grad_pre = (grad_latent * deriv).astype(jnp.bfloat16)
    total = lax.dot_general(
        inputs, grad_pre, (((0,), (0,)), ((), ())), preferred_element_type=jnp.float32
    )
    enc_grad = (total * tokens ** (-0.5)).astype(jnp.bfloat16)
    return (errors[None], enc_grad[None])


def solution(mesh):
    finer = Mesh(mesh.devices.reshape(mesh.shape["layer"], 4, 4), ("layer", *FEAT))
    in_specs = (
        P("layer", None, None),
        P("layer", FEAT, None),
        P("layer", None, FEAT),
        P("layer", FEAT),
        P("layer", FEAT, None, None),
        P("layer", None),
    )
    out_specs = (P("layer", FEAT, None), P("layer", None, FEAT))
    return jax.shard_map(local, mesh=finer, in_specs=in_specs, out_specs=out_specs, check_vma=False)
```

time: 262 us -> 198 us (0.76); the launches traced: 257 us -> 196 us
  waiting for transfers between devices: 150 us -> 62.7 us
  starting transfers between devices: 4.09 us -> 49.7 us
  blocking collectives: 41.8 us -> 12.3 us
  matrix products: 26.9 us -> 41.8 us
  between operations: 14.1 us -> 0.88 us
  other arithmetic: 1.67 us -> 14 us
  local copies, waits for them, and re-layouts: 18.7 us -> 14.8 us
    reduce_scatter x2 -> x0, waiting for transfers between devices: 112 us -> none  [summed_rows(): total = lax.psum_scatter(total, axis, scatter_dimension=0, tiled=True)]
    all_to_all x0 -> x11, waiting for transfers between devices: none -> 46.7 us  [the longest x6 35.6 us: summed_pieces(): pieces = lax.all_to_all(pieces, axis, 0, 0, tiled=True)]
    all_to_all x0 -> x11, starting transfers between devices: none -> 44.4 us  [the longest x6 24.6 us: summed_pieces(): pieces = lax.all_to_all(pieces, axis, 0, 0, tiled=True)]
    all_to_all x1, blocking collectives: 41.8 us -> 12.3 us  [gathered_over(): tiles = lax.all_to_all(copies, axis, 0, 0, tiled=True)]
    ppermute x2 -> x6, waiting for transfers between devices: 37.8 us -> 16 us  [the longest x2 16 us: across_chips(): return lax.ppermute(value, 'layer', pairs + [(j, i) for i, j in pairs])]
    dot_general x2 -> x5, matrix products: 11.2 us -> 20.1 us  [dot(): return jnp.dot(a, b, preferred_element_type=jnp.float32)]
    unnamed x17 -> x24, local copies, waits for them, and re-layouts: 17.5 us -> 9.59 us
    dot_general x1 -> x3, matrix products: 4.17 us -> 12 us  [contract_width(): lax.dot_general(errs, decoder, (((1,), (1,)), ((), ())), preferred_elemen...]
  transfers between devices with their start and end apart: 4 -> 17, of which waited for: 4 -> 11; matrix products, arithmetic and copies ran while one was open for 3% -> 17% of each run, Pallas kernels for 0% -> 0%
where the time goes in v1:
time: 198 us; the launch traced here: 196 us
  waiting for transfers between devices  62.7 us (32%)
  starting transfers between devices  49.7 us (25%)
  matrix products  41.8 us (21%)
  local copies, waits for them, and re-layouts  14.8 us (7%)
  other arithmetic  14 us (7%)
  blocking collectives  12.3 us (6%)
    all_to_all x6, waiting for transfers between devices, summed_pieces(): pieces = lax.all_to_all(pieces, axis, 0, 0, tiled=True)  35.6 us
    all_to_all x6, starting transfers between devices, summed_pieces(): pieces = lax.all_to_all(pieces, axis, 0, 0, tiled=True)  24.6 us
    dot_general x5, matrix products, dot(): return jnp.dot(a, b, preferred_element_type=jnp.float32)  20.1 us
    all_to_all x5, starting transfers between devices, gathered_over(): tiles = lax.all_to_all(copies, axis, 0, 0, tiled=True)  19.8 us
    ppermute x2, waiting for transfers between devices, across_chips(): return lax.ppermute(value, 'layer', pairs + [(j, i) for i, j in pairs])  16 us
    all_to_all x1, blocking collectives, gathered_over(): tiles = lax.all_to_all(copies, axis, 0, 0, tiled=True)  12.3 us
    dot_general x3, matrix products, contract_width(): lax.dot_general(errs, decoder, (((1,), (1,)), ((), ())), preferred_elemen...  12 us
    all_to_all x5, waiting for transfers between devices, gathered_over(): tiles = lax.all_to_all(copies, axis, 0, 0, tiled=True)  11.1 us
  transfers between devices with their start and end apart: 17, of which 11 were waited for; matrix products, arithmetic and copies ran while one was open for 17% of the time, Pallas kernels for 0%

profile of v1, /device:TPU:8, one launch (start us, length us, event | category | flops | bytes accessed | tf_op | source)
XLA Modules:
  0.0 196.2 jit_solution(8916675952681581809)
XLA Ops:
  0.7 4.3 %copy.14 = bf16[1,1280,2,1024]{3,1,2,0:T(8,128)(2,1)S(1)} copy(bf16[1,1280,2,1024]{3,2,1,0:T(2,128)(2,1)} %param.10) | data formatting | bytes 10485760 | tf_op args[4]
  8.6 7.7 %fusion.2 = (bf16[768,1280]{1,0:T(8,128)(2,1)S(1)}, f32[768,1280]{1,0:T(8,128)}) fusion(f32[1280]{0:T(1024)S(1)} %reduce.3, bf16[1,1024,1280]{2,1,0:T(8,128)(2,1)S(1)} %copy-done, bf16[1,768,1024]{2,1,0:T(8,128)(2,1)} %param.6), kind=kOutput, calls=%fused_computation.8 | convolution fusion | flops 2023096320 | bytes 10097664 | tf_op jit(solution)/shard_map/dot_general | solution.py:47
  18.4 4.3 %all-to-all-start.2 = ((bf16[4,192,512]{2,1,0:T(8,128)(2,1)}), bf16[4,192,512]{2,1,0:T(8,128)(2,1)S(1)}, u32[]{:S(2)}, u32[]{:S(2)}) async-start(bf16[4,192,512]{2,1,0:T(8,128)(2,1)} %bitcast.66), calls=%async_computation.2 | async-start | bytes 1572864 | tf_op jit(solution)/shard_map/all_to_all | solution.py:15
  22.7 4.1 %convolution_convert_fusion = bf16[768,512]{1,0:T(8,128)(2,1)} fusion(bf16[768,1280]{1,0:T(8,128)(2,1)} %copy-done.9, bf16[1280,512]{1,0:T(8,128)(2,1)} %get-tuple-element.7), kind=kOutput, calls=%fused_computation.18 | convolution fusion | flops 1007026176 | bytes 4063232 | tf_op jit(solution)/shard_map/dot_general | solution.py:47
  28.9 6.1 %all-to-all-done.2 = bf16[4,192,512]{2,1,0:T(8,128)(2,1)S(1)} async-done(((bf16[4,192,512]{2,1,0:T(8,128)(2,1)}), bf16[4,192,512]{2,1,0:T(8,128)(2,1)S(1)}, u32[]{:S(2)}, u32[]{:S(2)}) %all-to-all-start.2) | async-done | bytes 786464 | tf_op jit(solution)/shard_map/all_to_all | solution.py:15
  41.3 9.4 %all-to-all-done = bf16[4,192,512]{2,1,0:T(8,128)(2,1)S(1)} async-done(((bf16[4,192,512]{2,1,0:T(8,128)(2,1)}), bf16[4,192,512]{2,1,0:T(8,128)(2,1)S(1)}, u32[]{:S(2)}, u32[]{:S(2)}) %all-to-all-start) | async-done | bytes 786464 | tf_op jit(solution)/shard_map/all_to_all | solution.py:15
  50.7 5.9 %all-to-all-start.3 = ((bf16[4,48,512]{2,1,0:T(8,128)(2,1)}), bf16[4,48,512]{2,1,0:T(8,128)(2,1)}, u32[]{:S(2)}, u32[]{:S(2)}) async-start(bf16[4,48,512]{2,1,0:T(8,128)(2,1)} %bitcast.62), calls=%async_computation.3 | async-start | bytes 393216 | tf_op jit(solution)/shard_map/all_to_all | solution.py:15
  56.6 4.2 %add_convert_fusion = bf16[768,512]{1,0:T(8,128)(2,1)} fusion(bf16[768,512]{1,0:T(8,128)(2,1)} %collective-permute-done.2, bf16[768,1280]{1,0:T(8,128)(2,1)} %copy-done.9, bf16[1280,512]{1,0:T(8,128)(2,1)} %get-tuple-element.6), kind=kOutput, calls=%fused_computation.17 | convolution fusion | flops 1007812608 | bytes 4849664 | tf_op jit(solution)/shard_map/dot_general | solution.py:47
  62.9 4.2 %all-to-all-start.4 = ((bf16[4,192,512]{2,1,0:T(8,128)(2,1)}), bf16[4,192,512]{2,1,0:T(8,128)(2,1)}, u32[]{:S(2)}, u32[]{:S(2)}) async-start(bf16[4,192,512]{2,1,0:T(8,128)(2,1)} %bitcast.64), calls=%async_computation.4 | async-start | bytes 1572864 | tf_op jit(solution)/shard_map/all_to_all | solution.py:15
  67.9 8.7 %all-to-all-done.4 = bf16[4,192,512]{2,1,0:T(8,128)(2,1)} async-done(((bf16[4,192,512]{2,1,0:T(8,128)(2,1)}), bf16[4,192,512]{2,1,0:T(8,128)(2,1)}, u32[]{:S(2)}, u32[]{:S(2)}) %all-to-all-start.4) | async-done | bytes 786464 | tf_op jit(solution)/shard_map/all_to_all | solution.py:15
  82.0 4.2 %all-to-all-done.1 = bf16[4,48,512]{2,1,0:T(8,128)(2,1)S(1)} async-done(((bf16[4,48,512]{2,1,0:T(8,128)(2,1)}), bf16[4,48,512]{2,1,0:T(8,128)(2,1)S(1)}, u32[]{:S(2)}, u32[]{:S(2)}) %all-to-all-start.1) | async-done | bytes 196640 | tf_op jit(solution)/shard_map/all_to_all | solution.py:15
  90.8 5.0 %all-to-all-done.5 = bf16[4,48,512]{2,1,0:T(8,128)(2,1)S(1)} async-done(((bf16[4,48,512]{2,1,0:T(8,128)(2,1)}), bf16[4,48,512]{2,1,0:T(8,128)(2,1)S(1)}, u32[]{:S(2)}, u32[]{:S(2)}) %all-to-all-start.5) | async-done | bytes 196640 | tf_op jit(solution)/shard_map/all_to_all | solution.py:15
  104.2 7.7 %collective-permute-done = bf16[48,512]{1,0:T(8,128)(2,1)S(1)} collective-permute-done((bf16[48,512]{1,0:T(8,128)(2,1)}, bf16[48,512]{1,0:T(8,128)(2,1)S(1)}, u32[]{:S(2)}, u32[]{:S(2)}) %collective-permute-start) | collective-permute-done | bytes 49184 | tf_op jit(solution)/shard_map/ppermute | solution.py:43
  112.6 12.3 %all_to_all.60 = bf16[4,48,512]{2,1,0:T(8,128)(2,1)S(1)} all-to-all(bf16[4,48,512]{2,1,0:T(8,128)(2,1)S(1)} %broadcast_in_dim.55), channel_id=1, replica_groups=mesh['layer'=16,'feat_0'=4,'feat_1'=4] {'feat_1'}, dimensions={0} | all-to-all | bytes 393216 | tf_op jit(solution)/shard_map/all_to_all | solution.py:27
  125.9 4.2 %all-to-all-start.7 = ((bf16[4,192,512]{2,1,0:T(8,128)(2,1)}), bf16[4,192,512]{2,1,0:T(8,128)(2,1)}, u32[]{:S(2)}, u32[]{:S(2)}) async-start(bf16[4,192,512]{2,1,0:T(8,128)(2,1)} %broadcast_in_dim.54), calls=%async_computation.7 | async-start | bytes 1572864 | tf_op jit(solution)/shard_map/all_to_all | solution.py:27
  132.0 8.3 %collective-permute-done.1 = bf16[48,512]{1,0:T(8,128)(2,1)S(1)} collective-permute-done((bf16[48,512]{1,0:T(8,128)(2,1)S(1)}, bf16[48,512]{1,0:T(8,128)(2,1)S(1)}, u32[]{:S(2)}, u32[]{:S(2)}) %collective-permute-start.1) | collective-permute-done | bytes 49184 | tf_op jit(solution)/shard_map/ppermute | solution.py:43
  141.6 4.1 %all-to-all-start.10 = ((bf16[4,48,512]{2,1,0:T(8,128)(2,1)}), bf16[4,48,512]{2,1,0:T(8,128)(2,1)S(1)}, u32[]{:S(2)}, u32[]{:S(2)}) async-start(bf16[4,48,512]{2,1,0:T(8,128)(2,1)} %broadcast_in_dim.58), calls=%async_computation.10 | async-start | bytes 393216 | tf_op jit(solution)/shard_map/all_to_all | solution.py:27
  146.3 5.7 %all-to-all-done.10 = bf16[4,48,512]{2,1,0:T(8,128)(2,1)S(1)} async-done(((bf16[4,48,512]{2,1,0:T(8,128)(2,1)}), bf16[4,48,512]{2,1,0:T(8,128)(2,1)S(1)}, u32[]{:S(2)}, u32[]{:S(2)}) %all-to-all-start.10) | async-done | bytes 196640 | tf_op jit(solution)/shard_map/all_to_all | solution.py:27
  153.0 4.0 %all-to-all-start.9 = ((bf16[4,192,512]{2,1,0:T(8,128)(2,1)}), bf16[4,192,512]{2,1,0:T(8,128)(2,1)S(1)}, u32[]{:S(2)}, u32[]{:S(2)}) async-start(bf16[4,192,512]{2,1,0:T(8,128)(2,1)} %broadcast_in_dim.57), calls=%async_computation.9 | async-start | bytes 1572864 | tf_op jit(solution)/shard_map/all_to_all | solution.py:27
  158.7 4.7 %fusion.22 = f32[768,1280]{1,0:T(8,128)} fusion(bf16[768,512]{1,0:T(8,128)(2,1)} %bitcast.19, bf16[1280,512]{1,0:T(8,128)(2,1)} %get-tuple-element.6), kind=kOutput, calls=%fused_computation.47 | convolution fusion | flops 1006632960 | bytes 6029312 | tf_op jit(solution)/shard_map/dot_general | solution.py:51
  168.3 4.2 %all-to-all-start.11 = ((bf16[4,192,512]{2,1,0:T(8,128)(2,1)}), bf16[4,192,512]{2,1,0:T(8,128)(2,1)}, u32[]{:S(2)}, u32[]{:S(2)}) async-start(bf16[4,192,512]{2,1,0:T(8,128)(2,1)} %broadcast_in_dim.60), calls=%async_computation.11 | async-start | bytes 1572864 | tf_op jit(solution)/shard_map/all_to_all | solution.py:27
  172.5 4.1 %convolution_add_fusion.2 = f32[768,1280]{1,0:T(8,128)S(1)} fusion(f32[768,1280]{1,0:T(8,128)} %fusion.22, bf16[768,512]{1,0:T(8,128)(2,1)} %collective-permute-done.5, bf16[1280,512]{1,0:T(8,128)(2,1)} %get-tuple-element.7), kind=kOutput, calls=%fused_computation.6 | convolution fusion | flops 1007616000 | bytes 9961472 | tf_op jit(solution)/shard_map/dot_general | solution.py:51
  182.1 9.8 %fusion.4 = bf16[1,1024,1280]{1,2,0:T(8,128)(2,1)} fusion(bf16[1,768,1024]{2,1,0:T(8,128)(2,1)} %param.6, f32[768,1280]{1,0:T(8,128)} %get-tuple-element.31, f32[768,1280]{1,0:T(8,128)} %convolution_add_fusion.1, bf16[768,512]{1,0:T(8,128)(2,1)} %bitcast.23, bf16[1280,1024]{1,0:T(8,128)(2,1)} %fusion.5), kind=kOutput, calls=%fused_computation.11 | convolution fusion | flops 3028418560 | bytes 14155776 | tf_op jit(solution)/shard_map/dot_general | solution.py:107
  191.8 4.4 %copy.12 = bf16[1,1024,1280]{2,1,0:T(8,128)(2,1)} copy(bf16[1,1024,1280]{1,2,0:T(8,128)(2,1)} %fusion.4) | data formatting | bytes 5242880
  (65 shorter events, 53.9 us)
Async XLA Ops:
  0.6 8.0 %copy-start = (bf16[1,1024,1280]{2,1,0:T(8,128)(2,1)S(1)}, bf16[1,1024,1280]{2,1,0:T(8,128)(2,1)}, u32[]{:S(2)}) copy-start(bf16[1,1024,1280]{2,1,0:T(8,128)(2,1)} %param.8) | copy-start | bytes 7864324
  8.6 7.7 %copy-start.1 = (bf16[1280,1024]{1,0:T(8,128)(2,1)S(1)}, bf16[1280,1024]{1,0:T(8,128)(2,1)}, u32[]{:S(2)}) copy-start(bf16[1280,1024]{1,0:T(8,128)(2,1)} %fusion.5) | copy-start | bytes 7864324
  18.4 16.6 %all-to-all-start.2 = ((bf16[4,192,512]{2,1,0:T(8,128)(2,1)}), bf16[4,192,512]{2,1,0:T(8,128)(2,1)S(1)}, u32[]{:S(2)}, u32[]{:S(2)}) async-start(bf16[4,192,512]{2,1,0:T(8,128)(2,1)} %bitcast.66), calls=%async_computation.2 | async-start | bytes 1572864 | tf_op jit(solution)/shard_map/all_to_all | solution.py:15
  22.7 4.1 %copy-start.2 = (bf16[1280,1024]{1,0:T(8,128)(2,1)S(1)}, bf16[1280,1024]{1,0:T(8,128)(2,1)}, u32[]{:S(2)}) copy-start(bf16[1280,1024]{1,0:T(8,128)(2,1)} %fusion.5) | copy-start | bytes 7864324
  22.7 4.1 %copy-start.10 = (bf16[768,1280]{1,0:T(8,128)(2,1)S(1)}, bf16[768,1280]{1,0:T(8,128)(2,1)}, u32[]{:S(2)}) copy-start(bf16[768,1280]{1,0:T(8,128)(2,1)} %copy-done.9) | copy-start | bytes 5898244
  26.8 29.8 %collective-permute-start.2 = (bf16[768,512]{1,0:T(8,128)(2,1)}, bf16[768,512]{1,0:T(8,128)(2,1)}, u32[]{:S(2)}, u32[]{:S(2)}) collective-permute-start(bf16[768,512]{1,0:T(8,128)(2,1)} %convolution_convert_fusion), channel_id=1, source_target_pairs={{0,16},{16,0},{32,48},{48,32},{64,80},{80,64},{96,112},{112,96},{1... | collective-permute-start | bytes 2359304 | tf_op jit(solution)/shard_map/ppermute | solution.py:37
  35.8 14.8 %all-to-all-start = ((bf16[4,192,512]{2,1,0:T(8,128)(2,1)}), bf16[4,192,512]{2,1,0:T(8,128)(2,1)S(1)}, u32[]{:S(2)}, u32[]{:S(2)}) async-start(bf16[4,192,512]{2,1,0:T(8,128)(2,1)} %bitcast.65), calls=%async_computation | async-start | bytes 1572864 | tf_op jit(solution)/shard_map/all_to_all | solution.py:15
  50.7 12.2 %all-to-all-start.3 = ((bf16[4,48,512]{2,1,0:T(8,128)(2,1)}), bf16[4,48,512]{2,1,0:T(8,128)(2,1)}, u32[]{:S(2)}, u32[]{:S(2)}) async-start(bf16[4,48,512]{2,1,0:T(8,128)(2,1)} %bitcast.62), calls=%async_computation.3 | async-start | bytes 393216 | tf_op jit(solution)/shard_map/all_to_all | solution.py:15
  60.7 28.9 %copy-start.6 = (bf16[1,48,1024]{2,1,0:T(8,128)(2,1)S(1)}, bf16[1,48,1024]{2,1,0:T(8,128)(2,1)}, u32[]{:S(2)}) copy-start(bf16[1,48,1024]{2,1,0:T(8,128)(2,1)} %param.7) | copy-start | bytes 294916
  60.7 28.9 %copy-start.8 = (f32[1,1024]{1,0:T(1,128)S(1)}, f32[1,1024]{1,0:T(1,128)}, u32[]{:S(2)}) copy-start(f32[1,1024]{1,0:T(1,128)} %param.11) | copy-start | bytes 12292
  62.9 13.7 %all-to-all-start.4 = ((bf16[4,192,512]{2,1,0:T(8,128)(2,1)}), bf16[4,192,512]{2,1,0:T(8,128)(2,1)}, u32[]{:S(2)}, u32[]{:S(2)}) async-start(bf16[4,192,512]{2,1,0:T(8,128)(2,1)} %bitcast.64), calls=%async_computation.4 | async-start | bytes 1572864 | tf_op jit(solution)/shard_map/all_to_all | solution.py:15
  76.6 9.6 %all-to-all-start.1 = ((bf16[4,48,512]{2,1,0:T(8,128)(2,1)}), bf16[4,48,512]{2,1,0:T(8,128)(2,1)S(1)}, u32[]{:S(2)}, u32[]{:S(2)}) async-start(bf16[4,48,512]{2,1,0:T(8,128)(2,1)} %bitcast.63), calls=%async_computation.1 | async-start | bytes 393216 | tf_op jit(solution)/shard_map/all_to_all | solution.py:15
  86.2 9.6 %all-to-all-start.5 = ((bf16[4,48,512]{2,1,0:T(8,128)(2,1)}), bf16[4,48,512]{2,1,0:T(8,128)(2,1)S(1)}, u32[]{:S(2)}, u32[]{:S(2)}) async-start(bf16[4,48,512]{2,1,0:T(8,128)(2,1)} %bitcast.15), calls=%async_computation.5 | async-start | bytes 393216 | tf_op jit(solution)/shard_map/all_to_all | solution.py:15
  89.7 6.2 %collective-permute-start.3 = (f32[48,512]{1,0:T(8,128)S(1)}, f32[48,512]{1,0:T(8,128)}, u32[]{:S(2)}, u32[]{:S(2)}) collective-permute-start(f32[48,512]{1,0:T(8,128)S(1)} %slice.50), channel_id=1, source_target_pairs={{0,16},{16,0},{32,48},{48,32},{64,80},{80,64},{96,112},{112,96},{1... | collective-permute-start | bytes 294920 | tf_op jit(solution)/shard_map/ppermute | solution.py:37
  98.1 14.5 %all-to-all-start.6 = ((bf16[4,48,512]{2,1,0:T(8,128)(2,1)}), bf16[4,48,512]{2,1,0:T(8,128)(2,1)S(1)}, u32[]{:S(2)}, u32[]{:S(2)}) async-start(bf16[4,48,512]{2,1,0:T(8,128)(2,1)} %broadcast_in_dim.52), calls=%async_computation.6 | async-start | bytes 393216 | tf_op jit(solution)/shard_map/all_to_all | solution.py:27
  101.5 10.4 %collective-permute-start = (bf16[48,512]{1,0:T(8,128)(2,1)}, bf16[48,512]{1,0:T(8,128)(2,1)S(1)}, u32[]{:S(2)}, u32[]{:S(2)}) collective-permute-start(bf16[48,512]{1,0:T(8,128)(2,1)} %get-tuple-element.22), channel_id=1, source_target_pairs={{16,32},{48,64},{80,96},{112,128},{144,160},{176,192},{208,224},{3... | collective-permute-start | bytes 147464 | tf_op jit(solution)/shard_map/ppermute | solution.py:43
  125.9 15.1 %all-to-all-start.7 = ((bf16[4,192,512]{2,1,0:T(8,128)(2,1)}), bf16[4,192,512]{2,1,0:T(8,128)(2,1)}, u32[]{:S(2)}, u32[]{:S(2)}) async-start(bf16[4,192,512]{2,1,0:T(8,128)(2,1)} %broadcast_in_dim.54), calls=%async_computation.7 | async-start | bytes 1572864 | tf_op jit(solution)/shard_map/all_to_all | solution.py:27
  130.1 10.2 %collective-permute-start.1 = (bf16[48,512]{1,0:T(8,128)(2,1)S(1)}, bf16[48,512]{1,0:T(8,128)(2,1)S(1)}, u32[]{:S(2)}, u32[]{:S(2)}) collective-permute-start(bf16[48,512]{1,0:T(8,128)(2,1)S(1)} %get-tuple-element.24), channel_id=1, source_target_pairs={{16,32},{48,64},{80,96},{112,128},{144,160},{176,192},{208,224},{3... | collective-permute-start | bytes 147464 | tf_op jit(solution)/shard_map/ppermute | solution.py:43
  141.6 10.3 %all-to-all-start.10 = ((bf16[4,48,512]{2,1,0:T(8,128)(2,1)}), bf16[4,48,512]{2,1,0:T(8,128)(2,1)S(1)}, u32[]{:S(2)}, u32[]{:S(2)}) async-start(bf16[4,48,512]{2,1,0:T(8,128)(2,1)} %broadcast_in_dim.58), calls=%async_computation.10 | async-start | bytes 393216 | tf_op jit(solution)/shard_map/all_to_all | solution.py:27
  145.7 26.8 %collective-permute-start.5 = (bf16[768,512]{1,0:T(8,128)(2,1)}, bf16[768,512]{1,0:T(8,128)(2,1)}, u32[]{:S(2)}, u32[]{:S(2)}) collective-permute-start(bf16[768,512]{1,0:T(8,128)(2,1)} %bitcast.19), channel_id=1, source_target_pairs={{0,16},{16,0},{32,48},{48,32},{64,80},{80,64},{96,112},{112,96},{1... | collective-permute-start | bytes 2359304 | tf_op jit(solution)/shard_map/ppermute | solution.py:37
  145.7 11.2 %collective-permute-start.4 = (f32[48,512]{1,0:T(8,128)S(1)}, f32[48,512]{1,0:T(8,128)}, u32[]{:S(2)}, u32[]{:S(2)}) collective-permute-start(f32[48,512]{1,0:T(8,128)S(1)} %get-tuple-element.15), channel_id=1, source_target_pairs={{0,16},{16,0},{32,48},{48,32},{64,80},{80,64},{96,112},{112,96},{1... | collective-permute-start | bytes 294920 | tf_op jit(solution)/shard_map/ppermute | solution.py:37
  153.0 13.5 %all-to-all-start.9 = ((bf16[4,192,512]{2,1,0:T(8,128)(2,1)}), bf16[4,192,512]{2,1,0:T(8,128)(2,1)S(1)}, u32[]{:S(2)}, u32[]{:S(2)}) async-start(bf16[4,192,512]{2,1,0:T(8,128)(2,1)} %broadcast_in_dim.57), calls=%async_computation.9 | async-start | bytes 1572864 | tf_op jit(solution)/shard_map/all_to_all | solution.py:27
  168.3 13.7 %all-to-all-start.11 = ((bf16[4,192,512]{2,1,0:T(8,128)(2,1)}), bf16[4,192,512]{2,1,0:T(8,128)(2,1)}, u32[]{:S(2)}, u32[]{:S(2)}) async-start(bf16[4,192,512]{2,1,0:T(8,128)(2,1)} %broadcast_in_dim.60), calls=%async_computation.11 | async-start | bytes 1572864 | tf_op jit(solution)/shard_map/all_to_all | solution.py:27
  172.5 4.1 %copy-start.3 = (bf16[1280,1024]{1,0:T(8,128)(2,1)S(1)}, bf16[1280,1024]{1,0:T(8,128)(2,1)}, u32[]{:S(2)}) copy-start(bf16[1280,1024]{1,0:T(8,128)(2,1)} %fusion.5) | copy-start | bytes 7864324
  (4 other events, 5.7 us)

commit v2 on v1

v2 whole, which is shorter than its diff:
```python
import jax
import jax.numpy as jnp
from jax import lax
from jax.experimental import pallas as pl
from jax.experimental.pallas import tpu as pltpu
from jax.sharding import Mesh
from jax.sharding import PartitionSpec as P

FEAT = ("feat_0", "feat_1")
SIDE = 4
HIGH = jnp.float32
LOW = jnp.bfloat16


def exchanged(piece, axis, step):
    return lax.ppermute(piece, axis, [(i, i ^ step) for i in range(SIDE)])


def after(value, *others):
    return lax.optimization_barrier((value, *others))[0]


def turned_kernel(places, blocks, out):
    for i in range(SIDE * SIDE):
        out[i] = blocks[places[i]]


def turned(array, places):
    blocks = array.reshape(SIDE * SIDE, -1, array.shape[1])
    out = pl.pallas_call(
        turned_kernel,
        in_specs=[
            pl.BlockSpec(memory_space=pltpu.SMEM),
            pl.BlockSpec(memory_space=pltpu.VMEM),
        ],
        out_specs=pl.BlockSpec(memory_space=pltpu.VMEM),
        out_shape=jax.ShapeDtypeStruct(blocks.shape, blocks.dtype),
        name="turned",
    )(places, blocks)
    return out.reshape(array.shape)


def summed_pieces(pieces, axis, *before):
    parts = [exchanged(pieces[step], axis, step) for step in range(1, SIDE)]
    total = after(pieces[0], *before).astype(HIGH)
    for part in parts:
        total = total + part.astype(HIGH)
    return total


def row_pieces(array):
    rows = array.shape[0] // SIDE
    return [array[i * rows : (i + 1) * rows] for i in range(SIDE)]


def gathered_over(value, axis):
    tiles = [value] + [exchanged(value, axis, step) for step in range(1, SIDE)]
    return jnp.concatenate(tiles, 0)


def on_chip(value):
    layers = lax.axis_size("layer")
    return lax.ppermute(value, "layer", [(i, i ^ 1) for i in range(layers)])


def across_chips(value):
    layers = lax.axis_size("layer")
    pairs = [(i, i + 1) for i in range(1, layers - 1, 2)]
    return lax.ppermute(value, "layer", pairs + [(j, i) for i, j in pairs])


def dot(a, b):
    return jnp.dot(a, b, preferred_element_type=HIGH)


def contract_width(errs, decoder):
    return lax.dot_general(errs, decoder, (((1,), (1,)), ((), ())), preferred_element_type=HIGH)


def local(acts, targets, enc_weight, enc_bias, dec_weight, dec_bias):
    weight = enc_weight[0]
    bias = enc_bias[0]
    decoder = dec_weight[0]
    tokens, width = acts.shape[1:]
    half = width // 2
    layer = lax.axis_index("layer")
    first = layer % 2 == 0
    ends = layer == lax.axis_size("layer") - 1

    steps = jnp.arange(SIDE, dtype=jnp.int32)
    along = lax.axis_index(FEAT[0]) ^ steps
    across = lax.axis_index(FEAT[1]) ^ steps
    inputs = turned(acts[0], (along[:, None] * SIDE + across).reshape(-1))

    pre = dot(inputs, weight) + bias
    scaled = 4.0 * pre
    small = jnp.exp(-jnp.abs(scaled))
    latent = ((jnp.maximum(scaled, 0.0) + jnp.log1p(small)) * 0.25).astype(LOW)
    latent, pre = lax.optimization_barrier((latent, pre))

    main = after(jnp.where(first, decoder[:, 0, :], decoder[:, 1, :]))
    part = dot(latent, main).astype(LOW)
    part, latent, pre, decoder = lax.optimization_barrier((part, latent, pre, decoder))

    keep = jnp.where(first, decoder[:, 1, :half], decoder[:, 0, half:])
    give = jnp.where(first, decoder[:, 1, half:], decoder[:, 0, :half])
    keep, give = lax.optimization_barrier((keep, give))
    given = on_chip(dot(latent, give).astype(LOW))
    offset = dec_bias[0] - targets[0].astype(HIGH)
    peer_offset = on_chip(offset[:, :half])
    shared = (dot(latent, keep) + given.astype(HIGH)).astype(LOW)

    part = summed_pieces(row_pieces(part), FEAT[0], shared).astype(LOW)
    shared = summed_pieces(row_pieces(shared), FEAT[0], part).astype(LOW)
    deriv = after(jax.nn.sigmoid(4.0 * pre))
    part = summed_pieces(row_pieces(part), FEAT[1], shared)
    part = part + jnp.where(first, offset, 0.0)
    sent = part.astype(LOW)
    shared = summed_pieces(row_pieces(shared), FEAT[1], sent)
    shared = shared + jnp.where(first, peer_offset, offset[:, half:])
    shared_rows = shared.astype(LOW)
    part = after(part, shared_rows) + across_chips(sent).astype(HIGH)
    main_rows = jnp.where(ends, 0.0, part).astype(LOW)

    shared_rows = gathered_over(shared_rows, FEAT[1])
    main_rows = gathered_over(main_rows, FEAT[1])
    shared_rows = gathered_over(shared_rows, FEAT[0])
    main_rows = gathered_over(main_rows, FEAT[0])
    other_rows = on_chip(shared_rows)
    other = on_chip(shared)

    errors = jnp.where(first, part, jnp.concatenate([other, shared], 1))

    grad_latent = contract_width(shared_rows, keep) + contract_width(other_rows, give)
    grad_latent = after(grad_latent)
    grad_latent = grad_latent + contract_width(main_rows, main)
    grad_pre = after((grad_latent * deriv).astype(LOW))
    total = lax.dot_general(inputs, grad_pre, (((0,), (0,)), ((), ())), preferred_element_type=HIGH)
    enc_grad = (total * tokens ** (-0.5)).astype(LOW)
    return (errors[None], enc_grad[None])


def solution(mesh):
    finer = Mesh(mesh.devices.reshape(mesh.shape["layer"], SIDE, SIDE), ("layer", *FEAT))
    in_specs = (
        P("layer", None, None),
        P("layer", FEAT, None),
        P("layer", None, FEAT),
        P("layer", FEAT),
        P("layer", FEAT, None, None),
        P("layer", None),
    )
    out_specs = (P("layer", FEAT, None), P("layer", None, FEAT))
    return jax.shard_map(local, mesh=finer, in_specs=in_specs, out_specs=out_specs, check_vma=False)
```

time: 198 us -> 131 us (0.66)
  matrix products: 41.8 us -> 18.3 us
  waiting for transfers between devices: 62.7 us -> 45.4 us
  blocking collectives: 12.3 us -> 0 us
  other arithmetic: 14 us -> 7.93 us
  local copies, waits for them, and re-layouts: 14.8 us -> 9.32 us
  starting transfers between devices: 49.7 us -> 45.8 us
  Pallas kernels: 0 us -> 2.7 us
    all_to_all x11 -> x0, waiting for transfers between devices: 46.7 us -> none  [the longest x6 35.6 us: summed_pieces(): pieces = lax.all_to_all(pieces, axis, 0, 0, tiled=True)]
    ppermute x0 -> x24, waiting for transfers between devices: none -> 45.4 us  [exchanged(): return lax.ppermute(piece, axis, [(i, i ^ step) for i in range(SIDE)])]
    all_to_all x11 -> x0, starting transfers between devices: 44.4 us -> none  [the longest x6 24.6 us: summed_pieces(): pieces = lax.all_to_all(pieces, axis, 0, 0, tiled=True)]
    ppermute x0 -> x24, starting transfers between devices: none -> 38 us  [exchanged(): return lax.ppermute(piece, axis, [(i, i ^ step) for i in range(SIDE)])]
    ppermute x2 -> x1, waiting for transfers between devices: 16 us -> 0.01 us  [across_chips(): return lax.ppermute(value, 'layer', pairs + [(j, i) for i, j in pairs])]
    all_to_all x1 -> x0, blocking collectives: 12.3 us -> none  [gathered_over(): tiles = lax.all_to_all(copies, axis, 0, 0, tiled=True)]
    dot_general x5 -> x4, matrix products: 20.1 us -> 9.85 us  [dot(): return jnp.dot(a, b, preferred_element_type=HIGH)]
    dot_general x3, matrix products: 12 us -> 4.73 us  [contract_width(): lax.dot_general(errs, decoder, (((1,), (1,)), ((), ())), preferred_elemen...]
  transfers between devices with their start and end apart: 17 -> 29, of which waited for: 11 -> 10; matrix products, arithmetic and copies ran while one was open for 17% -> 7% of each run, Pallas kernels for 0% -> 0%
where the time goes in v2:
time: 131 us
  starting transfers between devices  45.8 us (35%)
  waiting for transfers between devices  45.4 us (35%)
  matrix products  18.3 us (14%)
  local copies, waits for them, and re-layouts  9.32 us (7%)
  other arithmetic  7.93 us (6%)
  Pallas kernels  2.7 us (2%)
    ppermute x24, waiting for transfers between devices, exchanged(): return lax.ppermute(piece, axis, [(i, i ^ step) for i in range(SIDE)])  45.4 us
    ppermute x24, starting transfers between devices, exchanged(): return lax.ppermute(piece, axis, [(i, i ^ step) for i in range(SIDE)])  38 us
    dot_general x4, matrix products, dot(): return jnp.dot(a, b, preferred_element_type=HIGH)  9.85 us
    unnamed x39, local copies, waits for them, and re-layouts  8.46 us
    ppermute x1, starting transfers between devices, across_chips(): return lax.ppermute(value, 'layer', pairs + [(j, i) for i, j in pairs])  7.48 us
    dot_general x3, matrix products, contract_width(): lax.dot_general(errs, decoder, (((1,), (1,)), ((), ())), preferred_elemen...  4.73 us
    dot_general x1, matrix products, local(): lax.dot_general(inputs, grad_pre, (((0,), (0,)), ((), ())), preferred_ele...  3.75 us
    div x1, other arithmetic, local(): deriv = after(jax.nn.sigmoid(4.0 * pre))  2.9 us
  transfers between devices with their start and end apart: 29, of which 10 were waited for; matrix products, arithmetic and copies ran while one was open for 7% of the time, Pallas kernels for 0%

profile of v2, /device:TPU:8, one launch (start us, length us, event | category | flops | bytes accessed | tf_op | source)
XLA Modules:
  0.0 130.5 jit_solution(6218379457981812612)
XLA Ops:
  1.3 4.2 %copy.10 = bf16[1,1280,2,1024]{3,1,2,0:T(8,128)(2,1)S(1)} copy(bf16[1,1280,2,1024]{3,2,1,0:T(2,128)(2,1)} %param.10) | data formatting | bytes 10485760 | tf_op args[4]
  5.6 2.3 %copy-done.1 = bf16[1,1280,2,1024]{3,1,2,0:T(8,128)(2,1)} copy-done((bf16[1,1280,2,1024]{3,1,2,0:T(8,128)(2,1)}, bf16[1,1280,2,1024]{3,1,2,0:T(8,128)(2,1)S(1)}, u32[]{:S(2)}) %copy-start.1) | copy-done | bytes 5242904
  9.7 2.7 %turned.1 = bf16[16,48,1024]{2,1,0:T(8,128)(2,1)} custom-call(s32[16]{0:T(128)} %add.95.places, bf16[16,48,1024]{2,1,0:T(8,128)(2,1)} %bitcast.44), custom_call_target="tpu_custom_call" | custom-call | tf_op jit(solution)/shard_map/turned/pallas_call | solution.py:30
  12.4 5.3 %multiply_convert_fusion.2 = (bf16[768,1280]{1,0:T(8,128)(2,1)S(1)}, f32[768,1280]{1,0:T(8,128)S(1)}) fusion(f32[1280]{0:T(1024)S(1)} %reduce, bf16[768,1024]{1,0:T(8,128)(2,1)} %bitcast.45, bf16[1,1024,1280]{2,1,0:T(8,128)(2,1)S(1)} %copy-done), kind=kOutput, calls=%fused_computation.5 | convolution fusion | flops 2021130240 | bytes 10097664 | tf_op jit(solution)/shard_map/dot_general | solution.py:73
  17.7 2.2 %convolution_convert_fusion = bf16[768,1024]{1,0:T(8,128)(2,1)S(1)} fusion(bf16[768,1280]{1,0:T(8,128)(2,1)S(1)} %get-tuple-element.18, bf16[1280,1024]{1,0:T(8,128)(2,1)S(1)} %copy-done.6), kind=kOutput, calls=%fused_computation.11 | convolution fusion | flops 2014052352 | bytes 6160384 | tf_op jit(solution)/shard_map/dot_general | solution.py:73
  21.9 2.8 %collective-permute-start.3 = (bf16[192,1024]{1,0:T(8,128)(2,1)S(1)}, bf16[192,1024]{1,0:T(8,128)(2,1)S(1)}, u32[]{:S(2)}, u32[]{:S(2)}) collective-permute-start(bf16[192,1024]{1,0:T(8,128)(2,1)S(1)} %get-tuple-element.38), channel_id=1, source_target_pairs={{0,12},{4,8},{8,4},{12,0},{1,13},{5,9},{9,5},{13,1},{2,14},{6,10},... | collective-permute-start | bytes 1179656 | tf_op jit(solution)/shard_map/ppermute | solution.py:16
  27.3 2.8 %collective-permute-start.6 = (bf16[192,512]{1,0:T(8,128)(2,1)S(1)}, bf16[192,512]{1,0:T(8,128)(2,1)S(1)}, u32[]{:S(2)}, u32[]{:S(2)}) collective-permute-start(bf16[192,512]{1,0:T(8,128)(2,1)S(1)} %get-tuple-element.42), channel_id=1, source_target_pairs={{0,12},{4,8},{8,4},{12,0},{1,13},{5,9},{9,5},{13,1},{2,14},{6,10},... | collective-permute-start | bytes 589832 | tf_op jit(solution)/shard_map/ppermute | solution.py:16
  31.0 12.6 %collective-permute-done.3 = bf16[192,1024]{1,0:T(8,128)(2,1)S(1)} collective-permute-done((bf16[192,1024]{1,0:T(8,128)(2,1)S(1)}, bf16[192,1024]{1,0:T(8,128)(2,1)S(1)}, u32[]{:S(2)}, u32[]{:S(2)}) %collective-permute-start.3) | collective-permute-done | bytes 393248 | tf_op jit(solution)/shard_map/ppermute | solution.py:16
  44.8 4.7 %collective-permute-start.9 = (bf16[48,1024]{1,0:T(8,128)(2,1)S(1)}, bf16[48,1024]{1,0:T(8,128)(2,1)S(1)}, u32[]{:S(2)}, u32[]{:S(2)}) collective-permute-start(bf16[48,1024]{1,0:T(8,128)(2,1)S(1)} %get-tuple-element.46), channel_id=1, source_target_pairs={{0,3},{1,2},{2,1},{3,0},{4,7},{5,6},{6,5},{7,4},{8,11},{9,10},{10,... | collective-permute-start | bytes 294920 | tf_op jit(solution)/shard_map/ppermute | solution.py:16
  49.5 2.1 %collective-permute-done.6 = bf16[192,512]{1,0:T(8,128)(2,1)S(1)} collective-permute-done((bf16[192,512]{1,0:T(8,128)(2,1)S(1)}, bf16[192,512]{1,0:T(8,128)(2,1)S(1)}, u32[]{:S(2)}, u32[]{:S(2)}) %collective-permute-start.6) | collective-permute-done | bytes 196640 | tf_op jit(solution)/shard_map/ppermute | solution.py:16
  53.6 2.9 %collective-permute-done.8 = bf16[48,1024]{1,0:T(8,128)(2,1)S(1)} collective-permute-done((bf16[48,1024]{1,0:T(8,128)(2,1)S(1)}, bf16[48,1024]{1,0:T(8,128)(2,1)S(1)}, u32[]{:S(2)}, u32[]{:S(2)}) %collective-permute-start.8) | collective-permute-done | bytes 98336 | tf_op jit(solution)/shard_map/ppermute | solution.py:16
  58.1 3.4 %collective-permute-start.12 = (bf16[48,512]{1,0:T(8,128)(2,1)S(1)}, bf16[48,512]{1,0:T(8,128)(2,1)S(1)}, u32[]{:S(2)}, u32[]{:S(2)}) collective-permute-start(bf16[48,512]{1,0:T(8,128)(2,1)S(1)} %get-tuple-element.50), channel_id=1, source_target_pairs={{0,3},{1,2},{2,1},{3,0},{4,7},{5,6},{6,5},{7,4},{8,11},{9,10},{10,... | collective-permute-start | bytes 147464 | tf_op jit(solution)/shard_map/ppermute | solution.py:16
  62.6 2.9 %add_divide_fusion = f32[768,1280]{1,0:T(8,128)} fusion(f32[768,1280]{1,0:T(8,128)S(1)} %get-tuple-element.27), kind=kLoop, calls=%fused_computation.4 | loop fusion | flops 3932160 | bytes 7864320 | tf_op jit(solution)/shard_map/div | solution.py:115
  65.5 7.5 %collective-permute-start.14 = (bf16[48,1024]{1,0:T(8,128)(2,1)S(1)}, bf16[48,1024]{1,0:T(8,128)(2,1)S(1)}, u32[]{:S(2)}, u32[]{:S(2)}) collective-permute-start(bf16[48,1024]{1,0:T(8,128)(2,1)S(1)} %get-tuple-element.33), channel_id=1, source_target_pairs={{16,32},{48,64},{80,96},{112,128},{144,160},{176,192},{208,224},{3... | collective-permute-start | bytes 294920 | tf_op jit(solution)/shard_map/ppermute | solution.py:69
  75.9 2.5 %collective-permute-start.16 = (bf16[48,512]{1,0:T(8,128)(2,1)S(1)}, bf16[48,512]{1,0:T(8,128)(2,1)S(1)}, u32[]{:S(2)}, u32[]{:S(2)}) collective-permute-start(bf16[48,512]{1,0:T(8,128)(2,1)S(1)} %get-tuple-element.31), channel_id=1, source_target_pairs={{0,1},{1,0},{2,3},{3,2},{4,5},{5,4},{6,7},{7,6},{8,9},{9,8},{10,11... | collective-permute-start | bytes 147464 | tf_op jit(solution)/shard_map/ppermute | solution.py:16
  82.9 4.1 %collective-permute-done.17 = bf16[48,512]{1,0:T(8,128)(2,1)S(1)} collective-permute-done((bf16[48,512]{1,0:T(8,128)(2,1)S(1)}, bf16[48,512]{1,0:T(8,128)(2,1)S(1)}, u32[]{:S(2)}, u32[]{:S(2)}) %collective-permute-start.17) | collective-permute-done | bytes 49184 | tf_op jit(solution)/shard_map/ppermute | solution.py:16
  87.0 2.8 %collective-permute-start.21 = (bf16[192,512]{1,0:T(8,128)(2,1)S(1)}, bf16[192,512]{1,0:T(8,128)(2,1)S(1)}, u32[]{:S(2)}, u32[]{:S(2)}) collective-permute-start(bf16[192,512]{1,0:T(8,128)(2,1)S(1)} %pad_maximum_fusion.1), channel_id=1, source_target_pairs={{0,12},{4,8},{8,4},{12,0},{1,13},{5,9},{9,5},{13,1},{2,14},{6,10},... | collective-permute-start | bytes 589832 | tf_op jit(solution)/shard_map/ppermute | solution.py:16
  92.6 2.2 %collective-permute-start.28 = (bf16[192,1024]{1,0:T(8,128)(2,1)S(1)}, bf16[192,1024]{1,0:T(8,128)(2,1)S(1)}, u32[]{:S(2)}, u32[]{:S(2)}) collective-permute-start(bf16[192,1024]{1,0:T(8,128)(2,1)S(1)} %pad_maximum_fusion), channel_id=1, source_target_pairs={{0,12},{4,8},{8,4},{12,0},{1,13},{5,9},{9,5},{13,1},{2,14},{6,10},... | collective-permute-start | bytes 1179656 | tf_op jit(solution)/shard_map/ppermute | solution.py:16
  96.8 4.5 %collective-permute-done.19 = bf16[192,512]{1,0:T(8,128)(2,1)S(1)} collective-permute-done((bf16[192,512]{1,0:T(8,128)(2,1)S(1)}, bf16[192,512]{1,0:T(8,128)(2,1)S(1)}, u32[]{:S(2)}, u32[]{:S(2)}) %collective-permute-start.19) | collective-permute-done | bytes 196640 | tf_op jit(solution)/shard_map/ppermute | solution.py:16
  101.3 2.5 %collective-permute-start.27 = (bf16[192,1024]{1,0:T(8,128)(2,1)S(1)}, bf16[192,1024]{1,0:T(8,128)(2,1)S(1)}, u32[]{:S(2)}, u32[]{:S(2)}) collective-permute-start(bf16[192,1024]{1,0:T(8,128)(2,1)S(1)} %pad_maximum_fusion), channel_id=1, source_target_pairs={{0,8},{4,12},{8,0},{12,4},{1,9},{5,13},{9,1},{13,5},{2,10},{6,14},... | collective-permute-start | bytes 1179656 | tf_op jit(solution)/shard_map/ppermute | solution.py:16
  103.9 5.8 %collective-permute-done.26 = bf16[192,1024]{1,0:T(8,128)(2,1)S(1)} collective-permute-done((bf16[192,1024]{1,0:T(8,128)(2,1)S(1)}, bf16[192,1024]{1,0:T(8,128)(2,1)S(1)}, u32[]{:S(2)}, u32[]{:S(2)}) %collective-permute-start.26) | collective-permute-done | bytes 393248 | tf_op jit(solution)/shard_map/ppermute | solution.py:16
  109.8 9.8 %collective-permute-done.27 = bf16[192,1024]{1,0:T(8,128)(2,1)S(1)} collective-permute-done((bf16[192,1024]{1,0:T(8,128)(2,1)S(1)}, bf16[192,1024]{1,0:T(8,128)(2,1)S(1)}, u32[]{:S(2)}, u32[]{:S(2)}) %collective-permute-start.27) | collective-permute-done | bytes 393248 | tf_op jit(solution)/shard_map/ppermute | solution.py:16
  119.7 2.2 %fusion.12 = f32[768,1280]{1,0:T(8,128)S(1)} fusion(bf16[768,1024]{1,0:T(8,128)(2,1)S(1)} %constant_dynamic-update-slice_fusion.7, bf16[1280,1024]{1,0:T(8,128)(2,1)S(1)} %copy-done.7), kind=kOutput, calls=%fused_computation.51 | convolution fusion | flops 2013265920 | bytes 8126464 | tf_op jit(solution)/shard_map/dot_general | solution.py:77
  126.8 3.8 %fusion = bf16[1,1024,1280]{2,1,0:T(8,128)(2,1)} fusion(bf16[768,1024]{1,0:T(8,128)(2,1)S(1)} %bitcast.46, bf16[768,1280]{1,0:T(8,128)(2,1)S(1)} %multiply_convert_fusion.1), kind=kOutput, calls=%fused_computation.7 | convolution fusion | flops 2015887360 | bytes 6160384 | tf_op jit(solution)/shard_map/dot_general | solution.py:138
  (105 shorter events, 30.8 us)
Async XLA Ops:
  21.9 21.6 %collective-permute-start.3 = (bf16[192,1024]{1,0:T(8,128)(2,1)S(1)}, bf16[192,1024]{1,0:T(8,128)(2,1)S(1)}, u32[]{:S(2)}, u32[]{:S(2)}) collective-permute-start(bf16[192,1024]{1,0:T(8,128)(2,1)S(1)} %get-tuple-element.38), channel_id=1, source_target_pairs={{0,12},{4,8},{8,4},{12,0},{1,13},{5,9},{9,5},{13,1},{2,14},{6,10},... | collective-permute-start | bytes 1179656 | tf_op jit(solution)/shard_map/ppermute | solution.py:16
  24.7 19.1 %collective-permute-start.2 = (bf16[192,1024]{1,0:T(8,128)(2,1)S(1)}, bf16[192,1024]{1,0:T(8,128)(2,1)S(1)}, u32[]{:S(2)}, u32[]{:S(2)}) collective-permute-start(bf16[192,1024]{1,0:T(8,128)(2,1)S(1)} %get-tuple-element.39), channel_id=1, source_target_pairs={{0,8},{4,12},{8,0},{12,4},{1,9},{5,13},{9,1},{13,5},{2,10},{6,14},... | collective-permute-start | bytes 1179656 | tf_op jit(solution)/shard_map/ppermute | solution.py:16
  25.5 18.9 %collective-permute-start.1 = (bf16[192,1024]{1,0:T(8,128)(2,1)S(1)}, bf16[192,1024]{1,0:T(8,128)(2,1)S(1)}, u32[]{:S(2)}, u32[]{:S(2)}) collective-permute-start(bf16[192,1024]{1,0:T(8,128)(2,1)S(1)} %get-tuple-element.40), channel_id=1, source_target_pairs={{0,4},{4,0},{8,12},{12,8},{1,5},{5,1},{9,13},{13,9},{2,6},{6,2},{1... | collective-permute-start | bytes 1179656 | tf_op jit(solution)/shard_map/ppermute | solution.py:16
  27.3 24.2 %collective-permute-start.6 = (bf16[192,512]{1,0:T(8,128)(2,1)S(1)}, bf16[192,512]{1,0:T(8,128)(2,1)S(1)}, u32[]{:S(2)}, u32[]{:S(2)}) collective-permute-start(bf16[192,512]{1,0:T(8,128)(2,1)S(1)} %get-tuple-element.42), channel_id=1, source_target_pairs={{0,12},{4,8},{8,4},{12,0},{1,13},{5,9},{9,5},{13,1},{2,14},{6,10},... | collective-permute-start | bytes 589832 | tf_op jit(solution)/shard_map/ppermute | solution.py:16
  30.2 23.3 %collective-permute-start.5 = (bf16[192,512]{1,0:T(8,128)(2,1)S(1)}, bf16[192,512]{1,0:T(8,128)(2,1)S(1)}, u32[]{:S(2)}, u32[]{:S(2)}) collective-permute-start(bf16[192,512]{1,0:T(8,128)(2,1)S(1)} %get-tuple-element.43), channel_id=1, source_target_pairs={{0,8},{4,12},{8,0},{12,4},{1,9},{5,13},{9,1},{13,5},{2,10},{6,14},... | collective-permute-start | bytes 589832 | tf_op jit(solution)/shard_map/ppermute | solution.py:16
  43.5 9.9 %collective-permute-start.4 = (bf16[192,512]{1,0:T(8,128)(2,1)S(1)}, bf16[192,512]{1,0:T(8,128)(2,1)S(1)}, u32[]{:S(2)}, u32[]{:S(2)}) collective-permute-start(bf16[192,512]{1,0:T(8,128)(2,1)S(1)} %get-tuple-element.44), channel_id=1, source_target_pairs={{0,4},{4,0},{8,12},{12,8},{1,5},{5,1},{9,13},{13,9},{2,6},{6,2},{1... | collective-permute-start | bytes 589832 | tf_op jit(solution)/shard_map/ppermute | solution.py:16
  44.8 8.8 %collective-permute-start.9 = (bf16[48,1024]{1,0:T(8,128)(2,1)S(1)}, bf16[48,1024]{1,0:T(8,128)(2,1)S(1)}, u32[]{:S(2)}, u32[]{:S(2)}) collective-permute-start(bf16[48,1024]{1,0:T(8,128)(2,1)S(1)} %get-tuple-element.46), channel_id=1, source_target_pairs={{0,3},{1,2},{2,1},{3,0},{4,7},{5,6},{6,5},{7,4},{8,11},{9,10},{10,... | collective-permute-start | bytes 294920 | tf_op jit(solution)/shard_map/ppermute | solution.py:16
  58.0 15.0 %collective-permute-start.13 = (f32[48,512]{1,0:T(8,128)S(1)}, f32[48,512]{1,0:T(8,128)S(1)}, u32[]{:S(2)}, u32[]{:S(2)}) collective-permute-start(f32[48,512]{1,0:T(8,128)S(1)} %slice.110), channel_id=1, source_target_pairs={{0,16},{16,0},{32,48},{48,32},{64,80},{80,64},{96,112},{112,96},{1... | collective-permute-start | bytes 294920 | tf_op jit(solution)/shard_map/ppermute | solution.py:63
  58.1 14.9 %collective-permute-start.12 = (bf16[48,512]{1,0:T(8,128)(2,1)S(1)}, bf16[48,512]{1,0:T(8,128)(2,1)S(1)}, u32[]{:S(2)}, u32[]{:S(2)}) collective-permute-start(bf16[48,512]{1,0:T(8,128)(2,1)S(1)} %get-tuple-element.50), channel_id=1, source_target_pairs={{0,3},{1,2},{2,1},{3,0},{4,7},{5,6},{6,5},{7,4},{8,11},{9,10},{10,... | collective-permute-start | bytes 147464 | tf_op jit(solution)/shard_map/ppermute | solution.py:16
  61.5 11.4 %collective-permute-start.11 = (bf16[48,512]{1,0:T(8,128)(2,1)S(1)}, bf16[48,512]{1,0:T(8,128)(2,1)}, u32[]{:S(2)}, u32[]{:S(2)}) collective-permute-start(bf16[48,512]{1,0:T(8,128)(2,1)S(1)} %get-tuple-element.51), channel_id=1, source_target_pairs={{0,2},{1,3},{2,0},{3,1},{4,6},{5,7},{6,4},{7,5},{8,10},{9,11},{10,... | collective-permute-start | bytes 147464 | tf_op jit(solution)/shard_map/ppermute | solution.py:16
  61.5 11.5 %collective-permute-start.10 = (bf16[48,512]{1,0:T(8,128)(2,1)S(1)}, bf16[48,512]{1,0:T(8,128)(2,1)}, u32[]{:S(2)}, u32[]{:S(2)}) collective-permute-start(bf16[48,512]{1,0:T(8,128)(2,1)S(1)} %get-tuple-element.52), channel_id=1, source_target_pairs={{0,1},{1,0},{2,3},{3,2},{4,5},{5,4},{6,7},{7,6},{8,9},{9,8},{10,11... | collective-permute-start | bytes 147464 | tf_op jit(solution)/shard_map/ppermute | solution.py:16
  65.5 12.9 %collective-permute-start.14 = (bf16[48,1024]{1,0:T(8,128)(2,1)S(1)}, bf16[48,1024]{1,0:T(8,128)(2,1)S(1)}, u32[]{:S(2)}, u32[]{:S(2)}) collective-permute-start(bf16[48,1024]{1,0:T(8,128)(2,1)S(1)} %get-tuple-element.33), channel_id=1, source_target_pairs={{16,32},{48,64},{80,96},{112,128},{144,160},{176,192},{208,224},{3... | collective-permute-start | bytes 294920 | tf_op jit(solution)/shard_map/ppermute | solution.py:69
  75.9 11.1 %collective-permute-start.17 = (bf16[48,512]{1,0:T(8,128)(2,1)S(1)}, bf16[48,512]{1,0:T(8,128)(2,1)S(1)}, u32[]{:S(2)}, u32[]{:S(2)}) collective-permute-start(bf16[48,512]{1,0:T(8,128)(2,1)S(1)} %get-tuple-element.31), channel_id=1, source_target_pairs={{0,2},{1,3},{2,0},{3,1},{4,6},{5,7},{6,4},{7,5},{8,10},{9,11},{10,... | collective-permute-start | bytes 147464 | tf_op jit(solution)/shard_map/ppermute | solution.py:16
  75.9 11.1 %collective-permute-start.16 = (bf16[48,512]{1,0:T(8,128)(2,1)S(1)}, bf16[48,512]{1,0:T(8,128)(2,1)S(1)}, u32[]{:S(2)}, u32[]{:S(2)}) collective-permute-start(bf16[48,512]{1,0:T(8,128)(2,1)S(1)} %get-tuple-element.31), channel_id=1, source_target_pairs={{0,1},{1,0},{2,3},{3,2},{4,5},{5,4},{6,7},{7,6},{8,9},{9,8},{10,11... | collective-permute-start | bytes 147464 | tf_op jit(solution)/shard_map/ppermute | solution.py:16
  78.4 11.5 %collective-permute-start.25 = (bf16[48,1024]{1,0:T(8,128)(2,1)S(1)}, bf16[48,1024]{1,0:T(8,128)(2,1)S(1)}, u32[]{:S(2)}, u32[]{:S(2)}) collective-permute-start(bf16[48,1024]{1,0:T(8,128)(2,1)S(1)} %get-tuple-element.29), channel_id=1, source_target_pairs={{0,3},{1,2},{2,1},{3,0},{4,7},{5,6},{6,5},{7,4},{8,11},{9,10},{10,... | collective-permute-start | bytes 294920 | tf_op jit(solution)/shard_map/ppermute | solution.py:16
  80.4 11.3 %collective-permute-start.24 = (bf16[48,1024]{1,0:T(8,128)(2,1)S(1)}, bf16[48,1024]{1,0:T(8,128)(2,1)S(1)}, u32[]{:S(2)}, u32[]{:S(2)}) collective-permute-start(bf16[48,1024]{1,0:T(8,128)(2,1)S(1)} %get-tuple-element.29), channel_id=1, source_target_pairs={{0,2},{1,3},{2,0},{3,1},{4,6},{5,7},{6,4},{7,5},{8,10},{9,11},{10,... | collective-permute-start | bytes 294920 | tf_op jit(solution)/shard_map/ppermute | solution.py:16
  81.1 11.5 %collective-permute-start.23 = (bf16[48,1024]{1,0:T(8,128)(2,1)S(1)}, bf16[48,1024]{1,0:T(8,128)(2,1)S(1)}, u32[]{:S(2)}, u32[]{:S(2)}) collective-permute-start(bf16[48,1024]{1,0:T(8,128)(2,1)S(1)} %get-tuple-element.29), channel_id=1, source_target_pairs={{0,1},{1,0},{2,3},{3,2},{4,5},{5,4},{6,7},{7,6},{8,9},{9,8},{10,11... | collective-permute-start | bytes 294920 | tf_op jit(solution)/shard_map/ppermute | solution.py:16
  87.0 16.8 %collective-permute-start.21 = (bf16[192,512]{1,0:T(8,128)(2,1)S(1)}, bf16[192,512]{1,0:T(8,128)(2,1)S(1)}, u32[]{:S(2)}, u32[]{:S(2)}) collective-permute-start(bf16[192,512]{1,0:T(8,128)(2,1)S(1)} %pad_maximum_fusion.1), channel_id=1, source_target_pairs={{0,12},{4,8},{8,4},{12,0},{1,13},{5,9},{9,5},{13,1},{2,14},{6,10},... | collective-permute-start | bytes 589832 | tf_op jit(solution)/shard_map/ppermute | solution.py:16
  89.9 13.9 %collective-permute-start.20 = (bf16[192,512]{1,0:T(8,128)(2,1)S(1)}, bf16[192,512]{1,0:T(8,128)(2,1)S(1)}, u32[]{:S(2)}, u32[]{:S(2)}) collective-permute-start(bf16[192,512]{1,0:T(8,128)(2,1)S(1)} %pad_maximum_fusion.1), channel_id=1, source_target_pairs={{0,8},{4,12},{8,0},{12,4},{1,9},{5,13},{9,1},{13,5},{2,10},{6,14},... | collective-permute-start | bytes 589832 | tf_op jit(solution)/shard_map/ppermute | solution.py:16
  91.7 9.6 %collective-permute-start.19 = (bf16[192,512]{1,0:T(8,128)(2,1)S(1)}, bf16[192,512]{1,0:T(8,128)(2,1)S(1)}, u32[]{:S(2)}, u32[]{:S(2)}) collective-permute-start(bf16[192,512]{1,0:T(8,128)(2,1)S(1)} %pad_maximum_fusion.1), channel_id=1, source_target_pairs={{0,4},{4,0},{8,12},{12,8},{1,5},{5,1},{9,13},{13,9},{2,6},{6,2},{1... | collective-permute-start | bytes 589832 | tf_op jit(solution)/shard_map/ppermute | solution.py:16
  92.6 27.0 %collective-permute-start.28 = (bf16[192,1024]{1,0:T(8,128)(2,1)S(1)}, bf16[192,1024]{1,0:T(8,128)(2,1)S(1)}, u32[]{:S(2)}, u32[]{:S(2)}) collective-permute-start(bf16[192,1024]{1,0:T(8,128)(2,1)S(1)} %pad_maximum_fusion), channel_id=1, source_target_pairs={{0,12},{4,8},{8,4},{12,0},{1,13},{5,9},{9,5},{13,1},{2,14},{6,10},... | collective-permute-start | bytes 1179656 | tf_op jit(solution)/shard_map/ppermute | solution.py:16
  94.9 14.9 %collective-permute-start.26 = (bf16[192,1024]{1,0:T(8,128)(2,1)S(1)}, bf16[192,1024]{1,0:T(8,128)(2,1)S(1)}, u32[]{:S(2)}, u32[]{:S(2)}) collective-permute-start(bf16[192,1024]{1,0:T(8,128)(2,1)S(1)} %pad_maximum_fusion), channel_id=1, source_target_pairs={{0,4},{4,0},{8,12},{12,8},{1,5},{5,1},{9,13},{13,9},{2,6},{6,2},{1... | collective-permute-start | bytes 1179656 | tf_op jit(solution)/shard_map/ppermute | solution.py:16
  101.3 18.3 %collective-permute-start.27 = (bf16[192,1024]{1,0:T(8,128)(2,1)S(1)}, bf16[192,1024]{1,0:T(8,128)(2,1)S(1)}, u32[]{:S(2)}, u32[]{:S(2)}) collective-permute-start(bf16[192,1024]{1,0:T(8,128)(2,1)S(1)} %pad_maximum_fusion), channel_id=1, source_target_pairs={{0,8},{4,12},{8,0},{12,4},{1,9},{5,13},{9,1},{13,5},{2,10},{6,14},... | collective-permute-start | bytes 1179656 | tf_op jit(solution)/shard_map/ppermute | solution.py:16
  103.8 18.1 %collective-permute-start.22 = (bf16[768,512]{1,0:T(8,128)(2,1)S(1)}, bf16[768,512]{1,0:T(8,128)(2,1)S(1)}, u32[]{:S(2)}, u32[]{:S(2)}) collective-permute-start(bf16[768,512]{1,0:T(8,128)(2,1)S(1)} %constant_dynamic-update-slice_fusion), channel_id=1, source_target_pairs={{0,16},{16,0},{32,48},{48,32},{64,80},{80,64},{96,112},{112,96},{1... | collective-permute-start | bytes 2359304 | tf_op jit(solution)/shard_map/ppermute | solution.py:63
  (19 other events, 122.1 us)

commit v3 on v2

v3 whole, which is shorter than its diff:
```python
import jax
import jax.numpy as jnp
from jax import lax
from jax.experimental import pallas as pl
from jax.experimental.pallas import tpu as pltpu
from jax.sharding import Mesh
from jax.sharding import PartitionSpec as P

FEAT = ("feat_0", "feat_1")
SIDE = 4
HIGH = jnp.float32
LOW = jnp.bfloat16


def exchanged(piece, axis, step):
    return lax.ppermute(piece, axis, [(i, i ^ step) for i in range(SIDE)])


def after(value, *others):
    return lax.optimization_barrier((value, *others))[0]


def sorted_kernel(blocks, decoder, rows, main, keep, give):
    first = lax.axis_index("layer") % 2 == 0
    half = keep.shape[1]

    @pl.when(pl.program_id(0) == 0)
    def _():
        x = lax.axis_index(FEAT[0])
        z = lax.axis_index(FEAT[1])
        for i in range(SIDE):
            for j in range(SIDE):
                rows[i * SIDE + j] = blocks[(x ^ i) * SIDE + (z ^ j)]

    planes = jnp.swapaxes(decoder[...], 0, 1)
    own = planes[0]
    later = planes[1]
    main[...] = jnp.where(first, own, later)
    keep[...] = jnp.where(first, later[:, :half], own[:, half:])
    give[...] = jnp.where(first, later[:, half:], own[:, :half])


def sorted_inputs(acts, decoder):
    tokens, width = acts.shape
    features = decoder.shape[0]
    blocks = acts.reshape(SIDE * SIDE, -1, width)
    tile = 256
    half = width // 2
    rows, main, keep, give = pl.pallas_call(
        sorted_kernel,
        grid=(features // tile,),
        in_specs=[
            pl.BlockSpec(blocks.shape, lambda n: (0, 0, 0)),
            pl.BlockSpec((tile, 2, width), lambda n: (n, 0, 0)),
        ],
        out_specs=[
            pl.BlockSpec(blocks.shape, lambda n: (0, 0, 0)),
            pl.BlockSpec((tile, width), lambda n: (n, 0)),
            pl.BlockSpec((tile, half), lambda n: (n, 0)),
            pl.BlockSpec((tile, half), lambda n: (n, 0)),
        ],
        out_shape=[
            jax.ShapeDtypeStruct(blocks.shape, acts.dtype),
            jax.ShapeDtypeStruct((features, width), decoder.dtype),
            jax.ShapeDtypeStruct((features, half), decoder.dtype),
            jax.ShapeDtypeStruct((features, half), decoder.dtype),
        ],
        compiler_params=pltpu.CompilerParams(vmem_limit_bytes=24 * 2**20),
        name="sorted_inputs",
    )(blocks, decoder)
    return rows.reshape(tokens, width), main, keep, give


def row_pieces(array):
    rows = array.shape[0] // SIDE
    return [array[i * rows : (i + 1) * rows] for i in range(SIDE)]


def received(pieces, axis):
    return [exchanged(pieces[step], axis, step) for step in range(1, SIDE)]


def totalled(piece, parts):
    total = piece.astype(HIGH)
    for part in parts:
        total = total + part.astype(HIGH)
    return total


def together(*values):
    return lax.optimization_barrier(values)


def on_chip(value):
    layers = lax.axis_size("layer")
    return lax.ppermute(value, "layer", [(i, i ^ 1) for i in range(layers)])


def across_chips(value):
    layers = lax.axis_size("layer")
    pairs = [(i, i + 1) for i in range(1, layers - 1, 2)]
    return lax.ppermute(value, "layer", pairs + [(j, i) for i, j in pairs])


def dot(a, b):
    return jnp.dot(a, b, preferred_element_type=HIGH)


def contract_width(errs, decoder):
    return lax.dot_general(errs, decoder, (((1,), (1,)), ((), ())), preferred_element_type=HIGH)


def local(acts, targets, enc_weight, enc_bias, dec_weight, dec_bias):
    weight = enc_weight[0]
    bias = enc_bias[0]
    decoder = dec_weight[0]
    tokens, width = acts.shape[1:]
    half = width // 2
    layer = lax.axis_index("layer")
    first = layer % 2 == 0
    ends = layer == lax.axis_size("layer") - 1

    inputs, main, keep, give = sorted_inputs(acts[0], decoder)

    pre = dot(inputs, weight) + bias
    scaled = 4.0 * pre
    small = jnp.exp(-jnp.abs(scaled))
    latent = ((jnp.maximum(scaled, 0.0) + jnp.log1p(small)) * 0.25).astype(LOW)
    latent, pre = lax.optimization_barrier((latent, pre))

    given, latent = together(dot(latent, give).astype(LOW), latent)
    given = on_chip(given)
    pieces = row_pieces(dot(latent, main).astype(LOW))
    pieces, latent, pre, lift, inputs = together(pieces, latent, pre, dec_bias[0], inputs)
    parts = received(pieces, FEAT[0])

    shared = (dot(latent, keep) + given.astype(HIGH)).astype(LOW)
    shared = shared.reshape(SIDE, SIDE, -1, half)
    side = together(*[shared[:, i].reshape(-1, half) for i in range(SIDE)])
    side_parts = received(side, FEAT[1])
    offset = lift - targets[0].astype(HIGH)
    peer_offset = on_chip(offset[:, :half])
    deriv, turned = together(jax.nn.sigmoid(4.0 * pre), inputs.T)

    piece, parts, side, side_parts, deriv, peer_offset, turned = together(
        pieces[0], parts, side[0], side_parts, deriv, peer_offset, turned
    )
    pieces = row_pieces(totalled(piece, parts).astype(LOW))
    side = row_pieces(totalled(side, side_parts).astype(LOW))

    pieces, side = together(pieces, side)
    parts = received(pieces, FEAT[1])
    side_parts = received(side, FEAT[0])

    piece, parts, side, side_parts = together(pieces[0], parts, side[0], side_parts)
    part = totalled(piece, parts) + jnp.where(first, offset, 0.0)
    shared = totalled(side, side_parts) + jnp.where(first, peer_offset, offset[:, half:])

    part, sent, shared, block = together(part, part.astype(LOW), shared, shared.astype(LOW))
    arrived = across_chips(sent)
    tiles = received([block] * SIDE, FEAT[1])
    other = on_chip(shared)

    part, arrived, block, tiles, other = together(part, arrived, block, tiles, other)
    part = part + arrived.astype(HIGH)
    rows = jnp.where(ends, 0.0, part).astype(LOW)
    block = jnp.concatenate([block, *tiles], 0)

    rows, block, part = together(rows, block, part)
    parts = received([rows] * SIDE, FEAT[1])
    tiles = received([block] * SIDE, FEAT[0])
    errors = jnp.where(first, part, jnp.concatenate([other, shared], 1))

    rows, parts, block, tiles, errors = together(rows, parts, block, tiles, errors)
    rows = jnp.concatenate([rows, *parts], 0)
    shared_rows = jnp.concatenate([block, *tiles], 0)

    rows, shared_rows = together(rows, shared_rows)
    parts = received([rows] * SIDE, FEAT[0])
    other_rows = on_chip(shared_rows)
    grad_latent = contract_width(shared_rows, keep) + contract_width(other_rows, give)

    grad_latent, rows, parts = together(grad_latent, rows, parts)
    main_rows = jnp.concatenate([rows, *parts], 0)
    grad_latent = grad_latent + contract_width(main_rows, main)
    grad_pre = after((grad_latent * deriv).astype(LOW))
    enc_grad = (dot(turned, grad_pre) * tokens ** (-0.5)).astype(LOW)
    return (errors[None], enc_grad[None])


def solution(mesh):
    finer = Mesh(mesh.devices.reshape(mesh.shape["layer"], SIDE, SIDE), ("layer", *FEAT))
    in_specs = (
        P("layer", None, None),
        P("layer", FEAT, None),
        P("layer", None, FEAT),
        P("layer", FEAT),
        P("layer", FEAT, None, None),
        P("layer", None),
    )
    out_specs = (P("layer", FEAT, None), P("layer", None, FEAT))
    return jax.shard_map(local, mesh=finer, in_specs=in_specs, out_specs=out_specs, check_vma=False)
```

time: 131 us -> 127 us (0.969)
  starting transfers between devices: 45.8 us -> 52.5 us
  waiting for transfers between devices: 45.4 us -> 40.3 us
  local copies, waits for them, and re-layouts: 9.32 us -> 5.99 us
  matrix products: 18.3 us -> 16.7 us
    ppermute x24, starting transfers between devices: 38 us -> 44.6 us  [exchanged(): return lax.ppermute(piece, axis, [(i, i ^ step) for i in range(SIDE)])]
    ppermute x24, waiting for transfers between devices: 45.4 us -> 40.3 us  [exchanged(): return lax.ppermute(piece, axis, [(i, i ^ step) for i in range(SIDE)])]
    dot_general x1 -> x0, matrix products: 3.75 us -> none  [local(): lax.dot_general(inputs, grad_pre, (((0,), (0,)), ((), ())), preferred_ele...]
    ppermute x4, starting transfers between devices: 0.34 us -> 3.75 us  [on_chip(): return lax.ppermute(value, 'layer', [(i, i ^ 1) for i in range(layers)])]
    unnamed x39 -> x30, local copies, waits for them, and re-layouts: 8.46 us -> 5.12 us
    ppermute x1, starting transfers between devices: 7.48 us -> 4.21 us  [across_chips(): return lax.ppermute(value, 'layer', pairs + [(j, i) for i, j in pairs])]
    dot_general x4 -> x5, matrix products: 9.85 us -> 12 us  [dot(): return jnp.dot(a, b, preferred_element_type=HIGH)]
    convert_element_type x3 -> x5, other arithmetic: 0.45 us -> 2.32 us  [the longest x1 1.04 us: local(): part.astype(LOW)]
  transfers between devices with their start and end apart: 29 -> 29, of which waited for: 10 -> 15; matrix products, arithmetic and copies ran while one was open for 7% -> 8% of each run, Pallas kernels for 0% -> 0%
where the time goes in v3:
time: 127 us
  starting transfers between devices  52.5 us (41%)
  waiting for transfers between devices  40.3 us (32%)
  matrix products  16.7 us (13%)
  other arithmetic  8.53 us (7%)
  local copies, waits for them, and re-layouts  5.99 us (5%)
  Pallas kernels  1.57 us (1%)
    ppermute x24, starting transfers between devices, exchanged(): return lax.ppermute(piece, axis, [(i, i ^ step) for i in range(SIDE)])  44.6 us
    ppermute x24, waiting for transfers between devices, exchanged(): return lax.ppermute(piece, axis, [(i, i ^ step) for i in range(SIDE)])  40.3 us
    dot_general x5, matrix products, dot(): return jnp.dot(a, b, preferred_element_type=HIGH)  12 us
    unnamed x30, local copies, waits for them, and re-layouts  5.12 us
    dot_general x3, matrix products, contract_width(): lax.dot_general(errs, decoder, (((1,), (1,)), ((), ())), preferred_elemen...  4.72 us
    ppermute x1, starting transfers between devices, across_chips(): return lax.ppermute(value, 'layer', pairs + [(j, i) for i, j in pairs])  4.21 us
    ppermute x4, starting transfers between devices, on_chip(): return lax.ppermute(value, 'layer', [(i, i ^ 1) for i in range(layers)])  3.75 us
    div x1, other arithmetic, local(): deriv, turned = together(jax.nn.sigmoid(4.0 * pre), inputs.T)  2.9 us
  transfers between devices with their start and end apart: 29, of which 15 were waited for; matrix products, arithmetic and copies ran while one was open for 8% of the time, Pallas kernels for 0%

profile of v3, /device:TPU:8, one launch (start us, length us, event | category | flops | bytes accessed | tf_op | source)
XLA Modules:
  0.0 126.6 jit_solution(12139730866695058579)
XLA Ops:
  1.5 2.5 %copy-done.1 = bf16[1,1280,2,1024]{3,2,1,0:T(2,128)(2,1)S(1)} copy-done((bf16[1,1280,2,1024]{3,2,1,0:T(2,128)(2,1)S(1)}, bf16[1,1280,2,1024]{3,2,1,0:T(2,128)(2,1)}, u32[]{:S(2)}) %copy-start.1) | copy-done | bytes 5242904
  7.0 3.7 %multiply_convert_fusion.2 = (bf16[768,1280]{1,0:T(8,128)(2,1)S(1)}, f32[768,1280]{1,0:T(8,128)S(1)}) fusion(f32[1280]{0:T(1024)S(1)} %reduce, bf16[768,1024]{1,0:T(8,128)(2,1)S(1)} %bitcast.40, bf16[1,1024,1280]{2,1,0:T(8,128)(2,1)S(1)} %copy-done), kind=kOutput, calls=%fused_computation.4 | convolution fusion | flops 2021130240 | bytes 10097664 | tf_op jit(solution)/shard_map/dot_general | solution.py:106
  12.1 2.2 %convolution_convert_fusion = bf16[768,1024]{1,0:T(8,128)(2,1)S(1)} fusion(bf16[768,1280]{1,0:T(8,128)(2,1)S(1)} %get-tuple-element.91, bf16[1280,1024]{1,0:T(8,128)(2,1)S(1)} %get-tuple-element.85), kind=kOutput, calls=%fused_computation.8 | convolution fusion | flops 2014052352 | bytes 6160384 | tf_op jit(solution)/shard_map/dot_general | solution.py:106
  16.0 2.7 %collective-permute-start.1 = (bf16[192,1024]{1,0:T(8,128)(2,1)S(1)}, bf16[192,1024]{1,0:T(8,128)(2,1)S(1)}, u32[]{:S(2)}, u32[]{:S(2)}) collective-permute-start(bf16[192,1024]{1,0:T(8,128)(2,1)S(1)} %get-tuple-element.89), channel_id=1, source_target_pairs={{0,8},{4,12},{8,0},{12,4},{1,9},{5,13},{9,1},{13,5},{2,10},{6,14},... | collective-permute-start | bytes 1179656 | tf_op jit(solution)/shard_map/ppermute | solution.py:16
  22.7 3.3 %collective-permute-start.5 = (bf16[192,512]{1,0:T(8,128)(2,1)S(1)}, bf16[192,512]{1,0:T(8,128)(2,1)S(1)}, u32[]{:S(2)}, u32[]{:S(2)}) collective-permute-start(bf16[192,512]{1,0:T(8,128)(2,1)S(1)} %bitcast.45), channel_id=1, source_target_pairs={{0,2},{1,3},{2,0},{3,1},{4,6},{5,7},{6,4},{7,5},{8,10},{9,11},{10,... | collective-permute-start | bytes 589832 | tf_op jit(solution)/shard_map/ppermute | solution.py:16
  26.4 4.6 %collective-permute-start.6 = (bf16[192,512]{1,0:T(8,128)(2,1)S(1)}, bf16[192,512]{1,0:T(8,128)(2,1)S(1)}, u32[]{:S(2)}, u32[]{:S(2)}) collective-permute-start(bf16[192,512]{1,0:T(8,128)(2,1)S(1)} %bitcast.44), channel_id=1, source_target_pairs={{0,3},{1,2},{2,1},{3,0},{4,7},{5,6},{6,5},{7,4},{8,11},{9,10},{10,... | collective-permute-start | bytes 589832 | tf_op jit(solution)/shard_map/ppermute | solution.py:16
  31.1 2.9 %add_divide_fusion = f32[768,1280]{1,0:T(8,128)} fusion(f32[768,1280]{1,0:T(8,128)S(1)} %get-tuple-element.98), kind=kLoop, calls=%fused_computation.3 | loop fusion | flops 3932160 | bytes 7864320 | tf_op jit(solution)/shard_map/div | solution.py:143
  34.0 2.8 %collective-permute-done.1 = bf16[192,1024]{1,0:T(8,128)(2,1)S(1)} collective-permute-done((bf16[192,1024]{1,0:T(8,128)(2,1)S(1)}, bf16[192,1024]{1,0:T(8,128)(2,1)S(1)}, u32[]{:S(2)}, u32[]{:S(2)}) %collective-permute-start.1) | collective-permute-done | bytes 393248 | tf_op jit(solution)/shard_map/ppermute | solution.py:16
  36.8 2.6 %collective-permute-done.2 = bf16[192,1024]{1,0:T(8,128)(2,1)S(1)} collective-permute-done((bf16[192,1024]{1,0:T(8,128)(2,1)S(1)}, bf16[192,1024]{1,0:T(8,128)(2,1)S(1)}, u32[]{:S(2)}, u32[]{:S(2)}) %collective-permute-start.2) | collective-permute-done | bytes 393248 | tf_op jit(solution)/shard_map/ppermute | solution.py:16
  41.4 4.4 %collective-permute-start.8 = (bf16[48,1024]{1,0:T(8,128)(2,1)S(1)}, bf16[48,1024]{1,0:T(8,128)(2,1)S(1)}, u32[]{:S(2)}, u32[]{:S(2)}) collective-permute-start(bf16[48,1024]{1,0:T(8,128)(2,1)S(1)} %get-tuple-element.112), channel_id=1, source_target_pairs={{0,1},{1,0},{2,3},{3,2},{4,5},{5,4},{6,7},{7,6},{8,9},{9,8},{10,11... | collective-permute-start | bytes 294920 | tf_op jit(solution)/shard_map/ppermute | solution.py:16
  48.3 3.9 %collective-permute-start.12 = (bf16[48,512]{1,0:T(8,128)(2,1)}, bf16[48,512]{1,0:T(8,128)(2,1)}, u32[]{:S(2)}, u32[]{:S(2)}) collective-permute-start(bf16[48,512]{1,0:T(8,128)(2,1)} %get-tuple-element.117), channel_id=1, source_target_pairs={{0,8},{4,12},{8,0},{12,4},{1,9},{5,13},{9,1},{13,5},{2,10},{6,14},... | collective-permute-start | bytes 147464 | tf_op jit(solution)/shard_map/ppermute | solution.py:16
  54.6 3.2 %collective-permute-done.13 = bf16[48,512]{1,0:T(8,128)(2,1)} collective-permute-done((bf16[48,512]{1,0:T(8,128)(2,1)}, bf16[48,512]{1,0:T(8,128)(2,1)}, u32[]{:S(2)}, u32[]{:S(2)}) %collective-permute-start.13) | collective-permute-done | bytes 49184 | tf_op jit(solution)/shard_map/ppermute | solution.py:16
  59.8 4.2 %collective-permute-start.14 = (bf16[48,1024]{1,0:T(8,128)(2,1)S(1)}, bf16[48,1024]{1,0:T(8,128)(2,1)S(1)}, u32[]{:S(2)}, u32[]{:S(2)}) collective-permute-start(bf16[48,1024]{1,0:T(8,128)(2,1)S(1)} %get-tuple-element.129), channel_id=1, source_target_pairs={{16,32},{48,64},{80,96},{112,128},{144,160},{176,192},{208,224},{3... | collective-permute-start | bytes 294920 | tf_op jit(solution)/shard_map/ppermute | solution.py:102
  64.0 3.5 %collective-permute-start.18 = (f32[48,512]{1,0:T(8,128)S(1)}, f32[48,512]{1,0:T(8,128)S(1)}, u32[]{:S(2)}, u32[]{:S(2)}) collective-permute-start(f32[48,512]{1,0:T(8,128)S(1)} %get-tuple-element.131), channel_id=1, source_target_pairs={{0,16},{16,0},{32,48},{48,32},{64,80},{80,64},{96,112},{112,96},{1... | collective-permute-start | bytes 294920 | tf_op jit(solution)/shard_map/ppermute | solution.py:96
  72.6 4.0 %collective-permute-done.16 = bf16[48,512]{1,0:T(8,128)(2,1)S(1)} collective-permute-done((bf16[48,512]{1,0:T(8,128)(2,1)S(1)}, bf16[48,512]{1,0:T(8,128)(2,1)S(1)}, u32[]{:S(2)}, u32[]{:S(2)}) %collective-permute-start.16) | collective-permute-done | bytes 49184 | tf_op jit(solution)/shard_map/ppermute | solution.py:16
  82.7 2.4 %collective-permute-start.23 = (bf16[192,512]{1,0:T(8,128)(2,1)S(1)}, bf16[192,512]{1,0:T(8,128)(2,1)S(1)}, u32[]{:S(2)}, u32[]{:S(2)}) collective-permute-start(bf16[192,512]{1,0:T(8,128)(2,1)S(1)} %pad_maximum_fusion.2), channel_id=1, source_target_pairs={{0,8},{4,12},{8,0},{12,4},{1,9},{5,13},{9,1},{13,5},{2,10},{6,14},... | collective-permute-start | bytes 589832 | tf_op jit(solution)/shard_map/ppermute | solution.py:16
  89.9 3.5 %collective-permute-done.23 = bf16[192,512]{1,0:T(8,128)(2,1)S(1)} collective-permute-done((bf16[192,512]{1,0:T(8,128)(2,1)S(1)}, bf16[192,512]{1,0:T(8,128)(2,1)S(1)}, u32[]{:S(2)}, u32[]{:S(2)}) %collective-permute-start.23) | collective-permute-done | bytes 196640 | tf_op jit(solution)/shard_map/ppermute | solution.py:16
  93.4 2.4 %collective-permute-done.24 = bf16[192,512]{1,0:T(8,128)(2,1)S(1)} collective-permute-done((bf16[192,512]{1,0:T(8,128)(2,1)S(1)}, bf16[192,512]{1,0:T(8,128)(2,1)S(1)}, u32[]{:S(2)}, u32[]{:S(2)}) %collective-permute-start.24) | collective-permute-done | bytes 196640 | tf_op jit(solution)/shard_map/ppermute | solution.py:16
  96.2 2.5 %collective-permute-start.27 = (bf16[192,1024]{1,0:T(8,128)(2,1)S(1)}, bf16[192,1024]{1,0:T(8,128)(2,1)S(1)}, u32[]{:S(2)}, u32[]{:S(2)}) collective-permute-start(bf16[192,1024]{1,0:T(8,128)(2,1)S(1)} %pad_maximum_fusion.1), channel_id=1, source_target_pairs={{0,8},{4,12},{8,0},{12,4},{1,9},{5,13},{9,1},{13,5},{2,10},{6,14},... | collective-permute-start | bytes 1179656 | tf_op jit(solution)/shard_map/ppermute | solution.py:16
  103.3 4.7 %collective-permute-done.26 = bf16[192,1024]{1,0:T(8,128)(2,1)S(1)} collective-permute-done((bf16[192,1024]{1,0:T(8,128)(2,1)S(1)}, bf16[192,1024]{1,0:T(8,128)(2,1)S(1)}, u32[]{:S(2)}, u32[]{:S(2)}) %collective-permute-start.26) | collective-permute-done | bytes 393248 | tf_op jit(solution)/shard_map/ppermute | solution.py:16
  108.0 8.6 %collective-permute-done.27 = bf16[192,1024]{1,0:T(8,128)(2,1)S(1)} collective-permute-done((bf16[192,1024]{1,0:T(8,128)(2,1)S(1)}, bf16[192,1024]{1,0:T(8,128)(2,1)S(1)}, u32[]{:S(2)}, u32[]{:S(2)}) %collective-permute-start.27) | collective-permute-done | bytes 393248 | tf_op jit(solution)/shard_map/ppermute | solution.py:16
  116.6 2.6 %collective-permute-done.28 = bf16[192,1024]{1,0:T(8,128)(2,1)S(1)} collective-permute-done((bf16[192,1024]{1,0:T(8,128)(2,1)S(1)}, bf16[192,1024]{1,0:T(8,128)(2,1)S(1)}, u32[]{:S(2)}, u32[]{:S(2)}) %collective-permute-start.28) | collective-permute-done | bytes 393248 | tf_op jit(solution)/shard_map/ppermute | solution.py:16
  119.2 2.2 %fusion.2 = f32[768,1280]{1,0:T(8,128)S(1)} fusion(bf16[1280,1024]{1,0:T(8,128)(2,1)S(1)} %copy-done.6, bf16[192,1024]{1,0:T(8,128)(2,1)S(1)} %collective-permute-done.28, bf16[192,1024]{1,0:T(8,128)(2,1)S(1)} %collective-permute-done.27, bf16[192,1024]{1,0:T(8,128)(2,1)S(1)} %collective-permute-done.26, bf16[192,1024]{1,0:T(8,128)(2,1)S(1)} %pad_maximum_fusion.1), kind=kOutput, calls=%fused_computation.9 | convolution fusion | flops 2019557376 | bytes 8126464 | tf_op jit(solution)/shard_map/dot_general | solution.py:110
  122.9 3.8 %fusion = bf16[1,1024,1280]{2,1,0:T(8,128)(2,1)} fusion(bf16[1024,768]{0,1:T(8,128)(2,1)S(1)} %bitcast.41, bf16[768,1280]{1,0:T(8,128)(2,1)S(1)} %multiply_convert_fusion.1), kind=kOutput, calls=%fused_computation.6 | convolution fusion | flops 2015887360 | bytes 6160384 | tf_op jit(solution)/shard_map/dot_general | solution.py:106
  (91 shorter events, 42.4 us)
Async XLA Ops:
  12.0 7.4 %collective-permute-start.3 = (bf16[768,512]{1,0:T(8,128)(2,1)S(1)}, bf16[768,512]{1,0:T(8,128)(2,1)S(1)}, u32[]{:S(2)}, u32[]{:S(2)}) collective-permute-start(bf16[768,512]{1,0:T(8,128)(2,1)S(1)} %convolution_convert_fusion.1), channel_id=1, source_target_pairs={{0,16},{16,0},{32,48},{48,32},{64,80},{80,64},{96,112},{112,96},{1... | collective-permute-start | bytes 2359304 | tf_op jit(solution)/shard_map/ppermute | solution.py:96
  14.4 12.0 %collective-permute-start = (bf16[192,1024]{1,0:T(8,128)(2,1)S(1)}, bf16[192,1024]{1,0:T(8,128)(2,1)S(1)}, u32[]{:S(2)}, u32[]{:S(2)}) collective-permute-start(bf16[192,1024]{1,0:T(8,128)(2,1)S(1)} %get-tuple-element.88), channel_id=1, source_target_pairs={{0,4},{4,0},{8,12},{12,8},{1,5},{5,1},{9,13},{13,9},{2,6},{6,2},{1... | collective-permute-start | bytes 1179656 | tf_op jit(solution)/shard_map/ppermute | solution.py:16
  16.0 20.7 %collective-permute-start.1 = (bf16[192,1024]{1,0:T(8,128)(2,1)S(1)}, bf16[192,1024]{1,0:T(8,128)(2,1)S(1)}, u32[]{:S(2)}, u32[]{:S(2)}) collective-permute-start(bf16[192,1024]{1,0:T(8,128)(2,1)S(1)} %get-tuple-element.89), channel_id=1, source_target_pairs={{0,8},{4,12},{8,0},{12,4},{1,9},{5,13},{9,1},{13,5},{2,10},{6,14},... | collective-permute-start | bytes 1179656 | tf_op jit(solution)/shard_map/ppermute | solution.py:16
  18.8 20.6 %collective-permute-start.2 = (bf16[192,1024]{1,0:T(8,128)(2,1)S(1)}, bf16[192,1024]{1,0:T(8,128)(2,1)S(1)}, u32[]{:S(2)}, u32[]{:S(2)}) collective-permute-start(bf16[192,1024]{1,0:T(8,128)(2,1)S(1)} %get-tuple-element.90), channel_id=1, source_target_pairs={{0,12},{4,8},{8,4},{12,0},{1,13},{5,9},{9,5},{13,1},{2,14},{6,10},... | collective-permute-start | bytes 1179656 | tf_op jit(solution)/shard_map/ppermute | solution.py:16
  20.6 18.7 %collective-permute-start.4 = (bf16[192,512]{1,0:T(8,128)(2,1)S(1)}, bf16[192,512]{1,0:T(8,128)(2,1)S(1)}, u32[]{:S(2)}, u32[]{:S(2)}) collective-permute-start(bf16[192,512]{1,0:T(8,128)(2,1)S(1)} %bitcast.46), channel_id=1, source_target_pairs={{0,1},{1,0},{2,3},{3,2},{4,5},{5,4},{6,7},{7,6},{8,9},{9,8},{10,11... | collective-permute-start | bytes 589832 | tf_op jit(solution)/shard_map/ppermute | solution.py:16
  22.7 17.4 %collective-permute-start.5 = (bf16[192,512]{1,0:T(8,128)(2,1)S(1)}, bf16[192,512]{1,0:T(8,128)(2,1)S(1)}, u32[]{:S(2)}, u32[]{:S(2)}) collective-permute-start(bf16[192,512]{1,0:T(8,128)(2,1)S(1)} %bitcast.45), channel_id=1, source_target_pairs={{0,2},{1,3},{2,0},{3,1},{4,6},{5,7},{6,4},{7,5},{8,10},{9,11},{10,... | collective-permute-start | bytes 589832 | tf_op jit(solution)/shard_map/ppermute | solution.py:16
  26.4 13.6 %collective-permute-start.6 = (bf16[192,512]{1,0:T(8,128)(2,1)S(1)}, bf16[192,512]{1,0:T(8,128)(2,1)S(1)}, u32[]{:S(2)}, u32[]{:S(2)}) collective-permute-start(bf16[192,512]{1,0:T(8,128)(2,1)S(1)} %bitcast.44), channel_id=1, source_target_pairs={{0,3},{1,2},{2,1},{3,0},{4,7},{5,6},{6,5},{7,4},{8,11},{9,10},{10,... | collective-permute-start | bytes 589832 | tf_op jit(solution)/shard_map/ppermute | solution.py:16
  41.1 11.1 %collective-permute-start.11 = (bf16[48,512]{1,0:T(8,128)(2,1)S(1)}, bf16[48,512]{1,0:T(8,128)(2,1)}, u32[]{:S(2)}, u32[]{:S(2)}) collective-permute-start(bf16[48,512]{1,0:T(8,128)(2,1)S(1)} %get-tuple-element.116), channel_id=1, source_target_pairs={{0,4},{4,0},{8,12},{12,8},{1,5},{5,1},{9,13},{13,9},{2,6},{6,2},{1... | collective-permute-start | bytes 147464 | tf_op jit(solution)/shard_map/ppermute | solution.py:16
  41.4 16.5 %collective-permute-start.8 = (bf16[48,1024]{1,0:T(8,128)(2,1)S(1)}, bf16[48,1024]{1,0:T(8,128)(2,1)S(1)}, u32[]{:S(2)}, u32[]{:S(2)}) collective-permute-start(bf16[48,1024]{1,0:T(8,128)(2,1)S(1)} %get-tuple-element.112), channel_id=1, source_target_pairs={{0,1},{1,0},{2,3},{3,2},{4,5},{5,4},{6,7},{7,6},{8,9},{9,8},{10,11... | collective-permute-start | bytes 294920 | tf_op jit(solution)/shard_map/ppermute | solution.py:16
  45.8 12.0 %collective-permute-start.9 = (bf16[48,1024]{1,0:T(8,128)(2,1)S(1)}, bf16[48,1024]{1,0:T(8,128)(2,1)}, u32[]{:S(2)}, u32[]{:S(2)}) collective-permute-start(bf16[48,1024]{1,0:T(8,128)(2,1)S(1)} %get-tuple-element.113), channel_id=1, source_target_pairs={{0,2},{1,3},{2,0},{3,1},{4,6},{5,7},{6,4},{7,5},{8,10},{9,11},{10,... | collective-permute-start | bytes 294920 | tf_op jit(solution)/shard_map/ppermute | solution.py:16
  46.8 11.0 %collective-permute-start.10 = (bf16[48,1024]{1,0:T(8,128)(2,1)S(1)}, bf16[48,1024]{1,0:T(8,128)(2,1)}, u32[]{:S(2)}, u32[]{:S(2)}) collective-permute-start(bf16[48,1024]{1,0:T(8,128)(2,1)S(1)} %get-tuple-element.114), channel_id=1, source_target_pairs={{0,3},{1,2},{2,1},{3,0},{4,7},{5,6},{6,5},{7,4},{8,11},{9,10},{10,... | collective-permute-start | bytes 294920 | tf_op jit(solution)/shard_map/ppermute | solution.py:16
  59.8 16.8 %collective-permute-start.14 = (bf16[48,1024]{1,0:T(8,128)(2,1)S(1)}, bf16[48,1024]{1,0:T(8,128)(2,1)S(1)}, u32[]{:S(2)}, u32[]{:S(2)}) collective-permute-start(bf16[48,1024]{1,0:T(8,128)(2,1)S(1)} %get-tuple-element.129), channel_id=1, source_target_pairs={{16,32},{48,64},{80,96},{112,128},{144,160},{176,192},{208,224},{3... | collective-permute-start | bytes 294920 | tf_op jit(solution)/shard_map/ppermute | solution.py:102
  64.0 13.2 %collective-permute-start.18 = (f32[48,512]{1,0:T(8,128)S(1)}, f32[48,512]{1,0:T(8,128)S(1)}, u32[]{:S(2)}, u32[]{:S(2)}) collective-permute-start(f32[48,512]{1,0:T(8,128)S(1)} %get-tuple-element.131), channel_id=1, source_target_pairs={{0,16},{16,0},{32,48},{48,32},{64,80},{80,64},{96,112},{112,96},{1... | collective-permute-start | bytes 294920 | tf_op jit(solution)/shard_map/ppermute | solution.py:96
  68.6 8.0 %collective-permute-start.16 = (bf16[48,512]{1,0:T(8,128)(2,1)S(1)}, bf16[48,512]{1,0:T(8,128)(2,1)S(1)}, u32[]{:S(2)}, u32[]{:S(2)}) collective-permute-start(bf16[48,512]{1,0:T(8,128)(2,1)S(1)} %get-tuple-element.134), channel_id=1, source_target_pairs={{0,2},{1,3},{2,0},{3,1},{4,6},{5,7},{6,4},{7,5},{8,10},{9,11},{10,... | collective-permute-start | bytes 147464 | tf_op jit(solution)/shard_map/ppermute | solution.py:16
  69.9 6.7 %collective-permute-start.17 = (bf16[48,512]{1,0:T(8,128)(2,1)S(1)}, bf16[48,512]{1,0:T(8,128)(2,1)S(1)}, u32[]{:S(2)}, u32[]{:S(2)}) collective-permute-start(bf16[48,512]{1,0:T(8,128)(2,1)S(1)} %get-tuple-element.134), channel_id=1, source_target_pairs={{0,3},{1,2},{2,1},{3,0},{4,7},{5,6},{6,5},{7,4},{8,11},{9,10},{10,... | collective-permute-start | bytes 147464 | tf_op jit(solution)/shard_map/ppermute | solution.py:16
  78.0 7.1 %collective-permute-start.19 = (bf16[48,1024]{1,0:T(8,128)(2,1)S(1)}, bf16[48,1024]{1,0:T(8,128)(2,1)S(1)}, u32[]{:S(2)}, u32[]{:S(2)}) collective-permute-start(bf16[48,1024]{1,0:T(8,128)(2,1)S(1)} %get-tuple-element.144), channel_id=1, source_target_pairs={{0,1},{1,0},{2,3},{3,2},{4,5},{5,4},{6,7},{7,6},{8,9},{9,8},{10,11... | collective-permute-start | bytes 294920 | tf_op jit(solution)/shard_map/ppermute | solution.py:16
  79.3 10.1 %collective-permute-start.20 = (bf16[48,1024]{1,0:T(8,128)(2,1)S(1)}, bf16[48,1024]{1,0:T(8,128)(2,1)S(1)}, u32[]{:S(2)}, u32[]{:S(2)}) collective-permute-start(bf16[48,1024]{1,0:T(8,128)(2,1)S(1)} %get-tuple-element.144), channel_id=1, source_target_pairs={{0,2},{1,3},{2,0},{3,1},{4,6},{5,7},{6,4},{7,5},{8,10},{9,11},{10,... | collective-permute-start | bytes 294920 | tf_op jit(solution)/shard_map/ppermute | solution.py:16
  80.8 8.6 %collective-permute-start.21 = (bf16[48,1024]{1,0:T(8,128)(2,1)S(1)}, bf16[48,1024]{1,0:T(8,128)(2,1)S(1)}, u32[]{:S(2)}, u32[]{:S(2)}) collective-permute-start(bf16[48,1024]{1,0:T(8,128)(2,1)S(1)} %get-tuple-element.144), channel_id=1, source_target_pairs={{0,3},{1,2},{2,1},{3,0},{4,7},{5,6},{6,5},{7,4},{8,11},{9,10},{10,... | collective-permute-start | bytes 294920 | tf_op jit(solution)/shard_map/ppermute | solution.py:16
  82.5 7.4 %collective-permute-start.22 = (bf16[192,512]{1,0:T(8,128)(2,1)S(1)}, bf16[192,512]{1,0:T(8,128)(2,1)S(1)}, u32[]{:S(2)}, u32[]{:S(2)}) collective-permute-start(bf16[192,512]{1,0:T(8,128)(2,1)S(1)} %pad_maximum_fusion.2), channel_id=1, source_target_pairs={{0,4},{4,0},{8,12},{12,8},{1,5},{5,1},{9,13},{13,9},{2,6},{6,2},{1... | collective-permute-start | bytes 589832 | tf_op jit(solution)/shard_map/ppermute | solution.py:16
  82.7 10.7 %collective-permute-start.23 = (bf16[192,512]{1,0:T(8,128)(2,1)S(1)}, bf16[192,512]{1,0:T(8,128)(2,1)S(1)}, u32[]{:S(2)}, u32[]{:S(2)}) collective-permute-start(bf16[192,512]{1,0:T(8,128)(2,1)S(1)} %pad_maximum_fusion.2), channel_id=1, source_target_pairs={{0,8},{4,12},{8,0},{12,4},{1,9},{5,13},{9,1},{13,5},{2,10},{6,14},... | collective-permute-start | bytes 589832 | tf_op jit(solution)/shard_map/ppermute | solution.py:16
  85.2 10.6 %collective-permute-start.24 = (bf16[192,512]{1,0:T(8,128)(2,1)S(1)}, bf16[192,512]{1,0:T(8,128)(2,1)S(1)}, u32[]{:S(2)}, u32[]{:S(2)}) collective-permute-start(bf16[192,512]{1,0:T(8,128)(2,1)S(1)} %pad_maximum_fusion.2), channel_id=1, source_target_pairs={{0,12},{4,8},{8,4},{12,0},{1,13},{5,9},{9,5},{13,1},{2,14},{6,10},... | collective-permute-start | bytes 589832 | tf_op jit(solution)/shard_map/ppermute | solution.py:16
  96.0 12.0 %collective-permute-start.26 = (bf16[192,1024]{1,0:T(8,128)(2,1)S(1)}, bf16[192,1024]{1,0:T(8,128)(2,1)S(1)}, u32[]{:S(2)}, u32[]{:S(2)}) collective-permute-start(bf16[192,1024]{1,0:T(8,128)(2,1)S(1)} %pad_maximum_fusion.1), channel_id=1, source_target_pairs={{0,4},{4,0},{8,12},{12,8},{1,5},{5,1},{9,13},{13,9},{2,6},{6,2},{1... | collective-permute-start | bytes 1179656 | tf_op jit(solution)/shard_map/ppermute | solution.py:16
  96.2 20.4 %collective-permute-start.27 = (bf16[192,1024]{1,0:T(8,128)(2,1)S(1)}, bf16[192,1024]{1,0:T(8,128)(2,1)S(1)}, u32[]{:S(2)}, u32[]{:S(2)}) collective-permute-start(bf16[192,1024]{1,0:T(8,128)(2,1)S(1)} %pad_maximum_fusion.1), channel_id=1, source_target_pairs={{0,8},{4,12},{8,0},{12,4},{1,9},{5,13},{9,1},{13,5},{2,10},{6,14},... | collective-permute-start | bytes 1179656 | tf_op jit(solution)/shard_map/ppermute | solution.py:16
  98.7 20.5 %collective-permute-start.28 = (bf16[192,1024]{1,0:T(8,128)(2,1)S(1)}, bf16[192,1024]{1,0:T(8,128)(2,1)S(1)}, u32[]{:S(2)}, u32[]{:S(2)}) collective-permute-start(bf16[192,1024]{1,0:T(8,128)(2,1)S(1)} %pad_maximum_fusion.1), channel_id=1, source_target_pairs={{0,12},{4,8},{8,4},{12,0},{1,13},{5,9},{9,5},{13,1},{2,14},{6,10},... | collective-permute-start | bytes 1179656 | tf_op jit(solution)/shard_map/ppermute | solution.py:16
  (20 other events, 128.4 us)

commit v4 on v3

v4 whole, which is shorter than its diff:
```python
import jax
import jax.numpy as jnp
from jax import lax
from jax.experimental import pallas as pl
from jax.experimental.pallas import tpu as pltpu
from jax.sharding import Mesh
from jax.sharding import PartitionSpec as P

FEAT = ("feat_0", "feat_1")
SIDE = 4
STEPS = (0, 1, 3, 2)
HIGH = jnp.float32
LOW = jnp.bfloat16


def exchanged(piece, axis, step):
    return lax.ppermute(piece, axis, [(i, i ^ step) for i in range(SIDE)])


def after(value, *others):
    return lax.optimization_barrier((value, *others))[0]


def turned_kernel(blocks, rows):
    x = lax.axis_index(FEAT[0])
    z = lax.axis_index(FEAT[1])
    for i, step in enumerate(STEPS):
        for j, other in enumerate(STEPS):
            rows[i * SIDE + j] = blocks[(x ^ step) * SIDE + (z ^ other)]


def turned_tokens(acts):
    blocks = acts.reshape(SIDE * SIDE, -1, acts.shape[1])
    rows = pl.pallas_call(
        turned_kernel,
        in_specs=[pl.BlockSpec(memory_space=pltpu.VMEM)],
        out_specs=pl.BlockSpec(memory_space=pltpu.VMEM),
        out_shape=jax.ShapeDtypeStruct(blocks.shape, blocks.dtype),
        compiler_params=pltpu.CompilerParams(vmem_limit_bytes=8 * 2**20),
        name="turned_tokens",
    )(blocks)
    return rows.reshape(acts.shape)


def planes_kernel(decoder, main, keep, give):
    first = lax.axis_index("layer") % 2 == 0
    half = keep.shape[1]
    planes = jnp.swapaxes(decoder[...], 0, 1)
    own = planes[0]
    later = planes[1]
    main[...] = jnp.where(first, own, later)
    keep[...] = jnp.where(first, later[:, :half], own[:, half:])
    give[...] = jnp.where(first, later[:, half:], own[:, :half])


def split_planes(decoder):
    features, _, width = decoder.shape
    tile = 256
    half = width // 2
    return pl.pallas_call(
        planes_kernel,
        grid=(features // tile,),
        in_specs=[pl.BlockSpec((tile, 2, width), lambda n: (n, 0, 0))],
        out_specs=[
            pl.BlockSpec((tile, width), lambda n: (n, 0)),
            pl.BlockSpec((tile, half), lambda n: (n, 0)),
            pl.BlockSpec((tile, half), lambda n: (n, 0)),
        ],
        out_shape=[
            jax.ShapeDtypeStruct((features, width), decoder.dtype),
            jax.ShapeDtypeStruct((features, half), decoder.dtype),
            jax.ShapeDtypeStruct((features, half), decoder.dtype),
        ],
        compiler_params=pltpu.CompilerParams(vmem_limit_bytes=16 * 2**20),
        name="split_planes",
    )(decoder)


def row_pieces(array):
    rows = array.shape[0] // SIDE
    return [array[i * rows : (i + 1) * rows] for i in range(SIDE)]


def received(pieces, axis):
    return [exchanged(piece, axis, step) for piece, step in zip(pieces[1:], STEPS[1:])]


def totalled(piece, parts):
    total = piece.astype(HIGH)
    for part in parts:
        total = total + part.astype(HIGH)
    return total


def together(*values):
    return lax.optimization_barrier(values)


def on_chip(value):
    layers = lax.axis_size("layer")
    return lax.ppermute(value, "layer", [(i, i ^ 1) for i in range(layers)])


def across_chips(value):
    layers = lax.axis_size("layer")
    pairs = [(i, i + 1) for i in range(1, layers - 1, 2)]
    return lax.ppermute(value, "layer", pairs + [(j, i) for i, j in pairs])


def dot(a, b):
    return jnp.dot(a, b, preferred_element_type=HIGH)


def contract_width(errs, decoder):
    return lax.dot_general(errs, decoder, (((1,), (1,)), ((), ())), preferred_element_type=HIGH)


def local(acts, targets, enc_weight, enc_bias, dec_weight, dec_bias):
    weight = enc_weight[0]
    bias = enc_bias[0]
    decoder = dec_weight[0]
    tokens, width = acts.shape[1:]
    half = width // 2
    layer = lax.axis_index("layer")
    first = layer % 2 == 0
    ends = layer == lax.axis_size("layer") - 1

    inputs = turned_tokens(acts[0])
    offset = dec_bias[0] - targets[0].astype(HIGH)
    peer_offset = on_chip(offset[:, :half])

    pre = dot(inputs, weight) + bias
    scaled = 4.0 * pre
    small = jnp.exp(-jnp.abs(scaled))
    latent = ((jnp.maximum(scaled, 0.0) + jnp.log1p(small)) * 0.25).astype(LOW)
    latent, pre, decoder, peer_offset = together(latent, pre, decoder, peer_offset)
    main, keep, give = split_planes(decoder)

    given, latent = together(dot(latent, give).astype(LOW), latent)
    given = on_chip(given)
    pieces = row_pieces(dot(latent, main).astype(LOW))
    pieces, latent, pre, inputs = together(pieces, latent, pre, inputs)
    parts = received(pieces, FEAT[0])

    shared = (dot(latent, keep) + given.astype(HIGH)).astype(LOW)
    shared = shared.reshape(SIDE, SIDE, -1, half)
    side = together(*[shared[:, i].reshape(-1, half) for i in range(SIDE)])
    side_parts = received(side, FEAT[1])
    deriv, turned = together(jax.nn.sigmoid(4.0 * pre), inputs.T)

    piece, parts, side, side_parts, deriv, turned = together(
        pieces[0], parts, side[0], side_parts, deriv, turned
    )
    pieces = row_pieces(totalled(piece, parts).astype(LOW))
    side = row_pieces(totalled(side, side_parts).astype(LOW))

    pieces, side = together(pieces, side)
    parts = received(pieces, FEAT[1])
    side_parts = received(side, FEAT[0])

    piece, parts, side, side_parts = together(pieces[0], parts, side[0], side_parts)
    part = totalled(piece, parts) + jnp.where(first, offset, 0.0)
    shared = totalled(side, side_parts) + jnp.where(first, peer_offset, offset[:, half:])

    part, sent, shared, block = together(part, part.astype(LOW), shared, shared.astype(LOW))
    arrived = across_chips(sent)
    tiles = received([block] * SIDE, FEAT[1])

    part, arrived, block, tiles = together(part, arrived, block, tiles)
    part = part + arrived.astype(HIGH)
    rows = jnp.where(ends, 0.0, part).astype(LOW)
    block = jnp.concatenate([block, *tiles], 0)

    rows, block, part = together(rows, block, part)
    parts = received([rows] * SIDE, FEAT[1])
    tiles = received([block] * SIDE, FEAT[0])

    rows, parts, block, tiles = together(rows, parts, block, tiles)
    rows = jnp.concatenate([rows, *parts], 0)
    shared_rows = jnp.concatenate([block, *tiles], 0)

    rows, shared_rows, shared = together(rows, shared_rows, shared)
    near = [exchanged(rows, FEAT[0], 1), exchanged(rows, FEAT[0], 3)]
    other_rows = on_chip(shared_rows)
    other = on_chip(shared)
    grad_latent = contract_width(shared_rows, keep) + contract_width(other_rows, give)
    errors = jnp.where(first, part, jnp.concatenate([other, shared], 1))

    grad_latent, rows, near, errors = together(grad_latent, rows, near, errors)
    middle = rows.shape[0] // 2
    far = [exchanged(near[1][:middle], FEAT[0], 1), exchanged(near[0][middle:], FEAT[0], 3)]
    cut = tokens - rows.shape[0]
    early = jnp.concatenate([rows, *near], 0)
    grads = grad_latent[:cut] + contract_width(early, main)
    grads = after((grads * deriv[:cut]).astype(LOW))
    total = dot(turned[:, :cut], grads)

    total, far, grad_latent = together(total, far, grad_latent)
    grads = grad_latent[cut:] + contract_width(jnp.concatenate(far, 0), main)
    grads = after((grads * deriv[cut:]).astype(LOW))
    total = total + dot(turned[:, cut:], grads)
    enc_grad = (total * tokens ** (-0.5)).astype(LOW)
    return (errors[None], enc_grad[None])


def solution(mesh):
    finer = Mesh(mesh.devices.reshape(mesh.shape["layer"], SIDE, SIDE), ("layer", *FEAT))
    in_specs = (
        P("layer", None, None),
        P("layer", FEAT, None),
        P("layer", None, FEAT),
        P("layer", FEAT),
        P("layer", FEAT, None, None),
        P("layer", None),
    )
    out_specs = (P("layer", FEAT, None), P("layer", None, FEAT))
    return jax.shard_map(local, mesh=finer, in_specs=in_specs, out_specs=out_specs, check_vma=False)
```

time: 127 us -> 116 us (0.913)
  starting transfers between devices: 52.5 us -> 41.8 us
  local copies, waits for them, and re-layouts: 5.99 us -> 3.66 us
  matrix products: 16.7 us -> 18.2 us
    ppermute x24 -> x25, starting transfers between devices: 44.6 us -> 35 us  [exchanged(): return lax.ppermute(piece, axis, [(i, i ^ step) for i in range(SIDE)])]
    ppermute x4, starting transfers between devices: 3.75 us -> 0.78 us  [on_chip(): return lax.ppermute(value, 'layer', [(i, i ^ 1) for i in range(layers)])]
    unnamed x30, local copies, waits for them, and re-layouts: 5.12 us -> 2.74 us
    broadcast_in_dim x0 -> x1, other arithmetic: none -> 2.24 us  [local(): return (errors[None], enc_grad[None])]
    ppermute x1, starting transfers between devices: 4.21 us -> 6 us  [across_chips(): return lax.ppermute(value, 'layer', pairs + [(j, i) for i, j in pairs])]
    dot_general x5 -> x6, matrix products: 12 us -> 13 us  [dot(): return jnp.dot(a, b, preferred_element_type=HIGH)]
    ppermute x24 -> x25, waiting for transfers between devices: 40.3 us -> 39.7 us  [exchanged(): return lax.ppermute(piece, axis, [(i, i ^ step) for i in range(SIDE)])]
    dot_general x3 -> x4, matrix products: 4.72 us -> 5.2 us  [contract_width(): lax.dot_general(errs, decoder, (((1,), (1,)), ((), ())), preferred_elemen...]
  transfers between devices with their start and end apart: 29 -> 30, of which waited for: 15 -> 15; matrix products, arithmetic and copies ran while one was open for 8% -> 16% of each run, Pallas kernels for 0% -> 0%
where the time goes in v4:
time: 116 us; the launch traced here: 115 us
  starting transfers between devices  41.8 us (36%)
  waiting for transfers between devices  39.8 us (34%)
  matrix products  18.2 us (16%)
  other arithmetic  9.35 us (8%)
  local copies, waits for them, and re-layouts  3.66 us (3%)
  Pallas kernels  1.61 us (1%)
    ppermute x25, waiting for transfers between devices, exchanged(): return lax.ppermute(piece, axis, [(i, i ^ step) for i in range(SIDE)])  39.7 us
    ppermute x25, starting transfers between devices, exchanged(): return lax.ppermute(piece, axis, [(i, i ^ step) for i in range(SIDE)])  35 us
    dot_general x6, matrix products, dot(): return jnp.dot(a, b, preferred_element_type=HIGH)  13 us
    ppermute x1, starting transfers between devices, across_chips(): return lax.ppermute(value, 'layer', pairs + [(j, i) for i, j in pairs])  6 us
    dot_general x4, matrix products, contract_width(): lax.dot_general(errs, decoder, (((1,), (1,)), ((), ())), preferred_elemen...  5.2 us
    div x1, other arithmetic, local(): deriv, turned = together(jax.nn.sigmoid(4.0 * pre), inputs.T)  2.9 us
    unnamed x30, local copies, waits for them, and re-layouts  2.74 us
  transfers between devices with their start and end apart: 30, of which 15 were waited for; matrix products, arithmetic and copies ran while one was open for 16% of the time, Pallas kernels for 0%

profile of v4, /device:TPU:8, one launch (start us, length us, event | category | flops | bytes accessed | tf_op | source)
XLA Modules:
  0.0 115.4 jit_solution(1911315200180432762)
XLA Ops:
  4.6 5.3 %multiply_convert_fusion.1 = (bf16[768,1280]{1,0:T(8,128)(2,1)S(1)}, f32[768,1280]{1,0:T(8,128)S(1)}) fusion(f32[1280]{0:T(1024)S(1)} %reduce, bf16[768,1024]{1,0:T(8,128)(2,1)} %bitcast.42, bf16[1,1024,1280]{2,1,0:T(8,128)(2,1)S(1)} %copy-done), kind=kOutput, calls=%fused_computation.3 | convolution fusion | flops 2021130240 | bytes 10097664 | tf_op jit(solution)/shard_map/dot_general | solution.py:111
  13.4 2.2 %convolution_convert_fusion = bf16[768,1024]{1,0:T(8,128)(2,1)S(1)} fusion(bf16[768,1280]{1,0:T(8,128)(2,1)S(1)} %get-tuple-element.93, bf16[1280,1024]{1,0:T(8,128)(2,1)S(1)} %get-tuple-element.87), kind=kOutput, calls=%fused_computation.8 | convolution fusion | flops 2014052352 | bytes 6160384 | tf_op jit(solution)/shard_map/dot_general | solution.py:111
  17.3 2.1 %collective-permute-start.2 = (bf16[192,1024]{1,0:T(8,128)(2,1)S(1)}, bf16[192,1024]{1,0:T(8,128)(2,1)S(1)}, u32[]{:S(2)}, u32[]{:S(2)}) collective-permute-start(bf16[192,1024]{1,0:T(8,128)(2,1)S(1)} %get-tuple-element.91), channel_id=1, source_target_pairs={{0,12},{4,8},{8,4},{12,0},{1,13},{5,9},{9,5},{13,1},{2,14},{6,10},... | collective-permute-start | bytes 1179656 | tf_op jit(solution)/shard_map/ppermute | solution.py:17
  21.3 2.0 %collective-permute-start.5 = (bf16[192,512]{1,0:T(8,128)(2,1)S(1)}, bf16[192,512]{1,0:T(8,128)(2,1)S(1)}, u32[]{:S(2)}, u32[]{:S(2)}) collective-permute-start(bf16[192,512]{1,0:T(8,128)(2,1)S(1)} %bitcast.50), channel_id=1, source_target_pairs={{0,1},{1,0},{2,3},{3,2},{4,5},{5,4},{6,7},{7,6},{8,9},{9,8},{10,11... | collective-permute-start | bytes 589832 | tf_op jit(solution)/shard_map/ppermute | solution.py:17
  23.3 2.8 %collective-permute-start.6 = (bf16[192,512]{1,0:T(8,128)(2,1)S(1)}, bf16[192,512]{1,0:T(8,128)(2,1)S(1)}, u32[]{:S(2)}, u32[]{:S(2)}) collective-permute-start(bf16[192,512]{1,0:T(8,128)(2,1)S(1)} %bitcast.49), channel_id=1, source_target_pairs={{0,3},{1,2},{2,1},{3,0},{4,7},{5,6},{6,5},{7,4},{8,11},{9,10},{10,... | collective-permute-start | bytes 589832 | tf_op jit(solution)/shard_map/ppermute | solution.py:17
  27.7 3.3 %collective-permute-start.7 = (bf16[192,512]{1,0:T(8,128)(2,1)S(1)}, bf16[192,512]{1,0:T(8,128)(2,1)S(1)}, u32[]{:S(2)}, u32[]{:S(2)}) collective-permute-start(bf16[192,512]{1,0:T(8,128)(2,1)S(1)} %bitcast.48), channel_id=1, source_target_pairs={{0,2},{1,3},{2,0},{3,1},{4,6},{5,7},{6,4},{7,5},{8,10},{9,11},{10,... | collective-permute-start | bytes 589832 | tf_op jit(solution)/shard_map/ppermute | solution.py:17
  31.0 2.9 %add_divide_fusion = f32[768,1280]{1,0:T(8,128)} fusion(f32[768,1280]{1,0:T(8,128)S(1)} %get-tuple-element.100), kind=kLoop, calls=%fused_computation.2 | loop fusion | flops 3932160 | bytes 7864320 | tf_op jit(solution)/shard_map/div | solution.py:149
  33.9 4.3 %collective-permute-done.2 = bf16[192,1024]{1,0:T(8,128)(2,1)S(1)} collective-permute-done((bf16[192,1024]{1,0:T(8,128)(2,1)S(1)}, bf16[192,1024]{1,0:T(8,128)(2,1)S(1)}, u32[]{:S(2)}, u32[]{:S(2)}) %collective-permute-start.2) | collective-permute-done | bytes 393248 | tf_op jit(solution)/shard_map/ppermute | solution.py:17
  38.2 5.7 %collective-permute-done.7 = bf16[192,512]{1,0:T(8,128)(2,1)S(1)} collective-permute-done((bf16[192,512]{1,0:T(8,128)(2,1)S(1)}, bf16[192,512]{1,0:T(8,128)(2,1)S(1)}, u32[]{:S(2)}, u32[]{:S(2)}) %collective-permute-start.7) | collective-permute-done | bytes 196640 | tf_op jit(solution)/shard_map/ppermute | solution.py:17
  46.0 2.6 %collective-permute-start.9 = (bf16[48,1024]{1,0:T(8,128)(2,1)S(1)}, bf16[48,1024]{1,0:T(8,128)(2,1)}, u32[]{:S(2)}, u32[]{:S(2)}) collective-permute-start(bf16[48,1024]{1,0:T(8,128)(2,1)S(1)} %get-tuple-element.114), channel_id=1, source_target_pairs={{0,3},{1,2},{2,1},{3,0},{4,7},{5,6},{6,5},{7,4},{8,11},{9,10},{10,... | collective-permute-start | bytes 294920 | tf_op jit(solution)/shard_map/ppermute | solution.py:17
  49.5 2.1 %collective-permute-start.12 = (bf16[48,512]{1,0:T(8,128)(2,1)}, bf16[48,512]{1,0:T(8,128)(2,1)}, u32[]{:S(2)}, u32[]{:S(2)}) collective-permute-start(bf16[48,512]{1,0:T(8,128)(2,1)} %get-tuple-element.118), channel_id=1, source_target_pairs={{0,12},{4,8},{8,4},{12,0},{1,13},{5,9},{9,5},{13,1},{2,14},{6,10},... | collective-permute-start | bytes 147464 | tf_op jit(solution)/shard_map/ppermute | solution.py:17
  52.5 2.8 %collective-permute-done.12 = bf16[48,512]{1,0:T(8,128)(2,1)} collective-permute-done((bf16[48,512]{1,0:T(8,128)(2,1)}, bf16[48,512]{1,0:T(8,128)(2,1)}, u32[]{:S(2)}, u32[]{:S(2)}) %collective-permute-start.12) | collective-permute-done | bytes 49184 | tf_op jit(solution)/shard_map/ppermute | solution.py:17
  55.3 2.2 %collective-permute-done.13 = bf16[48,512]{1,0:T(8,128)(2,1)} collective-permute-done((bf16[48,512]{1,0:T(8,128)(2,1)}, bf16[48,512]{1,0:T(8,128)(2,1)}, u32[]{:S(2)}, u32[]{:S(2)}) %collective-permute-start.13) | collective-permute-done | bytes 49184 | tf_op jit(solution)/shard_map/ppermute | solution.py:17
  59.6 6.0 %collective-permute-start.14 = (bf16[48,1024]{1,0:T(8,128)(2,1)S(1)}, bf16[48,1024]{1,0:T(8,128)(2,1)S(1)}, u32[]{:S(2)}, u32[]{:S(2)}) collective-permute-start(bf16[48,1024]{1,0:T(8,128)(2,1)S(1)} %get-tuple-element.130), channel_id=1, source_target_pairs={{16,32},{48,64},{80,96},{112,128},{144,160},{176,192},{208,224},{3... | collective-permute-start | bytes 294920 | tf_op jit(solution)/shard_map/ppermute | solution.py:107
  67.4 1.8 %collective-permute-start.15 = (bf16[48,512]{1,0:T(8,128)(2,1)S(1)}, bf16[48,512]{1,0:T(8,128)(2,1)S(1)}, u32[]{:S(2)}, u32[]{:S(2)}) collective-permute-start(bf16[48,512]{1,0:T(8,128)(2,1)S(1)} %get-tuple-element.134), channel_id=1, source_target_pairs={{0,1},{1,0},{2,3},{3,2},{4,5},{5,4},{6,7},{7,6},{8,9},{9,8},{10,11... | collective-permute-start | bytes 147464 | tf_op jit(solution)/shard_map/ppermute | solution.py:17
  69.2 6.6 %collective-permute-done.17 = bf16[48,512]{1,0:T(8,128)(2,1)S(1)} collective-permute-done((bf16[48,512]{1,0:T(8,128)(2,1)S(1)}, bf16[48,512]{1,0:T(8,128)(2,1)S(1)}, u32[]{:S(2)}, u32[]{:S(2)}) %collective-permute-start.17) | collective-permute-done | bytes 49184 | tf_op jit(solution)/shard_map/ppermute | solution.py:17
  75.9 2.1 %collective-permute-start.20 = (bf16[48,1024]{1,0:T(8,128)(2,1)S(1)}, bf16[48,1024]{1,0:T(8,128)(2,1)S(1)}, u32[]{:S(2)}, u32[]{:S(2)}) collective-permute-start(bf16[48,1024]{1,0:T(8,128)(2,1)S(1)} %get-tuple-element.140), channel_id=1, source_target_pairs={{0,2},{1,3},{2,0},{3,1},{4,6},{5,7},{6,4},{7,5},{8,10},{9,11},{10,... | collective-permute-start | bytes 294920 | tf_op jit(solution)/shard_map/ppermute | solution.py:17
  78.0 1.8 %collective-permute-start.23 = (bf16[192,512]{1,0:T(8,128)(2,1)S(1)}, bf16[192,512]{1,0:T(8,128)(2,1)S(1)}, u32[]{:S(2)}, u32[]{:S(2)}) collective-permute-start(bf16[192,512]{1,0:T(8,128)(2,1)S(1)} %pad_maximum_fusion.2), channel_id=1, source_target_pairs={{0,8},{4,12},{8,0},{12,4},{1,9},{5,13},{9,1},{13,5},{2,10},{6,14},... | collective-permute-start | bytes 589832 | tf_op jit(solution)/shard_map/ppermute | solution.py:17
  81.5 1.9 %collective-permute-start.19 = (bf16[48,1024]{1,0:T(8,128)(2,1)S(1)}, bf16[48,1024]{1,0:T(8,128)(2,1)S(1)}, u32[]{:S(2)}, u32[]{:S(2)}) collective-permute-start(bf16[48,1024]{1,0:T(8,128)(2,1)S(1)} %get-tuple-element.140), channel_id=1, source_target_pairs={{0,3},{1,2},{2,1},{3,0},{4,7},{5,6},{6,5},{7,4},{8,11},{9,10},{10,... | collective-permute-start | bytes 294920 | tf_op jit(solution)/shard_map/ppermute | solution.py:17
  84.5 3.7 %collective-permute-done.19 = bf16[48,1024]{1,0:T(8,128)(2,1)S(1)} collective-permute-done((bf16[48,1024]{1,0:T(8,128)(2,1)S(1)}, bf16[48,1024]{1,0:T(8,128)(2,1)S(1)}, u32[]{:S(2)}, u32[]{:S(2)}) %collective-permute-start.19) | collective-permute-done | bytes 98336 | tf_op jit(solution)/shard_map/ppermute | solution.py:17
  95.6 7.7 %collective-permute-done.26 = bf16[192,1024]{1,0:T(8,128)(2,1)S(1)} collective-permute-done((bf16[192,1024]{1,0:T(8,128)(2,1)S(1)}, bf16[192,1024]{1,0:T(8,128)(2,1)S(1)}, u32[]{:S(2)}, u32[]{:S(2)}) %collective-permute-start.26) | collective-permute-done | bytes 393248 | tf_op jit(solution)/shard_map/ppermute | solution.py:17
  103.7 1.8 %collective-permute-start.29 = (bf16[96,1024]{1,0:T(8,128)(2,1)S(1)}, bf16[96,1024]{1,0:T(8,128)(2,1)S(1)}, u32[]{:S(2)}, u32[]{:S(2)}) collective-permute-start(bf16[96,1024]{1,0:T(8,128)(2,1)S(1)} %slice.100), channel_id=1, source_target_pairs={{0,12},{4,8},{8,4},{12,0},{1,13},{5,9},{9,5},{13,1},{2,14},{6,10},... | collective-permute-start | bytes 589832 | tf_op jit(solution)/shard_map/ppermute | solution.py:17
  107.3 2.3 %fusion.10 = f32[1024,1280]{1,0:T(8,128)S(1)} fusion(bf16[576,1280]{1,0:T(8,128)(2,1)S(1)} %multiply_convert_fusion.2, bf16[1024,768]{0,1:T(8,128)(2,1)S(1)} %bitcast.43), kind=kOutput, calls=%fused_computation.17 | convolution fusion | flops 1509949440 | bytes 7897088 | tf_op jit(solution)/shard_map/dot_general | solution.py:111
  113.1 2.2 %fusion = bf16[1,1024,1280]{2,1,0:T(8,128)(2,1)} fusion(f32[1024,1280]{1,0:T(8,128)S(1)} %fusion.10, f32[1024,1280]{1,0:T(8,128)S(1)} %fusion.18), kind=kLoop, calls=%fused_computation.6 | loop fusion | flops 3932160 | bytes 13107200 | tf_op jit(solution)/shard_map/broadcast_in_dim | solution.py:203
  (99 shorter events, 36.1 us)
Async XLA Ops:
  1.7 8.1 %collective-permute-start = (f32[48,512]{1,0:T(8,128)S(1)}, f32[48,512]{1,0:T(8,128)S(1)}, u32[]{:S(2)}, u32[]{:S(2)}) collective-permute-start(f32[48,512]{1,0:T(8,128)S(1)} %slice.104), channel_id=1, source_target_pairs={{0,16},{16,0},{32,48},{48,32},{64,80},{80,64},{96,112},{112,96},{1... | collective-permute-start | bytes 294920 | tf_op jit(solution)/shard_map/ppermute | solution.py:101
  12.6 7.4 %collective-permute-start.4 = (bf16[768,512]{1,0:T(8,128)(2,1)S(1)}, bf16[768,512]{1,0:T(8,128)(2,1)S(1)}, u32[]{:S(2)}, u32[]{:S(2)}) collective-permute-start(bf16[768,512]{1,0:T(8,128)(2,1)S(1)} %convolution_convert_fusion.1), channel_id=1, source_target_pairs={{0,16},{16,0},{32,48},{48,32},{64,80},{80,64},{96,112},{112,96},{1... | collective-permute-start | bytes 2359304 | tf_op jit(solution)/shard_map/ppermute | solution.py:101
  15.7 12.0 %collective-permute-start.1 = (bf16[192,1024]{1,0:T(8,128)(2,1)S(1)}, bf16[192,1024]{1,0:T(8,128)(2,1)S(1)}, u32[]{:S(2)}, u32[]{:S(2)}) collective-permute-start(bf16[192,1024]{1,0:T(8,128)(2,1)S(1)} %get-tuple-element.90), channel_id=1, source_target_pairs={{0,4},{4,0},{8,12},{12,8},{1,5},{5,1},{9,13},{13,9},{2,6},{6,2},{1... | collective-permute-start | bytes 1179656 | tf_op jit(solution)/shard_map/ppermute | solution.py:17
  17.3 20.9 %collective-permute-start.2 = (bf16[192,1024]{1,0:T(8,128)(2,1)S(1)}, bf16[192,1024]{1,0:T(8,128)(2,1)S(1)}, u32[]{:S(2)}, u32[]{:S(2)}) collective-permute-start(bf16[192,1024]{1,0:T(8,128)(2,1)S(1)} %get-tuple-element.91), channel_id=1, source_target_pairs={{0,12},{4,8},{8,4},{12,0},{1,13},{5,9},{9,5},{13,1},{2,14},{6,10},... | collective-permute-start | bytes 1179656 | tf_op jit(solution)/shard_map/ppermute | solution.py:17
  19.4 18.8 %collective-permute-start.3 = (bf16[192,1024]{1,0:T(8,128)(2,1)S(1)}, bf16[192,1024]{1,0:T(8,128)(2,1)S(1)}, u32[]{:S(2)}, u32[]{:S(2)}) collective-permute-start(bf16[192,1024]{1,0:T(8,128)(2,1)S(1)} %get-tuple-element.92), channel_id=1, source_target_pairs={{0,8},{4,12},{8,0},{12,4},{1,9},{5,13},{9,1},{13,5},{2,10},{6,14},... | collective-permute-start | bytes 1179656 | tf_op jit(solution)/shard_map/ppermute | solution.py:17
  21.3 16.9 %collective-permute-start.5 = (bf16[192,512]{1,0:T(8,128)(2,1)S(1)}, bf16[192,512]{1,0:T(8,128)(2,1)S(1)}, u32[]{:S(2)}, u32[]{:S(2)}) collective-permute-start(bf16[192,512]{1,0:T(8,128)(2,1)S(1)} %bitcast.50), channel_id=1, source_target_pairs={{0,1},{1,0},{2,3},{3,2},{4,5},{5,4},{6,7},{7,6},{8,9},{9,8},{10,11... | collective-permute-start | bytes 589832 | tf_op jit(solution)/shard_map/ppermute | solution.py:17
  23.3 14.9 %collective-permute-start.6 = (bf16[192,512]{1,0:T(8,128)(2,1)S(1)}, bf16[192,512]{1,0:T(8,128)(2,1)S(1)}, u32[]{:S(2)}, u32[]{:S(2)}) collective-permute-start(bf16[192,512]{1,0:T(8,128)(2,1)S(1)} %bitcast.49), channel_id=1, source_target_pairs={{0,3},{1,2},{2,1},{3,0},{4,7},{5,6},{6,5},{7,4},{8,11},{9,10},{10,... | collective-permute-start | bytes 589832 | tf_op jit(solution)/shard_map/ppermute | solution.py:17
  27.7 16.2 %collective-permute-start.7 = (bf16[192,512]{1,0:T(8,128)(2,1)S(1)}, bf16[192,512]{1,0:T(8,128)(2,1)S(1)}, u32[]{:S(2)}, u32[]{:S(2)}) collective-permute-start(bf16[192,512]{1,0:T(8,128)(2,1)S(1)} %bitcast.48), channel_id=1, source_target_pairs={{0,2},{1,3},{2,0},{3,1},{4,6},{5,7},{6,4},{7,5},{8,10},{9,11},{10,... | collective-permute-start | bytes 589832 | tf_op jit(solution)/shard_map/ppermute | solution.py:17
  45.0 6.7 %collective-permute-start.11 = (bf16[48,512]{1,0:T(8,128)(2,1)S(1)}, bf16[48,512]{1,0:T(8,128)(2,1)}, u32[]{:S(2)}, u32[]{:S(2)}) collective-permute-start(bf16[48,512]{1,0:T(8,128)(2,1)S(1)} %get-tuple-element.117), channel_id=1, source_target_pairs={{0,4},{4,0},{8,12},{12,8},{1,5},{5,1},{9,13},{13,9},{2,6},{6,2},{1... | collective-permute-start | bytes 147464 | tf_op jit(solution)/shard_map/ppermute | solution.py:17
  46.0 11.5 %collective-permute-start.8 = (bf16[48,1024]{1,0:T(8,128)(2,1)S(1)}, bf16[48,1024]{1,0:T(8,128)(2,1)S(1)}, u32[]{:S(2)}, u32[]{:S(2)}) collective-permute-start(bf16[48,1024]{1,0:T(8,128)(2,1)S(1)} %get-tuple-element.113), channel_id=1, source_target_pairs={{0,1},{1,0},{2,3},{3,2},{4,5},{5,4},{6,7},{7,6},{8,9},{9,8},{10,11... | collective-permute-start | bytes 294920 | tf_op jit(solution)/shard_map/ppermute | solution.py:17
  46.0 11.5 %collective-permute-start.9 = (bf16[48,1024]{1,0:T(8,128)(2,1)S(1)}, bf16[48,1024]{1,0:T(8,128)(2,1)}, u32[]{:S(2)}, u32[]{:S(2)}) collective-permute-start(bf16[48,1024]{1,0:T(8,128)(2,1)S(1)} %get-tuple-element.114), channel_id=1, source_target_pairs={{0,3},{1,2},{2,1},{3,0},{4,7},{5,6},{6,5},{7,4},{8,11},{9,10},{10,... | collective-permute-start | bytes 294920 | tf_op jit(solution)/shard_map/ppermute | solution.py:17
  48.7 9.0 %collective-permute-start.10 = (bf16[48,1024]{1,0:T(8,128)(2,1)S(1)}, bf16[48,1024]{1,0:T(8,128)(2,1)}, u32[]{:S(2)}, u32[]{:S(2)}) collective-permute-start(bf16[48,1024]{1,0:T(8,128)(2,1)S(1)} %get-tuple-element.115), channel_id=1, source_target_pairs={{0,2},{1,3},{2,0},{3,1},{4,6},{5,7},{6,4},{7,5},{8,10},{9,11},{10,... | collective-permute-start | bytes 294920 | tf_op jit(solution)/shard_map/ppermute | solution.py:17
  59.6 16.2 %collective-permute-start.14 = (bf16[48,1024]{1,0:T(8,128)(2,1)S(1)}, bf16[48,1024]{1,0:T(8,128)(2,1)S(1)}, u32[]{:S(2)}, u32[]{:S(2)}) collective-permute-start(bf16[48,1024]{1,0:T(8,128)(2,1)S(1)} %get-tuple-element.130), channel_id=1, source_target_pairs={{16,32},{48,64},{80,96},{112,128},{144,160},{176,192},{208,224},{3... | collective-permute-start | bytes 294920 | tf_op jit(solution)/shard_map/ppermute | solution.py:107
  65.6 10.2 %collective-permute-start.17 = (bf16[48,512]{1,0:T(8,128)(2,1)S(1)}, bf16[48,512]{1,0:T(8,128)(2,1)S(1)}, u32[]{:S(2)}, u32[]{:S(2)}) collective-permute-start(bf16[48,512]{1,0:T(8,128)(2,1)S(1)} %get-tuple-element.134), channel_id=1, source_target_pairs={{0,2},{1,3},{2,0},{3,1},{4,6},{5,7},{6,4},{7,5},{8,10},{9,11},{10,... | collective-permute-start | bytes 147464 | tf_op jit(solution)/shard_map/ppermute | solution.py:17
  65.7 10.1 %collective-permute-start.16 = (bf16[48,512]{1,0:T(8,128)(2,1)S(1)}, bf16[48,512]{1,0:T(8,128)(2,1)S(1)}, u32[]{:S(2)}, u32[]{:S(2)}) collective-permute-start(bf16[48,512]{1,0:T(8,128)(2,1)S(1)} %get-tuple-element.134), channel_id=1, source_target_pairs={{0,3},{1,2},{2,1},{3,0},{4,7},{5,6},{6,5},{7,4},{8,11},{9,10},{10,... | collective-permute-start | bytes 147464 | tf_op jit(solution)/shard_map/ppermute | solution.py:17
  67.4 8.4 %collective-permute-start.15 = (bf16[48,512]{1,0:T(8,128)(2,1)S(1)}, bf16[48,512]{1,0:T(8,128)(2,1)S(1)}, u32[]{:S(2)}, u32[]{:S(2)}) collective-permute-start(bf16[48,512]{1,0:T(8,128)(2,1)S(1)} %get-tuple-element.134), channel_id=1, source_target_pairs={{0,1},{1,0},{2,3},{3,2},{4,5},{5,4},{6,7},{7,6},{8,9},{9,8},{10,11... | collective-permute-start | bytes 147464 | tf_op jit(solution)/shard_map/ppermute | solution.py:17
  75.9 8.7 %collective-permute-start.20 = (bf16[48,1024]{1,0:T(8,128)(2,1)S(1)}, bf16[48,1024]{1,0:T(8,128)(2,1)S(1)}, u32[]{:S(2)}, u32[]{:S(2)}) collective-permute-start(bf16[48,1024]{1,0:T(8,128)(2,1)S(1)} %get-tuple-element.140), channel_id=1, source_target_pairs={{0,2},{1,3},{2,0},{3,1},{4,6},{5,7},{6,4},{7,5},{8,10},{9,11},{10,... | collective-permute-start | bytes 294920 | tf_op jit(solution)/shard_map/ppermute | solution.py:17
  78.0 11.3 %collective-permute-start.23 = (bf16[192,512]{1,0:T(8,128)(2,1)S(1)}, bf16[192,512]{1,0:T(8,128)(2,1)S(1)}, u32[]{:S(2)}, u32[]{:S(2)}) collective-permute-start(bf16[192,512]{1,0:T(8,128)(2,1)S(1)} %pad_maximum_fusion.2), channel_id=1, source_target_pairs={{0,8},{4,12},{8,0},{12,4},{1,9},{5,13},{9,1},{13,5},{2,10},{6,14},... | collective-permute-start | bytes 589832 | tf_op jit(solution)/shard_map/ppermute | solution.py:17
  79.8 10.5 %collective-permute-start.22 = (bf16[192,512]{1,0:T(8,128)(2,1)S(1)}, bf16[192,512]{1,0:T(8,128)(2,1)S(1)}, u32[]{:S(2)}, u32[]{:S(2)}) collective-permute-start(bf16[192,512]{1,0:T(8,128)(2,1)S(1)} %pad_maximum_fusion.2), channel_id=1, source_target_pairs={{0,12},{4,8},{8,4},{12,0},{1,13},{5,9},{9,5},{13,1},{2,14},{6,10},... | collective-permute-start | bytes 589832 | tf_op jit(solution)/shard_map/ppermute | solution.py:17
  81.3 9.1 %collective-permute-start.21 = (bf16[192,512]{1,0:T(8,128)(2,1)S(1)}, bf16[192,512]{1,0:T(8,128)(2,1)S(1)}, u32[]{:S(2)}, u32[]{:S(2)}) collective-permute-start(bf16[192,512]{1,0:T(8,128)(2,1)S(1)} %pad_maximum_fusion.2), channel_id=1, source_target_pairs={{0,4},{4,0},{8,12},{12,8},{1,5},{5,1},{9,13},{13,9},{2,6},{6,2},{1... | collective-permute-start | bytes 589832 | tf_op jit(solution)/shard_map/ppermute | solution.py:17
  81.5 6.7 %collective-permute-start.19 = (bf16[48,1024]{1,0:T(8,128)(2,1)S(1)}, bf16[48,1024]{1,0:T(8,128)(2,1)S(1)}, u32[]{:S(2)}, u32[]{:S(2)}) collective-permute-start(bf16[48,1024]{1,0:T(8,128)(2,1)S(1)} %get-tuple-element.140), channel_id=1, source_target_pairs={{0,3},{1,2},{2,1},{3,0},{4,7},{5,6},{6,5},{7,4},{8,11},{9,10},{10,... | collective-permute-start | bytes 294920 | tf_op jit(solution)/shard_map/ppermute | solution.py:17
  90.6 12.7 %collective-permute-start.26 = (bf16[192,1024]{1,0:T(8,128)(2,1)S(1)}, bf16[192,1024]{1,0:T(8,128)(2,1)S(1)}, u32[]{:S(2)}, u32[]{:S(2)}) collective-permute-start(bf16[192,1024]{1,0:T(8,128)(2,1)S(1)} %pad_maximum_fusion.1), channel_id=1, source_target_pairs={{0,12},{4,8},{8,4},{12,0},{1,13},{5,9},{9,5},{13,1},{2,14},{6,10},... | collective-permute-start | bytes 1179656 | tf_op jit(solution)/shard_map/ppermute | solution.py:17
  91.9 11.4 %collective-permute-start.25 = (bf16[192,1024]{1,0:T(8,128)(2,1)S(1)}, bf16[192,1024]{1,0:T(8,128)(2,1)S(1)}, u32[]{:S(2)}, u32[]{:S(2)}) collective-permute-start(bf16[192,1024]{1,0:T(8,128)(2,1)S(1)} %pad_maximum_fusion.1), channel_id=1, source_target_pairs={{0,4},{4,0},{8,12},{12,8},{1,5},{5,1},{9,13},{13,9},{2,6},{6,2},{1... | collective-permute-start | bytes 1179656 | tf_op jit(solution)/shard_map/ppermute | solution.py:17
  103.7 7.5 %collective-permute-start.29 = (bf16[96,1024]{1,0:T(8,128)(2,1)S(1)}, bf16[96,1024]{1,0:T(8,128)(2,1)S(1)}, u32[]{:S(2)}, u32[]{:S(2)}) collective-permute-start(bf16[96,1024]{1,0:T(8,128)(2,1)S(1)} %slice.100), channel_id=1, source_target_pairs={{0,12},{4,8},{8,4},{12,0},{1,13},{5,9},{9,5},{13,1},{2,14},{6,10},... | collective-permute-start | bytes 589832 | tf_op jit(solution)/shard_map/ppermute | solution.py:17
  (21 other events, 137.9 us)

commit v5 on v4

--- a/solution.py
+++ b/solution.py
@@ -126,14 +126,12 @@
     ends = layer == lax.axis_size("layer") - 1
 
     inputs = turned_tokens(acts[0])
-    offset = dec_bias[0] - targets[0].astype(HIGH)
-    peer_offset = on_chip(offset[:, :half])
 
     pre = dot(inputs, weight) + bias
     scaled = 4.0 * pre
     small = jnp.exp(-jnp.abs(scaled))
     latent = ((jnp.maximum(scaled, 0.0) + jnp.log1p(small)) * 0.25).astype(LOW)
-    latent, pre, decoder, peer_offset = together(latent, pre, decoder, peer_offset)
+    latent, pre, decoder = together(latent, pre, decoder)
     main, keep, give = split_planes(decoder)
 
     given, latent = together(dot(latent, give).astype(LOW), latent)
@@ -145,20 +143,23 @@
     shared = (dot(latent, keep) + given.astype(HIGH)).astype(LOW)
     shared = shared.reshape(SIDE, SIDE, -1, half)
     side = together(*[shared[:, i].reshape(-1, half) for i in range(SIDE)])
-    side_parts = received(side, FEAT[1])
-    deriv, turned = together(jax.nn.sigmoid(4.0 * pre), inputs.T)
-
-    piece, parts, side, side_parts, deriv, turned = together(
-        pieces[0], parts, side[0], side_parts, deriv, turned
+    side, pre, inputs = together(side, pre, inputs)
+    side_parts = received(side, FEAT[1])[::-1]
+    deriv, turned, lift = together(jax.nn.sigmoid(4.0 * pre), inputs.T, dec_bias[0])
+    offset = lift - targets[0].astype(HIGH)
+    peer_offset = on_chip(offset[:, :half])
+
+    side_parts, parts, piece, side, deriv, turned, peer_offset = together(
+        side_parts, parts, pieces[0], side[0], deriv, turned, peer_offset
     )
     pieces = row_pieces(totalled(piece, parts).astype(LOW))
     side = row_pieces(totalled(side, side_parts).astype(LOW))
 
     pieces, side = together(pieces, side)
-    parts = received(pieces, FEAT[1])
+    parts = received(pieces, FEAT[1])[::-1]
     side_parts = received(side, FEAT[0])
 
-    piece, parts, side, side_parts = together(pieces[0], parts, side[0], side_parts)
+    parts, piece, side, side_parts = together(parts, pieces[0], side[0], side_parts)
     part = totalled(piece, parts) + jnp.where(first, offset, 0.0)
     shared = totalled(side, side_parts) + jnp.where(first, peer_offset, offset[:, half:])
 

time: 116 us -> 112 us (0.966)
  starting transfers between devices: 41.8 us -> 39.9 us
  waiting for transfers between devices: 39.8 us -> 38.6 us
    ppermute x25, waiting for transfers between devices: 39.7 us -> 37.3 us  [exchanged(): return lax.ppermute(piece, axis, [(i, i ^ step) for i in range(SIDE)])]
    ppermute x4, waiting for transfers between devices: 0.09 us -> 1.3 us  [on_chip(): return lax.ppermute(value, 'layer', [(i, i ^ 1) for i in range(layers)])]
    unnamed x30 -> x32, local copies, waits for them, and re-layouts: 2.74 us -> 3.38 us
  transfers between devices with their start and end apart: 30 -> 30, of which waited for: 15 -> 16; matrix products, arithmetic and copies ran while one was open for 16% -> 12% of each run, Pallas kernels for 0% -> 0%
where the time goes in v5:
time: 112 us
  starting transfers between devices  39.9 us (36%)
  waiting for transfers between devices  38.6 us (34%)
  matrix products  18.2 us (16%)
  other arithmetic  8.36 us (7%)
  local copies, waits for them, and re-layouts  4.27 us (4%)
  Pallas kernels  1.61 us (1%)
    ppermute x25, waiting for transfers between devices, exchanged(): return lax.ppermute(piece, axis, [(i, i ^ step) for i in range(SIDE)])  37.3 us
    ppermute x25, starting transfers between devices, exchanged(): return lax.ppermute(piece, axis, [(i, i ^ step) for i in range(SIDE)])  34.8 us
    dot_general x6, matrix products, dot(): return jnp.dot(a, b, preferred_element_type=HIGH)  13 us
    dot_general x4, matrix products, contract_width(): lax.dot_general(errs, decoder, (((1,), (1,)), ((), ())), preferred_elemen...  5.21 us
    ppermute x1, starting transfers between devices, across_chips(): return lax.ppermute(value, 'layer', pairs + [(j, i) for i, j in pairs])  4.84 us
    unnamed x32, local copies, waits for them, and re-layouts  3.38 us
    div x1, other arithmetic, local(): jax.nn.sigmoid(4.0 * pre)  2.9 us
    broadcast_in_dim x1, other arithmetic, local(): return (errors[None], enc_grad[None])  2.3 us
  transfers between devices with their start and end apart: 30, of which 16 were waited for; matrix products, arithmetic and copies ran while one was open for 12% of the time, Pallas kernels for 0%

profile of v5, /device:TPU:8, one launch (start us, length us, event | category | flops | bytes accessed | tf_op | source)
XLA Modules:
  0.0 111.9 jit_solution(9220415395919567498)
XLA Ops:
  3.5 5.3 %multiply_convert_fusion.1 = (bf16[768,1280]{1,0:T(8,128)(2,1)S(1)}, f32[768,1280]{1,0:T(8,128)S(1)}) fusion(f32[1280]{0:T(1024)S(1)} %reduce, bf16[768,1024]{1,0:T(8,128)(2,1)} %bitcast.42, bf16[1,1024,1280]{2,1,0:T(8,128)(2,1)S(1)} %copy-done), kind=kOutput, calls=%fused_computation.3 | convolution fusion | flops 2021130240 | bytes 10097664 | tf_op jit(solution)/shard_map/dot_general | solution.py:111
  12.3 2.2 %convolution_convert_fusion = bf16[768,1024]{1,0:T(8,128)(2,1)S(1)} fusion(bf16[768,1280]{1,0:T(8,128)(2,1)S(1)} %get-tuple-element.96, bf16[1280,1024]{1,0:T(8,128)(2,1)S(1)} %get-tuple-element.94), kind=kOutput, calls=%fused_computation.8 | convolution fusion | flops 2014052352 | bytes 6160384 | tf_op jit(solution)/shard_map/dot_general | solution.py:111
  16.2 2.1 %collective-permute-start.5 = (bf16[192,1024]{1,0:T(8,128)(2,1)S(1)}, bf16[192,1024]{1,0:T(8,128)(2,1)S(1)}, u32[]{:S(2)}, u32[]{:S(2)}) collective-permute-start(bf16[192,1024]{1,0:T(8,128)(2,1)S(1)} %get-tuple-element.109), channel_id=1, source_target_pairs={{0,12},{4,8},{8,4},{12,0},{1,13},{5,9},{9,5},{13,1},{2,14},{6,10},... | collective-permute-start | bytes 1179656 | tf_op jit(solution)/shard_map/ppermute | solution.py:17
  20.2 3.4 %collective-permute-start.1 = (bf16[192,512]{1,0:T(8,128)(2,1)S(1)}, bf16[192,512]{1,0:T(8,128)(2,1)S(1)}, u32[]{:S(2)}, u32[]{:S(2)}) collective-permute-start(bf16[192,512]{1,0:T(8,128)(2,1)S(1)} %bitcast.50), channel_id=1, source_target_pairs={{0,2},{1,3},{2,0},{3,1},{4,6},{5,7},{6,4},{7,5},{8,10},{9,11},{10,... | collective-permute-start | bytes 589832 | tf_op jit(solution)/shard_map/ppermute | solution.py:17
  25.0 2.9 %add_divide_fusion = f32[768,1280]{1,0:T(8,128)} fusion(f32[768,1280]{1,0:T(8,128)S(1)} %get-tuple-element.113), kind=kLoop, calls=%fused_computation.2 | loop fusion | flops 3932160 | bytes 7864320 | tf_op jit(solution)/shard_map/div | solution.py:148
  28.7 7.8 %collective-permute-done.5 = bf16[192,1024]{1,0:T(8,128)(2,1)S(1)} collective-permute-done((bf16[192,1024]{1,0:T(8,128)(2,1)S(1)}, bf16[192,1024]{1,0:T(8,128)(2,1)S(1)}, u32[]{:S(2)}, u32[]{:S(2)}) %collective-permute-start.5) | collective-permute-done | bytes 393248 | tf_op jit(solution)/shard_map/ppermute | solution.py:17
  37.9 2.2 %collective-permute-done.3 = bf16[192,512]{1,0:T(8,128)(2,1)S(1)} collective-permute-done((bf16[192,512]{1,0:T(8,128)(2,1)S(1)}, bf16[192,512]{1,0:T(8,128)(2,1)S(1)}, u32[]{:S(2)}, u32[]{:S(2)}) %collective-permute-start.3) | collective-permute-done | bytes 196640 | tf_op jit(solution)/shard_map/ppermute | solution.py:17
  42.0 3.4 %collective-permute-start.8 = (bf16[48,1024]{1,0:T(8,128)(2,1)S(1)}, bf16[48,1024]{1,0:T(8,128)(2,1)S(1)}, u32[]{:S(2)}, u32[]{:S(2)}) collective-permute-start(bf16[48,1024]{1,0:T(8,128)(2,1)S(1)} %get-tuple-element.126), channel_id=1, source_target_pairs={{0,2},{1,3},{2,0},{3,1},{4,6},{5,7},{6,4},{7,5},{8,10},{9,11},{10,... | collective-permute-start | bytes 294920 | tf_op jit(solution)/shard_map/ppermute | solution.py:17
  46.2 2.1 %collective-permute-start.12 = (bf16[48,512]{1,0:T(8,128)(2,1)}, bf16[48,512]{1,0:T(8,128)(2,1)}, u32[]{:S(2)}, u32[]{:S(2)}) collective-permute-start(bf16[48,512]{1,0:T(8,128)(2,1)} %get-tuple-element.132), channel_id=1, source_target_pairs={{0,12},{4,8},{8,4},{12,0},{1,13},{5,9},{9,5},{13,1},{2,14},{6,10},... | collective-permute-start | bytes 147464 | tf_op jit(solution)/shard_map/ppermute | solution.py:17
  49.2 3.2 %collective-permute-done.12 = bf16[48,512]{1,0:T(8,128)(2,1)} collective-permute-done((bf16[48,512]{1,0:T(8,128)(2,1)}, bf16[48,512]{1,0:T(8,128)(2,1)}, u32[]{:S(2)}, u32[]{:S(2)}) %collective-permute-start.12) | collective-permute-done | bytes 49184 | tf_op jit(solution)/shard_map/ppermute | solution.py:17
  52.4 1.9 %collective-permute-done.13 = bf16[48,512]{1,0:T(8,128)(2,1)} collective-permute-done((bf16[48,512]{1,0:T(8,128)(2,1)}, bf16[48,512]{1,0:T(8,128)(2,1)}, u32[]{:S(2)}, u32[]{:S(2)}) %collective-permute-start.13) | collective-permute-done | bytes 49184 | tf_op jit(solution)/shard_map/ppermute | solution.py:17
  56.2 4.8 %collective-permute-start.14 = (bf16[48,1024]{1,0:T(8,128)(2,1)S(1)}, bf16[48,1024]{1,0:T(8,128)(2,1)S(1)}, u32[]{:S(2)}, u32[]{:S(2)}) collective-permute-start(bf16[48,1024]{1,0:T(8,128)(2,1)S(1)} %get-tuple-element.144), channel_id=1, source_target_pairs={{16,32},{48,64},{80,96},{112,128},{144,160},{176,192},{208,224},{3... | collective-permute-start | bytes 294920 | tf_op jit(solution)/shard_map/ppermute | solution.py:107
  61.0 2.2 %collective-permute-start.17 = (bf16[48,512]{1,0:T(8,128)(2,1)S(1)}, bf16[48,512]{1,0:T(8,128)(2,1)S(1)}, u32[]{:S(2)}, u32[]{:S(2)}) collective-permute-start(bf16[48,512]{1,0:T(8,128)(2,1)S(1)} %get-tuple-element.148), channel_id=1, source_target_pairs={{0,2},{1,3},{2,0},{3,1},{4,6},{5,7},{6,4},{7,5},{8,10},{9,11},{10,... | collective-permute-start | bytes 147464 | tf_op jit(solution)/shard_map/ppermute | solution.py:17
  63.2 1.9 %collective-permute-start.16 = (bf16[48,512]{1,0:T(8,128)(2,1)S(1)}, bf16[48,512]{1,0:T(8,128)(2,1)S(1)}, u32[]{:S(2)}, u32[]{:S(2)}) collective-permute-start(bf16[48,512]{1,0:T(8,128)(2,1)S(1)} %get-tuple-element.148), channel_id=1, source_target_pairs={{0,3},{1,2},{2,1},{3,0},{4,7},{5,6},{6,5},{7,4},{8,11},{9,10},{10,... | collective-permute-start | bytes 147464 | tf_op jit(solution)/shard_map/ppermute | solution.py:17
  66.2 2.9 %collective-permute-done.16 = bf16[48,512]{1,0:T(8,128)(2,1)S(1)} collective-permute-done((bf16[48,512]{1,0:T(8,128)(2,1)S(1)}, bf16[48,512]{1,0:T(8,128)(2,1)S(1)}, u32[]{:S(2)}, u32[]{:S(2)}) %collective-permute-start.16) | collective-permute-done | bytes 49184 | tf_op jit(solution)/shard_map/ppermute | solution.py:17
  70.4 4.2 %collective-permute-start.20 = (bf16[48,1024]{1,0:T(8,128)(2,1)S(1)}, bf16[48,1024]{1,0:T(8,128)(2,1)S(1)}, u32[]{:S(2)}, u32[]{:S(2)}) collective-permute-start(bf16[48,1024]{1,0:T(8,128)(2,1)S(1)} %get-tuple-element.154), channel_id=1, source_target_pairs={{0,2},{1,3},{2,0},{3,1},{4,6},{5,7},{6,4},{7,5},{8,10},{9,11},{10,... | collective-permute-start | bytes 294920 | tf_op jit(solution)/shard_map/ppermute | solution.py:17
  75.8 2.0 %collective-permute-start.22 = (bf16[192,512]{1,0:T(8,128)(2,1)S(1)}, bf16[192,512]{1,0:T(8,128)(2,1)S(1)}, u32[]{:S(2)}, u32[]{:S(2)}) collective-permute-start(bf16[192,512]{1,0:T(8,128)(2,1)S(1)} %pad_maximum_fusion.2), channel_id=1, source_target_pairs={{0,12},{4,8},{8,4},{12,0},{1,13},{5,9},{9,5},{13,1},{2,14},{6,10},... | collective-permute-start | bytes 589832 | tf_op jit(solution)/shard_map/ppermute | solution.py:17
  78.0 1.8 %collective-permute-start.19 = (bf16[48,1024]{1,0:T(8,128)(2,1)S(1)}, bf16[48,1024]{1,0:T(8,128)(2,1)S(1)}, u32[]{:S(2)}, u32[]{:S(2)}) collective-permute-start(bf16[48,1024]{1,0:T(8,128)(2,1)S(1)} %get-tuple-element.154), channel_id=1, source_target_pairs={{0,3},{1,2},{2,1},{3,0},{4,7},{5,6},{6,5},{7,4},{8,11},{9,10},{10,... | collective-permute-start | bytes 294920 | tf_op jit(solution)/shard_map/ppermute | solution.py:17
  80.0 5.3 %collective-permute-done.19 = bf16[48,1024]{1,0:T(8,128)(2,1)S(1)} collective-permute-done((bf16[48,1024]{1,0:T(8,128)(2,1)S(1)}, bf16[48,1024]{1,0:T(8,128)(2,1)S(1)}, u32[]{:S(2)}, u32[]{:S(2)}) %collective-permute-start.19) | collective-permute-done | bytes 98336 | tf_op jit(solution)/shard_map/ppermute | solution.py:17
  91.6 8.2 %collective-permute-done.26 = bf16[192,1024]{1,0:T(8,128)(2,1)S(1)} collective-permute-done((bf16[192,1024]{1,0:T(8,128)(2,1)S(1)}, bf16[192,1024]{1,0:T(8,128)(2,1)S(1)}, u32[]{:S(2)}, u32[]{:S(2)}) %collective-permute-start.26) | collective-permute-done | bytes 393248 | tf_op jit(solution)/shard_map/ppermute | solution.py:17
  100.0 2.0 %collective-permute-start.29 = (bf16[96,1024]{1,0:T(8,128)(2,1)S(1)}, bf16[96,1024]{1,0:T(8,128)(2,1)S(1)}, u32[]{:S(2)}, u32[]{:S(2)}) collective-permute-start(bf16[96,1024]{1,0:T(8,128)(2,1)S(1)} %slice.100), channel_id=1, source_target_pairs={{0,12},{4,8},{8,4},{12,0},{1,13},{5,9},{9,5},{13,1},{2,14},{6,10},... | collective-permute-start | bytes 589832 | tf_op jit(solution)/shard_map/ppermute | solution.py:17
  102.0 1.8 %multiply_convert_fusion.2 = bf16[576,1280]{1,0:T(8,128)(2,1)S(1)} fusion(f32[768,1280]{1,0:T(8,128)S(1)} %copy-done.10, f32[768,1280]{1,0:T(8,128)S(1)} %convolution_add_fusion, bf16[1280,1024]{1,0:T(8,128)(2,1)S(1)} %copy-done.4, bf16[192,1024]{1,0:T(8,128)(2,1)S(1)} %collective-permute-done.26, bf16[192,1024]{1,0:T(8,128)(2,1)S(1)} %collective-permute-done.25, ...), kind=kOutput, calls=%fused_computation.5 | convolution fusion | flops 1515700224 | bytes 11173888 | tf_op jit(solution)/shard_map/dot_general | solution.py:115
  103.8 2.3 %fusion.10 = f32[1024,1280]{1,0:T(8,128)S(1)} fusion(bf16[576,1280]{1,0:T(8,128)(2,1)S(1)} %multiply_convert_fusion.2, bf16[1024,768]{0,1:T(8,128)(2,1)S(1)} %bitcast.43), kind=kOutput, calls=%fused_computation.17 | convolution fusion | flops 1509949440 | bytes 7897088 | tf_op jit(solution)/shard_map/dot_general | solution.py:111
  109.6 2.3 %fusion = bf16[1,1024,1280]{2,1,0:T(8,128)(2,1)} fusion(f32[1024,1280]{1,0:T(8,128)S(1)} %fusion.10, f32[1024,1280]{1,0:T(8,128)S(1)} %fusion.18), kind=kLoop, calls=%fused_computation.6 | loop fusion | flops 3932160 | bytes 13107200 | tf_op jit(solution)/shard_map/broadcast_in_dim | solution.py:204
  (101 shorter events, 32.9 us)
Async XLA Ops:
  11.6 7.4 %collective-permute-start = (bf16[768,512]{1,0:T(8,128)(2,1)S(1)}, bf16[768,512]{1,0:T(8,128)(2,1)S(1)}, u32[]{:S(2)}, u32[]{:S(2)}) collective-permute-start(bf16[768,512]{1,0:T(8,128)(2,1)S(1)} %convolution_convert_fusion.1), channel_id=1, source_target_pairs={{0,16},{16,0},{32,48},{48,32},{64,80},{80,64},{96,112},{112,96},{1... | collective-permute-start | bytes 2359304 | tf_op jit(solution)/shard_map/ppermute | solution.py:101
  14.6 13.3 %collective-permute-start.4 = (bf16[192,1024]{1,0:T(8,128)(2,1)S(1)}, bf16[192,1024]{1,0:T(8,128)(2,1)S(1)}, u32[]{:S(2)}, u32[]{:S(2)}) collective-permute-start(bf16[192,1024]{1,0:T(8,128)(2,1)S(1)} %get-tuple-element.108), channel_id=1, source_target_pairs={{0,4},{4,0},{8,12},{12,8},{1,5},{5,1},{9,13},{13,9},{2,6},{6,2},{1... | collective-permute-start | bytes 1179656 | tf_op jit(solution)/shard_map/ppermute | solution.py:17
  16.2 20.3 %collective-permute-start.5 = (bf16[192,1024]{1,0:T(8,128)(2,1)S(1)}, bf16[192,1024]{1,0:T(8,128)(2,1)S(1)}, u32[]{:S(2)}, u32[]{:S(2)}) collective-permute-start(bf16[192,1024]{1,0:T(8,128)(2,1)S(1)} %get-tuple-element.109), channel_id=1, source_target_pairs={{0,12},{4,8},{8,4},{12,0},{1,13},{5,9},{9,5},{13,1},{2,14},{6,10},... | collective-permute-start | bytes 1179656 | tf_op jit(solution)/shard_map/ppermute | solution.py:17
  18.3 18.2 %collective-permute-start.6 = (bf16[192,1024]{1,0:T(8,128)(2,1)S(1)}, bf16[192,1024]{1,0:T(8,128)(2,1)S(1)}, u32[]{:S(2)}, u32[]{:S(2)}) collective-permute-start(bf16[192,1024]{1,0:T(8,128)(2,1)S(1)} %get-tuple-element.110), channel_id=1, source_target_pairs={{0,8},{4,12},{8,0},{12,4},{1,9},{5,13},{9,1},{13,5},{2,10},{6,14},... | collective-permute-start | bytes 1179656 | tf_op jit(solution)/shard_map/ppermute | solution.py:17
  20.2 17.6 %collective-permute-start.1 = (bf16[192,512]{1,0:T(8,128)(2,1)S(1)}, bf16[192,512]{1,0:T(8,128)(2,1)S(1)}, u32[]{:S(2)}, u32[]{:S(2)}) collective-permute-start(bf16[192,512]{1,0:T(8,128)(2,1)S(1)} %bitcast.50), channel_id=1, source_target_pairs={{0,2},{1,3},{2,0},{3,1},{4,6},{5,7},{6,4},{7,5},{8,10},{9,11},{10,... | collective-permute-start | bytes 589832 | tf_op jit(solution)/shard_map/ppermute | solution.py:17
  23.6 14.3 %collective-permute-start.2 = (bf16[192,512]{1,0:T(8,128)(2,1)S(1)}, bf16[192,512]{1,0:T(8,128)(2,1)S(1)}, u32[]{:S(2)}, u32[]{:S(2)}) collective-permute-start(bf16[192,512]{1,0:T(8,128)(2,1)S(1)} %bitcast.49), channel_id=1, source_target_pairs={{0,3},{1,2},{2,1},{3,0},{4,7},{5,6},{6,5},{7,4},{8,11},{9,10},{10,... | collective-permute-start | bytes 589832 | tf_op jit(solution)/shard_map/ppermute | solution.py:17
  27.9 12.1 %collective-permute-start.3 = (bf16[192,512]{1,0:T(8,128)(2,1)S(1)}, bf16[192,512]{1,0:T(8,128)(2,1)S(1)}, u32[]{:S(2)}, u32[]{:S(2)}) collective-permute-start(bf16[192,512]{1,0:T(8,128)(2,1)S(1)} %bitcast.48), channel_id=1, source_target_pairs={{0,1},{1,0},{2,3},{3,2},{4,5},{5,4},{6,7},{7,6},{8,9},{9,8},{10,11... | collective-permute-start | bytes 589832 | tf_op jit(solution)/shard_map/ppermute | solution.py:17
  41.1 7.2 %collective-permute-start.11 = (bf16[48,512]{1,0:T(8,128)(2,1)S(1)}, bf16[48,512]{1,0:T(8,128)(2,1)}, u32[]{:S(2)}, u32[]{:S(2)}) collective-permute-start(bf16[48,512]{1,0:T(8,128)(2,1)S(1)} %get-tuple-element.131), channel_id=1, source_target_pairs={{0,4},{4,0},{8,12},{12,8},{1,5},{5,1},{9,13},{13,9},{2,6},{6,2},{1... | collective-permute-start | bytes 147464 | tf_op jit(solution)/shard_map/ppermute | solution.py:17
  42.0 12.2 %collective-permute-start.8 = (bf16[48,1024]{1,0:T(8,128)(2,1)S(1)}, bf16[48,1024]{1,0:T(8,128)(2,1)S(1)}, u32[]{:S(2)}, u32[]{:S(2)}) collective-permute-start(bf16[48,1024]{1,0:T(8,128)(2,1)S(1)} %get-tuple-element.126), channel_id=1, source_target_pairs={{0,2},{1,3},{2,0},{3,1},{4,6},{5,7},{6,4},{7,5},{8,10},{9,11},{10,... | collective-permute-start | bytes 294920 | tf_op jit(solution)/shard_map/ppermute | solution.py:17
  45.5 8.8 %collective-permute-start.9 = (bf16[48,1024]{1,0:T(8,128)(2,1)S(1)}, bf16[48,1024]{1,0:T(8,128)(2,1)}, u32[]{:S(2)}, u32[]{:S(2)}) collective-permute-start(bf16[48,1024]{1,0:T(8,128)(2,1)S(1)} %get-tuple-element.127), channel_id=1, source_target_pairs={{0,3},{1,2},{2,1},{3,0},{4,7},{5,6},{6,5},{7,4},{8,11},{9,10},{10,... | collective-permute-start | bytes 294920 | tf_op jit(solution)/shard_map/ppermute | solution.py:17
  45.9 8.3 %collective-permute-start.10 = (bf16[48,1024]{1,0:T(8,128)(2,1)S(1)}, bf16[48,1024]{1,0:T(8,128)(2,1)}, u32[]{:S(2)}, u32[]{:S(2)}) collective-permute-start(bf16[48,1024]{1,0:T(8,128)(2,1)S(1)} %get-tuple-element.128), channel_id=1, source_target_pairs={{0,1},{1,0},{2,3},{3,2},{4,5},{5,4},{6,7},{7,6},{8,9},{9,8},{10,11... | collective-permute-start | bytes 294920 | tf_op jit(solution)/shard_map/ppermute | solution.py:17
  46.2 6.1 %collective-permute-start.12 = (bf16[48,512]{1,0:T(8,128)(2,1)}, bf16[48,512]{1,0:T(8,128)(2,1)}, u32[]{:S(2)}, u32[]{:S(2)}) collective-permute-start(bf16[48,512]{1,0:T(8,128)(2,1)} %get-tuple-element.132), channel_id=1, source_target_pairs={{0,12},{4,8},{8,4},{12,0},{1,13},{5,9},{9,5},{13,1},{2,14},{6,10},... | collective-permute-start | bytes 147464 | tf_op jit(solution)/shard_map/ppermute | solution.py:17
  48.3 5.9 %collective-permute-start.13 = (bf16[48,512]{1,0:T(8,128)(2,1)}, bf16[48,512]{1,0:T(8,128)(2,1)}, u32[]{:S(2)}, u32[]{:S(2)}) collective-permute-start(bf16[48,512]{1,0:T(8,128)(2,1)} %get-tuple-element.133), channel_id=1, source_target_pairs={{0,8},{4,12},{8,0},{12,4},{1,9},{5,13},{9,1},{13,5},{2,10},{6,14},... | collective-permute-start | bytes 147464 | tf_op jit(solution)/shard_map/ppermute | solution.py:17
  56.2 14.1 %collective-permute-start.14 = (bf16[48,1024]{1,0:T(8,128)(2,1)S(1)}, bf16[48,1024]{1,0:T(8,128)(2,1)S(1)}, u32[]{:S(2)}, u32[]{:S(2)}) collective-permute-start(bf16[48,1024]{1,0:T(8,128)(2,1)S(1)} %get-tuple-element.144), channel_id=1, source_target_pairs={{16,32},{48,64},{80,96},{112,128},{144,160},{176,192},{208,224},{3... | collective-permute-start | bytes 294920 | tf_op jit(solution)/shard_map/ppermute | solution.py:107
  70.4 9.6 %collective-permute-start.20 = (bf16[48,1024]{1,0:T(8,128)(2,1)S(1)}, bf16[48,1024]{1,0:T(8,128)(2,1)S(1)}, u32[]{:S(2)}, u32[]{:S(2)}) collective-permute-start(bf16[48,1024]{1,0:T(8,128)(2,1)S(1)} %get-tuple-element.154), channel_id=1, source_target_pairs={{0,2},{1,3},{2,0},{3,1},{4,6},{5,7},{6,4},{7,5},{8,10},{9,11},{10,... | collective-permute-start | bytes 294920 | tf_op jit(solution)/shard_map/ppermute | solution.py:17
  74.5 11.6 %collective-permute-start.23 = (bf16[192,512]{1,0:T(8,128)(2,1)S(1)}, bf16[192,512]{1,0:T(8,128)(2,1)S(1)}, u32[]{:S(2)}, u32[]{:S(2)}) collective-permute-start(bf16[192,512]{1,0:T(8,128)(2,1)S(1)} %pad_maximum_fusion.2), channel_id=1, source_target_pairs={{0,8},{4,12},{8,0},{12,4},{1,9},{5,13},{9,1},{13,5},{2,10},{6,14},... | collective-permute-start | bytes 589832 | tf_op jit(solution)/shard_map/ppermute | solution.py:17
  75.8 11.1 %collective-permute-start.22 = (bf16[192,512]{1,0:T(8,128)(2,1)S(1)}, bf16[192,512]{1,0:T(8,128)(2,1)S(1)}, u32[]{:S(2)}, u32[]{:S(2)}) collective-permute-start(bf16[192,512]{1,0:T(8,128)(2,1)S(1)} %pad_maximum_fusion.2), channel_id=1, source_target_pairs={{0,12},{4,8},{8,4},{12,0},{1,13},{5,9},{9,5},{13,1},{2,14},{6,10},... | collective-permute-start | bytes 589832 | tf_op jit(solution)/shard_map/ppermute | solution.py:17
  77.8 9.1 %collective-permute-start.21 = (bf16[192,512]{1,0:T(8,128)(2,1)S(1)}, bf16[192,512]{1,0:T(8,128)(2,1)S(1)}, u32[]{:S(2)}, u32[]{:S(2)}) collective-permute-start(bf16[192,512]{1,0:T(8,128)(2,1)S(1)} %pad_maximum_fusion.2), channel_id=1, source_target_pairs={{0,4},{4,0},{8,12},{12,8},{1,5},{5,1},{9,13},{13,9},{2,6},{6,2},{1... | collective-permute-start | bytes 589832 | tf_op jit(solution)/shard_map/ppermute | solution.py:17
  78.0 7.3 %collective-permute-start.19 = (bf16[48,1024]{1,0:T(8,128)(2,1)S(1)}, bf16[48,1024]{1,0:T(8,128)(2,1)S(1)}, u32[]{:S(2)}, u32[]{:S(2)}) collective-permute-start(bf16[48,1024]{1,0:T(8,128)(2,1)S(1)} %get-tuple-element.154), channel_id=1, source_target_pairs={{0,3},{1,2},{2,1},{3,0},{4,7},{5,6},{6,5},{7,4},{8,11},{9,10},{10,... | collective-permute-start | bytes 294920 | tf_op jit(solution)/shard_map/ppermute | solution.py:17
  80.0 6.2 %collective-permute-start.18 = (bf16[48,1024]{1,0:T(8,128)(2,1)S(1)}, bf16[48,1024]{1,0:T(8,128)(2,1)S(1)}, u32[]{:S(2)}, u32[]{:S(2)}) collective-permute-start(bf16[48,1024]{1,0:T(8,128)(2,1)S(1)} %get-tuple-element.154), channel_id=1, source_target_pairs={{0,1},{1,0},{2,3},{3,2},{4,5},{5,4},{6,7},{7,6},{8,9},{9,8},{10,11... | collective-permute-start | bytes 294920 | tf_op jit(solution)/shard_map/ppermute | solution.py:17
  87.1 12.7 %collective-permute-start.26 = (bf16[192,1024]{1,0:T(8,128)(2,1)S(1)}, bf16[192,1024]{1,0:T(8,128)(2,1)S(1)}, u32[]{:S(2)}, u32[]{:S(2)}) collective-permute-start(bf16[192,1024]{1,0:T(8,128)(2,1)S(1)} %pad_maximum_fusion.1), channel_id=1, source_target_pairs={{0,12},{4,8},{8,4},{12,0},{1,13},{5,9},{9,5},{13,1},{2,14},{6,10},... | collective-permute-start | bytes 1179656 | tf_op jit(solution)/shard_map/ppermute | solution.py:17
  88.3 11.5 %collective-permute-start.25 = (bf16[192,1024]{1,0:T(8,128)(2,1)S(1)}, bf16[192,1024]{1,0:T(8,128)(2,1)S(1)}, u32[]{:S(2)}, u32[]{:S(2)}) collective-permute-start(bf16[192,1024]{1,0:T(8,128)(2,1)S(1)} %pad_maximum_fusion.1), channel_id=1, source_target_pairs={{0,4},{4,0},{8,12},{12,8},{1,5},{5,1},{9,13},{13,9},{2,6},{6,2},{1... | collective-permute-start | bytes 1179656 | tf_op jit(solution)/shard_map/ppermute | solution.py:17
  99.9 6.5 %collective-permute-start.28 = (bf16[96,1024]{1,0:T(8,128)(2,1)S(1)}, bf16[96,1024]{1,0:T(8,128)(2,1)S(1)}, u32[]{:S(2)}, u32[]{:S(2)}) collective-permute-start(bf16[96,1024]{1,0:T(8,128)(2,1)S(1)} %slice.99), channel_id=1, source_target_pairs={{0,4},{4,0},{8,12},{12,8},{1,5},{5,1},{9,13},{13,9},{2,6},{6,2},{1... | collective-permute-start | bytes 589832 | tf_op jit(solution)/shard_map/ppermute | solution.py:17
  100.0 7.7 %collective-permute-start.29 = (bf16[96,1024]{1,0:T(8,128)(2,1)S(1)}, bf16[96,1024]{1,0:T(8,128)(2,1)S(1)}, u32[]{:S(2)}, u32[]{:S(2)}) collective-permute-start(bf16[96,1024]{1,0:T(8,128)(2,1)S(1)} %slice.100), channel_id=1, source_target_pairs={{0,12},{4,8},{8,4},{12,0},{1,13},{5,9},{9,5},{13,1},{2,14},{6,10},... | collective-permute-start | bytes 589832 | tf_op jit(solution)/shard_map/ppermute | solution.py:17
  (22 other events, 122.3 us)

commit v6 on v5

--- a/solution.py
+++ b/solution.py
@@ -145,7 +145,10 @@
     side = together(*[shared[:, i].reshape(-1, half) for i in range(SIDE)])
     side, pre, inputs = together(side, pre, inputs)
     side_parts = received(side, FEAT[1])[::-1]
-    deriv, turned, lift = together(jax.nn.sigmoid(4.0 * pre), inputs.T, dec_bias[0])
+    cut = tokens - tokens // SIDE
+    deriv, *turned, lift = together(
+        jax.nn.sigmoid(4.0 * pre), inputs[:cut].T, inputs[cut:].T, dec_bias[0]
+    )
     offset = lift - targets[0].astype(HIGH)
     peer_offset = on_chip(offset[:, :half])
 
@@ -190,16 +193,15 @@
     grad_latent, rows, near, errors = together(grad_latent, rows, near, errors)
     middle = rows.shape[0] // 2
     far = [exchanged(near[1][:middle], FEAT[0], 1), exchanged(near[0][middle:], FEAT[0], 3)]
-    cut = tokens - rows.shape[0]
     early = jnp.concatenate([rows, *near], 0)
     grads = grad_latent[:cut] + contract_width(early, main)
     grads = after((grads * deriv[:cut]).astype(LOW))
-    total = dot(turned[:, :cut], grads)
+    total = dot(turned[0], grads)
 
     total, far, grad_latent = together(total, far, grad_latent)
     grads = grad_latent[cut:] + contract_width(jnp.concatenate(far, 0), main)
     grads = after((grads * deriv[cut:]).astype(LOW))
-    total = total + dot(turned[:, cut:], grads)
+    total = total + dot(turned[1], grads)
     enc_grad = (total * tokens ** (-0.5)).astype(LOW)
     return (errors[None], enc_grad[None])
 

time: 112 us -> 117 us (1.045)
  other arithmetic: 8.36 us -> 10.6 us
  local copies, waits for them, and re-layouts: 4.27 us -> 6.29 us
    transpose x0 -> x2, local copies, waits for them, and re-layouts: none -> 1.19 us  [the longest x1 1.16 us: local(): inputs[:cut]]
    unnamed x32 -> x36, local copies, waits for them, and re-layouts: 3.38 us -> 3.56 us
  transfers between devices with their start and end apart: 30 -> 30, of which waited for: 16 -> 16; matrix products, arithmetic and copies ran while one was open for 12% -> 13% of each run, Pallas kernels for 0% -> 0%
where the time goes in v6:
time: 117 us; the launch traced here: 116 us
  starting transfers between devices  39.7 us (34%)
  waiting for transfers between devices  38.9 us (33%)
  matrix products  18.2 us (16%)
  other arithmetic  10.6 us (9%)
  local copies, waits for them, and re-layouts  6.29 us (5%)
  Pallas kernels  1.61 us (1%)
    ppermute x25, waiting for transfers between devices, exchanged(): return lax.ppermute(piece, axis, [(i, i ^ step) for i in range(SIDE)])  37.5 us
    ppermute x25, starting transfers between devices, exchanged(): return lax.ppermute(piece, axis, [(i, i ^ step) for i in range(SIDE)])  34.5 us
    dot_general x6, matrix products, dot(): return jnp.dot(a, b, preferred_element_type=HIGH)  13 us
    dot_general x4, matrix products, contract_width(): lax.dot_general(errs, decoder, (((1,), (1,)), ((), ())), preferred_elemen...  5.21 us
    ppermute x1, starting transfers between devices, across_chips(): return lax.ppermute(value, 'layer', pairs + [(j, i) for i, j in pairs])  4.94 us
    unnamed x36, local copies, waits for them, and re-layouts  3.56 us
    div x1, other arithmetic, local(): jax.nn.sigmoid(4.0 * pre)  2.91 us
  transfers between devices with their start and end apart: 30, of which 16 were waited for; matrix products, arithmetic and copies ran while one was open for 13% of the time, Pallas kernels for 0%

profile of v6, /device:TPU:8, one launch (start us, length us, event | category | flops | bytes accessed | tf_op | source)
XLA Modules:
  0.0 116.3 jit_solution(6841223922716453192)
XLA Ops:
  3.6 5.3 %multiply_convert_fusion.1 = (bf16[768,1280]{1,0:T(8,128)(2,1)S(1)}, f32[768,1280]{1,0:T(8,128)S(1)}) fusion(f32[1280]{0:T(1024)S(1)} %reduce, bf16[768,1024]{1,0:T(8,128)(2,1)} %bitcast.44, bf16[1,1024,1280]{2,1,0:T(8,128)(2,1)S(1)} %copy-done), kind=kOutput, calls=%fused_computation.3 | convolution fusion | flops 2021130240 | bytes 10097664 | tf_op jit(solution)/shard_map/dot_general | solution.py:111
  12.3 2.2 %convolution_convert_fusion = bf16[768,1024]{1,0:T(8,128)(2,1)S(1)} fusion(bf16[768,1280]{1,0:T(8,128)(2,1)S(1)} %get-tuple-element.98, bf16[1280,1024]{1,0:T(8,128)(2,1)S(1)} %get-tuple-element.96), kind=kOutput, calls=%fused_computation.8 | convolution fusion | flops 2014052352 | bytes 6160384 | tf_op jit(solution)/shard_map/dot_general | solution.py:111
  16.2 2.1 %collective-permute-start.5 = (bf16[192,1024]{1,0:T(8,128)(2,1)S(1)}, bf16[192,1024]{1,0:T(8,128)(2,1)S(1)}, u32[]{:S(2)}, u32[]{:S(2)}) collective-permute-start(bf16[192,1024]{1,0:T(8,128)(2,1)S(1)} %get-tuple-element.111), channel_id=1, source_target_pairs={{0,12},{4,8},{8,4},{12,0},{1,13},{5,9},{9,5},{13,1},{2,14},{6,10},... | collective-permute-start | bytes 1179656 | tf_op jit(solution)/shard_map/ppermute | solution.py:17
  21.6 3.3 %collective-permute-start.1 = (bf16[192,512]{1,0:T(8,128)(2,1)S(1)}, bf16[192,512]{1,0:T(8,128)(2,1)S(1)}, u32[]{:S(2)}, u32[]{:S(2)}) collective-permute-start(bf16[192,512]{1,0:T(8,128)(2,1)S(1)} %bitcast.55), channel_id=1, source_target_pairs={{0,2},{1,3},{2,0},{3,1},{4,6},{5,7},{6,4},{7,5},{8,10},{9,11},{10,... | collective-permute-start | bytes 589832 | tf_op jit(solution)/shard_map/ppermute | solution.py:17
  26.2 2.9 %add_divide_fusion = f32[768,1280]{1,0:T(8,128)} fusion(f32[768,1280]{1,0:T(8,128)S(1)} %get-tuple-element.115), kind=kLoop, calls=%fused_computation.2 | loop fusion | flops 3932160 | bytes 7864320 | tf_op jit(solution)/shard_map/div | solution.py:150
  29.7 6.8 %collective-permute-done.5 = bf16[192,1024]{1,0:T(8,128)(2,1)S(1)} collective-permute-done((bf16[192,1024]{1,0:T(8,128)(2,1)S(1)}, bf16[192,1024]{1,0:T(8,128)(2,1)S(1)}, u32[]{:S(2)}, u32[]{:S(2)}) %collective-permute-start.5) | collective-permute-done | bytes 393248 | tf_op jit(solution)/shard_map/ppermute | solution.py:17
  39.1 2.1 %collective-permute-done.3 = bf16[192,512]{1,0:T(8,128)(2,1)S(1)} collective-permute-done((bf16[192,512]{1,0:T(8,128)(2,1)S(1)}, bf16[192,512]{1,0:T(8,128)(2,1)S(1)}, u32[]{:S(2)}, u32[]{:S(2)}) %collective-permute-start.3) | collective-permute-done | bytes 196640 | tf_op jit(solution)/shard_map/ppermute | solution.py:17
  43.9 3.5 %collective-permute-start.8 = (bf16[48,1024]{1,0:T(8,128)(2,1)}, bf16[48,1024]{1,0:T(8,128)(2,1)}, u32[]{:S(2)}, u32[]{:S(2)}) collective-permute-start(bf16[48,1024]{1,0:T(8,128)(2,1)} %get-tuple-element.129), channel_id=1, source_target_pairs={{0,2},{1,3},{2,0},{3,1},{4,6},{5,7},{6,4},{7,5},{8,10},{9,11},{10,... | collective-permute-start | bytes 294920 | tf_op jit(solution)/shard_map/ppermute | solution.py:17
  47.9 2.1 %collective-permute-start.12 = (bf16[48,512]{1,0:T(8,128)(2,1)}, bf16[48,512]{1,0:T(8,128)(2,1)}, u32[]{:S(2)}, u32[]{:S(2)}) collective-permute-start(bf16[48,512]{1,0:T(8,128)(2,1)} %get-tuple-element.135), channel_id=1, source_target_pairs={{0,12},{4,8},{8,4},{12,0},{1,13},{5,9},{9,5},{13,1},{2,14},{6,10},... | collective-permute-start | bytes 147464 | tf_op jit(solution)/shard_map/ppermute | solution.py:17
  51.0 3.1 %collective-permute-done.12 = bf16[48,512]{1,0:T(8,128)(2,1)} collective-permute-done((bf16[48,512]{1,0:T(8,128)(2,1)}, bf16[48,512]{1,0:T(8,128)(2,1)}, u32[]{:S(2)}, u32[]{:S(2)}) %collective-permute-start.12) | collective-permute-done | bytes 49184 | tf_op jit(solution)/shard_map/ppermute | solution.py:17
  54.1 1.9 %collective-permute-done.13 = bf16[48,512]{1,0:T(8,128)(2,1)} collective-permute-done((bf16[48,512]{1,0:T(8,128)(2,1)}, bf16[48,512]{1,0:T(8,128)(2,1)}, u32[]{:S(2)}, u32[]{:S(2)}) %collective-permute-start.13) | collective-permute-done | bytes 49184 | tf_op jit(solution)/shard_map/ppermute | solution.py:17
  56.0 1.8 %fusion.21 = (bf16[48,1024]{1,0:T(8,128)(2,1)}, f32[48,1024]{1,0:T(8,128)S(1)}) fusion(bf16[1,48,1024]{2,1,0:T(8,128)(2,1)} %param.7, f32[1024]{0:T(1024)} %bitcast.57, pred[]{:T(512)S(6)} %eq.9, bf16[48,1024]{1,0:T(8,128)(2,1)} %collective-permute-done.10, bf16[48,1024]{1,0:T(8,128)(2,1)} %collective-permute-done.9, ...), kind=kLoop, calls=%fused_computation.39 | loop fusion | flops 589824 | bytes 790529 | tf_op jit(solution)/shard_map/convert_element_type | solution.py:169
  59.3 4.9 %collective-permute-start.14 = (bf16[48,1024]{1,0:T(8,128)(2,1)}, bf16[48,1024]{1,0:T(8,128)(2,1)S(1)}, u32[]{:S(2)}, u32[]{:S(2)}) collective-permute-start(bf16[48,1024]{1,0:T(8,128)(2,1)} %get-tuple-element.147), channel_id=1, source_target_pairs={{16,32},{48,64},{80,96},{112,128},{144,160},{176,192},{208,224},{3... | collective-permute-start | bytes 294920 | tf_op jit(solution)/shard_map/ppermute | solution.py:107
  64.3 2.2 %collective-permute-start.17 = (bf16[48,512]{1,0:T(8,128)(2,1)}, bf16[48,512]{1,0:T(8,128)(2,1)S(1)}, u32[]{:S(2)}, u32[]{:S(2)}) collective-permute-start(bf16[48,512]{1,0:T(8,128)(2,1)} %get-tuple-element.151), channel_id=1, source_target_pairs={{0,2},{1,3},{2,0},{3,1},{4,6},{5,7},{6,4},{7,5},{8,10},{9,11},{10,... | collective-permute-start | bytes 147464 | tf_op jit(solution)/shard_map/ppermute | solution.py:17
  66.4 1.9 %collective-permute-start.16 = (bf16[48,512]{1,0:T(8,128)(2,1)}, bf16[48,512]{1,0:T(8,128)(2,1)S(1)}, u32[]{:S(2)}, u32[]{:S(2)}) collective-permute-start(bf16[48,512]{1,0:T(8,128)(2,1)} %get-tuple-element.151), channel_id=1, source_target_pairs={{0,3},{1,2},{2,1},{3,0},{4,7},{5,6},{6,5},{7,4},{8,11},{9,10},{10,... | collective-permute-start | bytes 147464 | tf_op jit(solution)/shard_map/ppermute | solution.py:17
  69.6 2.9 %collective-permute-done.16 = bf16[48,512]{1,0:T(8,128)(2,1)S(1)} collective-permute-done((bf16[48,512]{1,0:T(8,128)(2,1)}, bf16[48,512]{1,0:T(8,128)(2,1)S(1)}, u32[]{:S(2)}, u32[]{:S(2)}) %collective-permute-start.16) | collective-permute-done | bytes 49184 | tf_op jit(solution)/shard_map/ppermute | solution.py:17
  74.6 4.2 %collective-permute-start.20 = (bf16[48,1024]{1,0:T(8,128)(2,1)S(1)}, bf16[48,1024]{1,0:T(8,128)(2,1)S(1)}, u32[]{:S(2)}, u32[]{:S(2)}) collective-permute-start(bf16[48,1024]{1,0:T(8,128)(2,1)S(1)} %get-tuple-element.157), channel_id=1, source_target_pairs={{0,2},{1,3},{2,0},{3,1},{4,6},{5,7},{6,4},{7,5},{8,10},{9,11},{10,... | collective-permute-start | bytes 294920 | tf_op jit(solution)/shard_map/ppermute | solution.py:17
  80.2 1.9 %collective-permute-start.22 = (bf16[192,512]{1,0:T(8,128)(2,1)S(1)}, bf16[192,512]{1,0:T(8,128)(2,1)S(1)}, u32[]{:S(2)}, u32[]{:S(2)}) collective-permute-start(bf16[192,512]{1,0:T(8,128)(2,1)S(1)} %pad_maximum_fusion.2), channel_id=1, source_target_pairs={{0,12},{4,8},{8,4},{12,0},{1,13},{5,9},{9,5},{13,1},{2,14},{6,10},... | collective-permute-start | bytes 589832 | tf_op jit(solution)/shard_map/ppermute | solution.py:17
  82.3 1.8 %collective-permute-start.19 = (bf16[48,1024]{1,0:T(8,128)(2,1)S(1)}, bf16[48,1024]{1,0:T(8,128)(2,1)S(1)}, u32[]{:S(2)}, u32[]{:S(2)}) collective-permute-start(bf16[48,1024]{1,0:T(8,128)(2,1)S(1)} %get-tuple-element.157), channel_id=1, source_target_pairs={{0,3},{1,2},{2,1},{3,0},{4,7},{5,6},{6,5},{7,4},{8,11},{9,10},{10,... | collective-permute-start | bytes 294920 | tf_op jit(solution)/shard_map/ppermute | solution.py:17
  84.3 5.2 %collective-permute-done.19 = bf16[48,1024]{1,0:T(8,128)(2,1)S(1)} collective-permute-done((bf16[48,1024]{1,0:T(8,128)(2,1)S(1)}, bf16[48,1024]{1,0:T(8,128)(2,1)S(1)}, u32[]{:S(2)}, u32[]{:S(2)}) %collective-permute-start.19) | collective-permute-done | bytes 98336 | tf_op jit(solution)/shard_map/ppermute | solution.py:17
  96.0 8.2 %collective-permute-done.26 = bf16[192,1024]{1,0:T(8,128)(2,1)S(1)} collective-permute-done((bf16[192,1024]{1,0:T(8,128)(2,1)S(1)}, bf16[192,1024]{1,0:T(8,128)(2,1)S(1)}, u32[]{:S(2)}, u32[]{:S(2)}) %collective-permute-start.26) | collective-permute-done | bytes 393248 | tf_op jit(solution)/shard_map/ppermute | solution.py:17
  104.3 2.0 %collective-permute-start.29 = (bf16[96,1024]{1,0:T(8,128)(2,1)S(1)}, bf16[96,1024]{1,0:T(8,128)(2,1)S(1)}, u32[]{:S(2)}, u32[]{:S(2)}) collective-permute-start(bf16[96,1024]{1,0:T(8,128)(2,1)S(1)} %slice.101), channel_id=1, source_target_pairs={{0,12},{4,8},{8,4},{12,0},{1,13},{5,9},{9,5},{13,1},{2,14},{6,10},... | collective-permute-start | bytes 589832 | tf_op jit(solution)/shard_map/ppermute | solution.py:17
  108.1 2.3 %fusion.27 = f32[1024,1280]{1,0:T(8,128)S(1)} fusion(bf16[1024,576]{0,1:T(8,128)(2,1)S(1)} %copy-done.11, bf16[576,1280]{1,0:T(8,128)(2,1)S(1)} %multiply_convert_fusion.2), kind=kOutput, calls=%fused_computation.45 | convolution fusion | flops 1509949440 | bytes 7897088 | tf_op jit(solution)/shard_map/dot_general | solution.py:111
  114.0 2.3 %fusion = bf16[1,1024,1280]{2,1,0:T(8,128)(2,1)} fusion(f32[1024,1280]{1,0:T(8,128)S(1)} %fusion.27, f32[1024,1280]{1,0:T(8,128)S(1)} %fusion.28), kind=kLoop, calls=%fused_computation.6 | loop fusion | flops 3932160 | bytes 13107200 | tf_op jit(solution)/shard_map/broadcast_in_dim | solution.py:206
  (107 shorter events, 38.5 us)
Async XLA Ops:
  11.6 7.4 %collective-permute-start = (bf16[768,512]{1,0:T(8,128)(2,1)S(1)}, bf16[768,512]{1,0:T(8,128)(2,1)S(1)}, u32[]{:S(2)}, u32[]{:S(2)}) collective-permute-start(bf16[768,512]{1,0:T(8,128)(2,1)S(1)} %convolution_convert_fusion.1), channel_id=1, source_target_pairs={{0,16},{16,0},{32,48},{48,32},{64,80},{80,64},{96,112},{112,96},{1... | collective-permute-start | bytes 2359304 | tf_op jit(solution)/shard_map/ppermute | solution.py:101
  14.7 14.5 %collective-permute-start.4 = (bf16[192,1024]{1,0:T(8,128)(2,1)S(1)}, bf16[192,1024]{1,0:T(8,128)(2,1)S(1)}, u32[]{:S(2)}, u32[]{:S(2)}) collective-permute-start(bf16[192,1024]{1,0:T(8,128)(2,1)S(1)} %get-tuple-element.110), channel_id=1, source_target_pairs={{0,4},{4,0},{8,12},{12,8},{1,5},{5,1},{9,13},{13,9},{2,6},{6,2},{1... | collective-permute-start | bytes 1179656 | tf_op jit(solution)/shard_map/ppermute | solution.py:17
  16.2 20.3 %collective-permute-start.5 = (bf16[192,1024]{1,0:T(8,128)(2,1)S(1)}, bf16[192,1024]{1,0:T(8,128)(2,1)S(1)}, u32[]{:S(2)}, u32[]{:S(2)}) collective-permute-start(bf16[192,1024]{1,0:T(8,128)(2,1)S(1)} %get-tuple-element.111), channel_id=1, source_target_pairs={{0,12},{4,8},{8,4},{12,0},{1,13},{5,9},{9,5},{13,1},{2,14},{6,10},... | collective-permute-start | bytes 1179656 | tf_op jit(solution)/shard_map/ppermute | solution.py:17
  18.3 18.2 %collective-permute-start.6 = (bf16[192,1024]{1,0:T(8,128)(2,1)S(1)}, bf16[192,1024]{1,0:T(8,128)(2,1)S(1)}, u32[]{:S(2)}, u32[]{:S(2)}) collective-permute-start(bf16[192,1024]{1,0:T(8,128)(2,1)S(1)} %get-tuple-element.112), channel_id=1, source_target_pairs={{0,8},{4,12},{8,0},{12,4},{1,9},{5,13},{9,1},{13,5},{2,10},{6,14},... | collective-permute-start | bytes 1179656 | tf_op jit(solution)/shard_map/ppermute | solution.py:17
  21.6 17.5 %collective-permute-start.1 = (bf16[192,512]{1,0:T(8,128)(2,1)S(1)}, bf16[192,512]{1,0:T(8,128)(2,1)S(1)}, u32[]{:S(2)}, u32[]{:S(2)}) collective-permute-start(bf16[192,512]{1,0:T(8,128)(2,1)S(1)} %bitcast.55), channel_id=1, source_target_pairs={{0,2},{1,3},{2,0},{3,1},{4,6},{5,7},{6,4},{7,5},{8,10},{9,11},{10,... | collective-permute-start | bytes 589832 | tf_op jit(solution)/shard_map/ppermute | solution.py:17
  24.9 14.3 %collective-permute-start.2 = (bf16[192,512]{1,0:T(8,128)(2,1)S(1)}, bf16[192,512]{1,0:T(8,128)(2,1)S(1)}, u32[]{:S(2)}, u32[]{:S(2)}) collective-permute-start(bf16[192,512]{1,0:T(8,128)(2,1)S(1)} %bitcast.54), channel_id=1, source_target_pairs={{0,3},{1,2},{2,1},{3,0},{4,7},{5,6},{6,5},{7,4},{8,11},{9,10},{10,... | collective-permute-start | bytes 589832 | tf_op jit(solution)/shard_map/ppermute | solution.py:17
  29.1 12.1 %collective-permute-start.3 = (bf16[192,512]{1,0:T(8,128)(2,1)S(1)}, bf16[192,512]{1,0:T(8,128)(2,1)S(1)}, u32[]{:S(2)}, u32[]{:S(2)}) collective-permute-start(bf16[192,512]{1,0:T(8,128)(2,1)S(1)} %bitcast.53), channel_id=1, source_target_pairs={{0,1},{1,0},{2,3},{3,2},{4,5},{5,4},{6,7},{7,6},{8,9},{9,8},{10,11... | collective-permute-start | bytes 589832 | tf_op jit(solution)/shard_map/ppermute | solution.py:17
  43.0 7.1 %collective-permute-start.11 = (bf16[48,512]{1,0:T(8,128)(2,1)S(1)}, bf16[48,512]{1,0:T(8,128)(2,1)}, u32[]{:S(2)}, u32[]{:S(2)}) collective-permute-start(bf16[48,512]{1,0:T(8,128)(2,1)S(1)} %get-tuple-element.134), channel_id=1, source_target_pairs={{0,4},{4,0},{8,12},{12,8},{1,5},{5,1},{9,13},{13,9},{2,6},{6,2},{1... | collective-permute-start | bytes 147464 | tf_op jit(solution)/shard_map/ppermute | solution.py:17
  43.9 12.1 %collective-permute-start.8 = (bf16[48,1024]{1,0:T(8,128)(2,1)}, bf16[48,1024]{1,0:T(8,128)(2,1)}, u32[]{:S(2)}, u32[]{:S(2)}) collective-permute-start(bf16[48,1024]{1,0:T(8,128)(2,1)} %get-tuple-element.129), channel_id=1, source_target_pairs={{0,2},{1,3},{2,0},{3,1},{4,6},{5,7},{6,4},{7,5},{8,10},{9,11},{10,... | collective-permute-start | bytes 294920 | tf_op jit(solution)/shard_map/ppermute | solution.py:17
  47.4 8.6 %collective-permute-start.9 = (bf16[48,1024]{1,0:T(8,128)(2,1)S(1)}, bf16[48,1024]{1,0:T(8,128)(2,1)}, u32[]{:S(2)}, u32[]{:S(2)}) collective-permute-start(bf16[48,1024]{1,0:T(8,128)(2,1)S(1)} %get-tuple-element.130), channel_id=1, source_target_pairs={{0,3},{1,2},{2,1},{3,0},{4,7},{5,6},{6,5},{7,4},{8,11},{9,10},{10,... | collective-permute-start | bytes 294920 | tf_op jit(solution)/shard_map/ppermute | solution.py:17
  47.8 8.1 %collective-permute-start.10 = (bf16[48,1024]{1,0:T(8,128)(2,1)S(1)}, bf16[48,1024]{1,0:T(8,128)(2,1)}, u32[]{:S(2)}, u32[]{:S(2)}) collective-permute-start(bf16[48,1024]{1,0:T(8,128)(2,1)S(1)} %get-tuple-element.131), channel_id=1, source_target_pairs={{0,1},{1,0},{2,3},{3,2},{4,5},{5,4},{6,7},{7,6},{8,9},{9,8},{10,11... | collective-permute-start | bytes 294920 | tf_op jit(solution)/shard_map/ppermute | solution.py:17
  47.9 6.1 %collective-permute-start.12 = (bf16[48,512]{1,0:T(8,128)(2,1)}, bf16[48,512]{1,0:T(8,128)(2,1)}, u32[]{:S(2)}, u32[]{:S(2)}) collective-permute-start(bf16[48,512]{1,0:T(8,128)(2,1)} %get-tuple-element.135), channel_id=1, source_target_pairs={{0,12},{4,8},{8,4},{12,0},{1,13},{5,9},{9,5},{13,1},{2,14},{6,10},... | collective-permute-start | bytes 147464 | tf_op jit(solution)/shard_map/ppermute | solution.py:17
  59.3 14.5 %collective-permute-start.14 = (bf16[48,1024]{1,0:T(8,128)(2,1)}, bf16[48,1024]{1,0:T(8,128)(2,1)S(1)}, u32[]{:S(2)}, u32[]{:S(2)}) collective-permute-start(bf16[48,1024]{1,0:T(8,128)(2,1)} %get-tuple-element.147), channel_id=1, source_target_pairs={{16,32},{48,64},{80,96},{112,128},{144,160},{176,192},{208,224},{3... | collective-permute-start | bytes 294920 | tf_op jit(solution)/shard_map/ppermute | solution.py:107
  66.4 6.1 %collective-permute-start.16 = (bf16[48,512]{1,0:T(8,128)(2,1)}, bf16[48,512]{1,0:T(8,128)(2,1)S(1)}, u32[]{:S(2)}, u32[]{:S(2)}) collective-permute-start(bf16[48,512]{1,0:T(8,128)(2,1)} %get-tuple-element.151), channel_id=1, source_target_pairs={{0,3},{1,2},{2,1},{3,0},{4,7},{5,6},{6,5},{7,4},{8,11},{9,10},{10,... | collective-permute-start | bytes 147464 | tf_op jit(solution)/shard_map/ppermute | solution.py:17
  74.6 9.7 %collective-permute-start.20 = (bf16[48,1024]{1,0:T(8,128)(2,1)S(1)}, bf16[48,1024]{1,0:T(8,128)(2,1)S(1)}, u32[]{:S(2)}, u32[]{:S(2)}) collective-permute-start(bf16[48,1024]{1,0:T(8,128)(2,1)S(1)} %get-tuple-element.157), channel_id=1, source_target_pairs={{0,2},{1,3},{2,0},{3,1},{4,6},{5,7},{6,4},{7,5},{8,10},{9,11},{10,... | collective-permute-start | bytes 294920 | tf_op jit(solution)/shard_map/ppermute | solution.py:17
  78.8 11.6 %collective-permute-start.23 = (bf16[192,512]{1,0:T(8,128)(2,1)S(1)}, bf16[192,512]{1,0:T(8,128)(2,1)S(1)}, u32[]{:S(2)}, u32[]{:S(2)}) collective-permute-start(bf16[192,512]{1,0:T(8,128)(2,1)S(1)} %pad_maximum_fusion.2), channel_id=1, source_target_pairs={{0,8},{4,12},{8,0},{12,4},{1,9},{5,13},{9,1},{13,5},{2,10},{6,14},... | collective-permute-start | bytes 589832 | tf_op jit(solution)/shard_map/ppermute | solution.py:17
  80.2 11.0 %collective-permute-start.22 = (bf16[192,512]{1,0:T(8,128)(2,1)S(1)}, bf16[192,512]{1,0:T(8,128)(2,1)S(1)}, u32[]{:S(2)}, u32[]{:S(2)}) collective-permute-start(bf16[192,512]{1,0:T(8,128)(2,1)S(1)} %pad_maximum_fusion.2), channel_id=1, source_target_pairs={{0,12},{4,8},{8,4},{12,0},{1,13},{5,9},{9,5},{13,1},{2,14},{6,10},... | collective-permute-start | bytes 589832 | tf_op jit(solution)/shard_map/ppermute | solution.py:17
  82.1 9.1 %collective-permute-start.21 = (bf16[192,512]{1,0:T(8,128)(2,1)S(1)}, bf16[192,512]{1,0:T(8,128)(2,1)S(1)}, u32[]{:S(2)}, u32[]{:S(2)}) collective-permute-start(bf16[192,512]{1,0:T(8,128)(2,1)S(1)} %pad_maximum_fusion.2), channel_id=1, source_target_pairs={{0,4},{4,0},{8,12},{12,8},{1,5},{5,1},{9,13},{13,9},{2,6},{6,2},{1... | collective-permute-start | bytes 589832 | tf_op jit(solution)/shard_map/ppermute | solution.py:17
  82.3 7.2 %collective-permute-start.19 = (bf16[48,1024]{1,0:T(8,128)(2,1)S(1)}, bf16[48,1024]{1,0:T(8,128)(2,1)S(1)}, u32[]{:S(2)}, u32[]{:S(2)}) collective-permute-start(bf16[48,1024]{1,0:T(8,128)(2,1)S(1)} %get-tuple-element.157), channel_id=1, source_target_pairs={{0,3},{1,2},{2,1},{3,0},{4,7},{5,6},{6,5},{7,4},{8,11},{9,10},{10,... | collective-permute-start | bytes 294920 | tf_op jit(solution)/shard_map/ppermute | solution.py:17
  84.3 6.1 %collective-permute-start.18 = (bf16[48,1024]{1,0:T(8,128)(2,1)S(1)}, bf16[48,1024]{1,0:T(8,128)(2,1)S(1)}, u32[]{:S(2)}, u32[]{:S(2)}) collective-permute-start(bf16[48,1024]{1,0:T(8,128)(2,1)S(1)} %get-tuple-element.157), channel_id=1, source_target_pairs={{0,1},{1,0},{2,3},{3,2},{4,5},{5,4},{6,7},{7,6},{8,9},{9,8},{10,11... | collective-permute-start | bytes 294920 | tf_op jit(solution)/shard_map/ppermute | solution.py:17
  91.4 12.7 %collective-permute-start.26 = (bf16[192,1024]{1,0:T(8,128)(2,1)S(1)}, bf16[192,1024]{1,0:T(8,128)(2,1)S(1)}, u32[]{:S(2)}, u32[]{:S(2)}) collective-permute-start(bf16[192,1024]{1,0:T(8,128)(2,1)S(1)} %pad_maximum_fusion.1), channel_id=1, source_target_pairs={{0,12},{4,8},{8,4},{12,0},{1,13},{5,9},{9,5},{13,1},{2,14},{6,10},... | collective-permute-start | bytes 1179656 | tf_op jit(solution)/shard_map/ppermute | solution.py:17
  92.6 11.5 %collective-permute-start.25 = (bf16[192,1024]{1,0:T(8,128)(2,1)S(1)}, bf16[192,1024]{1,0:T(8,128)(2,1)S(1)}, u32[]{:S(2)}, u32[]{:S(2)}) collective-permute-start(bf16[192,1024]{1,0:T(8,128)(2,1)S(1)} %pad_maximum_fusion.1), channel_id=1, source_target_pairs={{0,4},{4,0},{8,12},{12,8},{1,5},{5,1},{9,13},{13,9},{2,6},{6,2},{1... | collective-permute-start | bytes 1179656 | tf_op jit(solution)/shard_map/ppermute | solution.py:17
  104.2 6.5 %collective-permute-start.28 = (bf16[96,1024]{1,0:T(8,128)(2,1)S(1)}, bf16[96,1024]{1,0:T(8,128)(2,1)S(1)}, u32[]{:S(2)}, u32[]{:S(2)}) collective-permute-start(bf16[96,1024]{1,0:T(8,128)(2,1)S(1)} %slice.100), channel_id=1, source_target_pairs={{0,4},{4,0},{8,12},{12,8},{1,5},{5,1},{9,13},{13,9},{2,6},{6,2},{1... | collective-permute-start | bytes 589832 | tf_op jit(solution)/shard_map/ppermute | solution.py:17
  104.3 7.7 %collective-permute-start.29 = (bf16[96,1024]{1,0:T(8,128)(2,1)S(1)}, bf16[96,1024]{1,0:T(8,128)(2,1)S(1)}, u32[]{:S(2)}, u32[]{:S(2)}) collective-permute-start(bf16[96,1024]{1,0:T(8,128)(2,1)S(1)} %slice.101), channel_id=1, source_target_pairs={{0,12},{4,8},{8,4},{12,0},{1,13},{5,9},{9,5},{13,1},{2,14},{6,10},... | collective-permute-start | bytes 589832 | tf_op jit(solution)/shard_map/ppermute | solution.py:17
  (24 other events, 128.3 us)
